TPU v7x, 32 devices: a whole 2x2x4 slice. The times are simulated.
32 devices in a mesh: seq: 16 (over z, x, core), batch: 2 (over y).
Axes of the slice: x: 2, y: 2, z: 4, core: 2. Of those that a mesh axis runs over, the one named last changes fastest.
Arguments:
- queries: bfloat16 [8192, 2048], P(('batch', 'seq')), parts along dimension 0, may hold values from -9 to 9
- key_rows: bfloat16 [8192, 2048], P(('batch', 'seq')), parts along dimension 0, may hold values from -9 to 9
- values: bfloat16 [8192, 2048], P(('batch', 'seq')), parts along dimension 0, may hold values from -6 to 6
- bias_tiles: bfloat16 [3, 256, 256], replicated, may hold values from -6 to 6
- buckets: int32 [5], replicated, may hold values from 0 to 2
- slopes: float32 [32], replicated, may hold values from 0.3 to 1.5
Outputs:
- attended: bfloat16 [8192, 2048], P(('batch', 'seq')), parts along dimension 0
There are 2 independent parts, one for each index of `batch`. A program takes and returns all parts, laid end to end along the dimension named above; an argument that names none is the same for every part. Nothing has to cross between parts.
All inputs are finite; a program needn't handle non-finite values.
Results may differ from a plain program's by a relative error of at most 0.0043.
Values may be sent and summed in bfloat16 or wider, within the bound.
No kernel may reach another device: no remote copies, remote signals or barrier semaphores. Data moves between devices by JAX's collectives and lax.ppermute only.
A program may use at most 128 MiB of HBM per device.

v0:
```python
import jax
import jax.numpy as jnp
from jax import lax
from jax.sharding import PartitionSpec as P

HD = 64
WIN = 4


def window_bias(bias_tiles, buckets):
    pieces = []
    for offset in range(-WIN, WIN + 1):
        tile = bias_tiles[buckets[abs(offset)]].astype(jnp.float32)
        if offset < 0:
            tile = tile.T
        pieces.append(tile)
    return jnp.concatenate(pieces, axis=1)


def block_attention(query_part, key_part, value_part, bias_window, slope_part):
    head_count = slope_part.shape[0]
    head_width = query_part.shape[1] // head_count
    group_size = min(head_count, 4)
    group_count = head_count // group_size
    row_count = query_part.shape[0]
    key_count = key_part.shape[0]
    query_groups = query_part.reshape(row_count, group_count, group_size, head_width).transpose(
        1, 0, 2, 3
    )
    key_groups = key_part.reshape(key_count, group_count, group_size, head_width).transpose(
        1, 0, 2, 3
    )
    value_groups = value_part.reshape(key_count, group_count, group_size, head_width).transpose(
        1, 0, 2, 3
    )
    slope_groups = slope_part.reshape(group_count, group_size)

    def per_group(packed):
        query_one, key_one, value_one, slope_one = packed
        scores = jnp.einsum("qgd,kgd->gqk", query_one, key_one, preferred_element_type=jnp.float32)
        scores = scores * HD ** (-0.5) + slope_one[:, None, None] * bias_window[None]
        peaks = jnp.max(scores, axis=-1, keepdims=True)
        raised = jnp.exp(scores - peaks)
        totals = jnp.sum(raised, axis=-1)
        weights = raised.astype(jnp.bfloat16)
        weighted = jnp.einsum(
            "gqk,kgd->qgd", weights, value_one, preferred_element_type=jnp.float32
        )
        return (weighted / totals.T[:, :, None]).astype(jnp.bfloat16)

    results = lax.map(per_group, (query_groups, key_groups, value_groups, slope_groups))
    return results.transpose(1, 0, 2, 3).reshape(row_count, head_count * head_width)


def per_device(queries, key_rows, values, bias_tiles, buckets, slopes):
    block_len = queries.shape[0]
    bias_window = window_bias(bias_tiles, buckets)
    all_queries, all_keys, all_values = (
        lax.all_to_all(queries, "seq", split_axis=1, concat_axis=0, tiled=True),
        lax.all_to_all(key_rows, "seq", split_axis=1, concat_axis=0, tiled=True),
        lax.all_to_all(values, "seq", split_axis=1, concat_axis=0, tiled=True),
    )
    cycle_len = lax.axis_size("seq")
    local_heads = slopes.shape[0] // cycle_len
    slope_part = lax.dynamic_slice_in_dim(
        slopes, lax.axis_index("seq") * local_heads, local_heads, 0
    )
    width_part = all_queries.shape[1]
    query_blocks = all_queries.reshape(cycle_len, block_len, width_part)
    key_blocks = all_keys.reshape(cycle_len, block_len, width_part)
    value_blocks = all_values.reshape(cycle_len, block_len, width_part)
    shifted_keys = jnp.stack(
        [jnp.roll(key_blocks, -offset, axis=0) for offset in range(-WIN, WIN + 1)], axis=1
    )
    shifted_values = jnp.stack(
        [jnp.roll(value_blocks, -offset, axis=0) for offset in range(-WIN, WIN + 1)], axis=1
    )
    shifted_keys = shifted_keys.reshape(cycle_len, -1, width_part)
    shifted_values = shifted_values.reshape(cycle_len, -1, width_part)

    def per_block(packed):
        return block_attention(packed[0], packed[1], packed[2], bias_window, slope_part)

    results = lax.map(per_block, (query_blocks, shifted_keys, shifted_values))
    local_rows = results.reshape(-1, width_part)
    return lax.all_to_all(local_rows, "seq", split_axis=0, concat_axis=1, tiled=True)


def solution(mesh):
    in_specs = (
        P(("batch", "seq"), None),
        P(("batch", "seq"), None),
        P(("batch", "seq"), None),
        P(),
        P(),
        P(),
    )
    out_specs = P(("batch", "seq"), None)
    return jax.shard_map(
        per_device, mesh=mesh, in_specs=in_specs, out_specs=out_specs, check_vma=False
    )
```

profile of v0, /device:TPU:1, one launch (start us, length us, event | category | flops | bytes accessed | tf_op | source)
XLA Modules:
  0.0 263.8 jit_solution(3500788233365403591)
XLA Ops:
  0.0 2.4 copy.41
  2.4 7.4 %all-to-all-start = ((bf16[256,16,128]{0,2,1:T(8,128)(2,1)}), bf16[256,16,128]{0,2,1:T(8,128)(2,1)S(1)}, u32[]{:S(2)}, u32[]{:S(2)}) async-start(bf16[256,16,128]{0,2,1:T(8,128)(2,1)} %bitcast.6), calls=%async_computation | async-start | bytes 2097152 | tf_op jit(solution)/shard_map/all_to_all | solution.py:61
  16.7 1.3 copy.45
  18.1 1.3 copy.46
  30.0 3.0 %all-to-all-done = bf16[256,16,128]{0,2,1:T(8,128)(2,1)S(1)} async-done(((bf16[256,16,128]{0,2,1:T(8,128)(2,1)}), bf16[256,16,128]{0,2,1:T(8,128)(2,1)S(1)}, u32[]{:S(2)}, u32[]{:S(2)}) %all-to-all-start) | async-done | bytes 1048608 | tf_op jit(solution)/shard_map/all_to_all | solution.py:61
  33.0 6.5 %all-to-all-start.2 = ((bf16[256,16,128]{0,2,1:T(8,128)(2,1)}), bf16[256,16,128]{0,2,1:T(8,128)(2,1)S(1)}, u32[]{:S(2)}, u32[]{:S(2)}) async-start(bf16[256,16,128]{0,2,1:T(8,128)(2,1)} %bitcast.20), calls=%async_computation.2 | async-start | bytes 2097152 | tf_op jit(solution)/shard_map/all_to_all | solution.py:60
  42.6 1.3 fusion.40
  43.9 1.4 fusion.42
  45.4 1.5 fusion.44
  48.1 14.6 %all-to-all-done.2 = bf16[256,16,128]{0,2,1:T(8,128)(2,1)S(1)} async-done(((bf16[256,16,128]{0,2,1:T(8,128)(2,1)}), bf16[256,16,128]{0,2,1:T(8,128)(2,1)S(1)}, u32[]{:S(2)}, u32[]{:S(2)}) %all-to-all-start.2) | async-done | bytes 1048608 | tf_op jit(solution)/shard_map/all_to_all | solution.py:60
  62.7 6.5 %all-to-all-start.1 = ((bf16[256,16,128]{0,2,1:T(8,128)(2,1)}), bf16[256,16,128]{0,2,1:T(8,128)(2,1)}, u32[]{:S(2)}, u32[]{:S(2)}) async-start(bf16[256,16,128]{0,2,1:T(8,128)(2,1)} %bitcast.18), calls=%async_computation.1 | async-start | bytes 2097152 | tf_op jit(solution)/shard_map/all_to_all | solution.py:59
  83.9 12.6 %copy.44 = bf16[16,9,256,128]{3,2,1,0:T(8,128)(2,1)} copy(bf16[16,9,256,128]{2,3,0,1:T(8,128)(2,1)} %fusion.22) | data formatting | bytes 18874368 | tf_op jit(solution)/shard_map/stack | solution.py:75
  105.1 12.8 %copy.49 = bf16[16,9,256,128]{3,2,1,0:T(8,128)(2,1)} copy(bf16[16,9,256,128]{2,3,0,1:T(8,128)(2,1)} %fusion.30) | data formatting | bytes 18874368 | tf_op jit(solution)/shard_map/stack | solution.py:72
  117.9 113.4 %while.10 = (s32[]{:T(128)}, bf16[16,256,128]{1,2,0:T(8,128)(2,1)S(1)}, bf16[16,2304,128]{2,1,0:T(8,128)(2,1)}, bf16[16,256,128]{1,2,0:T(8,128)(2,1)}, bf16[16,2...) while((s32[]{:T(128)}, bf16[16,256,128]{1,2,0:T(8,128)(2,1)S(1)}, ...), condition=%wide.region_3.4_spmd, body=%wide.region_0.3_spmd.sunk | while | flops 311491584 | bytes 22816880 | solution.py:84
  117.9 1.3 constant_dynamic-slice_fusion.5
  120.6 2.7 %fusion.63 = (f32[2,256]{1,0:T(2,128)S(1)}, f32[2,256,2304]{2,1,0:T(8,128)S(1)}) fusion(f32[256,2304]{1,0:T(8,128)} %get-tuple-element.210, f32[2]{0:T(128)S(1)} %get-tuple-element.209, bf16[256,2,64]{0,2,1:T(8,128)(2,1)S(1)} %bitcast.166, bf16[2304,2,64]{0,2,1:T(8,128)(2,1)S(1)} %bitcast.162), kind=kOutput, calls=%fused_computation.61.clone.1 | convolution fusion | flops 155713024 | bytes 7735304 | tf_op jit(solution)/shard_map/while/body/eval_jaxpr/while/body/eval_jaxpr/qgd,kgd->gqk/dot_general | solution.py:40
  125.0 1.3 constant_dynamic-slice_fusion.5
  127.7 2.6 %fusion.63 = (f32[2,256]{1,0:T(2,128)S(1)}, f32[2,256,2304]{2,1,0:T(8,128)S(1)}) fusion(f32[256,2304]{1,0:T(8,128)} %get-tuple-element.210, f32[2]{0:T(128)S(1)} %get-tuple-element.209, bf16[256,2,64]{0,2,1:T(8,128)(2,1)S(1)} %bitcast.166, bf16[2304,2,64]{0,2,1:T(8,128)(2,1)S(1)} %bitcast.162), kind=kOutput, calls=%fused_computation.61.clone.1 | convolution fusion | flops 155713024 | bytes 7735304 | tf_op jit(solution)/shard_map/while/body/eval_jaxpr/while/body/eval_jaxpr/qgd,kgd->gqk/dot_general | solution.py:40
  132.1 1.3 constant_dynamic-slice_fusion.5
  134.8 2.6 %fusion.63 = (f32[2,256]{1,0:T(2,128)S(1)}, f32[2,256,2304]{2,1,0:T(8,128)S(1)}) fusion(f32[256,2304]{1,0:T(8,128)} %get-tuple-element.210, f32[2]{0:T(128)S(1)} %get-tuple-element.209, bf16[256,2,64]{0,2,1:T(8,128)(2,1)S(1)} %bitcast.166, bf16[2304,2,64]{0,2,1:T(8,128)(2,1)S(1)} %bitcast.162), kind=kOutput, calls=%fused_computation.61.clone.1 | convolution fusion | flops 155713024 | bytes 7735304 | tf_op jit(solution)/shard_map/while/body/eval_jaxpr/while/body/eval_jaxpr/qgd,kgd->gqk/dot_general | solution.py:40
  139.2 1.3 constant_dynamic-slice_fusion.5
  141.9 2.6 %fusion.63 = (f32[2,256]{1,0:T(2,128)S(1)}, f32[2,256,2304]{2,1,0:T(8,128)S(1)}) fusion(f32[256,2304]{1,0:T(8,128)} %get-tuple-element.210, f32[2]{0:T(128)S(1)} %get-tuple-element.209, bf16[256,2,64]{0,2,1:T(8,128)(2,1)S(1)} %bitcast.166, bf16[2304,2,64]{0,2,1:T(8,128)(2,1)S(1)} %bitcast.162), kind=kOutput, calls=%fused_computation.61.clone.1 | convolution fusion | flops 155713024 | bytes 7735304 | tf_op jit(solution)/shard_map/while/body/eval_jaxpr/while/body/eval_jaxpr/qgd,kgd->gqk/dot_general | solution.py:40
  146.3 1.3 constant_dynamic-slice_fusion.5
  148.9 2.7 %fusion.63 = (f32[2,256]{1,0:T(2,128)S(1)}, f32[2,256,2304]{2,1,0:T(8,128)S(1)}) fusion(f32[256,2304]{1,0:T(8,128)} %get-tuple-element.210, f32[2]{0:T(128)S(1)} %get-tuple-element.209, bf16[256,2,64]{0,2,1:T(8,128)(2,1)S(1)} %bitcast.166, bf16[2304,2,64]{0,2,1:T(8,128)(2,1)S(1)} %bitcast.162), kind=kOutput, calls=%fused_computation.61.clone.1 | convolution fusion | flops 155713024 | bytes 7735304 | tf_op jit(solution)/shard_map/while/body/eval_jaxpr/while/body/eval_jaxpr/qgd,kgd->gqk/dot_general | solution.py:40
  153.4 1.3 constant_dynamic-slice_fusion.5
  156.0 2.6 %fusion.63 = (f32[2,256]{1,0:T(2,128)S(1)}, f32[2,256,2304]{2,1,0:T(8,128)S(1)}) fusion(f32[256,2304]{1,0:T(8,128)} %get-tuple-element.210, f32[2]{0:T(128)S(1)} %get-tuple-element.209, bf16[256,2,64]{0,2,1:T(8,128)(2,1)S(1)} %bitcast.166, bf16[2304,2,64]{0,2,1:T(8,128)(2,1)S(1)} %bitcast.162), kind=kOutput, calls=%fused_computation.61.clone.1 | convolution fusion | flops 155713024 | bytes 7735304 | tf_op jit(solution)/shard_map/while/body/eval_jaxpr/while/body/eval_jaxpr/qgd,kgd->gqk/dot_general | solution.py:40
  160.4 1.3 constant_dynamic-slice_fusion.5
  163.1 2.7 %fusion.63 = (f32[2,256]{1,0:T(2,128)S(1)}, f32[2,256,2304]{2,1,0:T(8,128)S(1)}) fusion(f32[256,2304]{1,0:T(8,128)} %get-tuple-element.210, f32[2]{0:T(128)S(1)} %get-tuple-element.209, bf16[256,2,64]{0,2,1:T(8,128)(2,1)S(1)} %bitcast.166, bf16[2304,2,64]{0,2,1:T(8,128)(2,1)S(1)} %bitcast.162), kind=kOutput, calls=%fused_computation.61.clone.1 | convolution fusion | flops 155713024 | bytes 7735304 | tf_op jit(solution)/shard_map/while/body/eval_jaxpr/while/body/eval_jaxpr/qgd,kgd->gqk/dot_general | solution.py:40
  167.5 1.3 constant_dynamic-slice_fusion.5
  170.2 2.6 %fusion.63 = (f32[2,256]{1,0:T(2,128)S(1)}, f32[2,256,2304]{2,1,0:T(8,128)S(1)}) fusion(f32[256,2304]{1,0:T(8,128)} %get-tuple-element.210, f32[2]{0:T(128)S(1)} %get-tuple-element.209, bf16[256,2,64]{0,2,1:T(8,128)(2,1)S(1)} %bitcast.166, bf16[2304,2,64]{0,2,1:T(8,128)(2,1)S(1)} %bitcast.162), kind=kOutput, calls=%fused_computation.61.clone.1 | convolution fusion | flops 155713024 | bytes 7735304 | tf_op jit(solution)/shard_map/while/body/eval_jaxpr/while/body/eval_jaxpr/qgd,kgd->gqk/dot_general | solution.py:40
  174.6 1.3 constant_dynamic-slice_fusion.5
  177.3 2.7 %fusion.63 = (f32[2,256]{1,0:T(2,128)S(1)}, f32[2,256,2304]{2,1,0:T(8,128)S(1)}) fusion(f32[256,2304]{1,0:T(8,128)} %get-tuple-element.210, f32[2]{0:T(128)S(1)} %get-tuple-element.209, bf16[256,2,64]{0,2,1:T(8,128)(2,1)S(1)} %bitcast.166, bf16[2304,2,64]{0,2,1:T(8,128)(2,1)S(1)} %bitcast.162), kind=kOutput, calls=%fused_computation.61.clone.1 | convolution fusion | flops 155713024 | bytes 7735304 | tf_op jit(solution)/shard_map/while/body/eval_jaxpr/while/body/eval_jaxpr/qgd,kgd->gqk/dot_general | solution.py:40
  181.7 1.3 constant_dynamic-slice_fusion.5
  184.4 2.6 %fusion.63 = (f32[2,256]{1,0:T(2,128)S(1)}, f32[2,256,2304]{2,1,0:T(8,128)S(1)}) fusion(f32[256,2304]{1,0:T(8,128)} %get-tuple-element.210, f32[2]{0:T(128)S(1)} %get-tuple-element.209, bf16[256,2,64]{0,2,1:T(8,128)(2,1)S(1)} %bitcast.166, bf16[2304,2,64]{0,2,1:T(8,128)(2,1)S(1)} %bitcast.162), kind=kOutput, calls=%fused_computation.61.clone.1 | convolution fusion | flops 155713024 | bytes 7735304 | tf_op jit(solution)/shard_map/while/body/eval_jaxpr/while/body/eval_jaxpr/qgd,kgd->gqk/dot_general | solution.py:40
  188.8 1.3 constant_dynamic-slice_fusion.5
  191.5 2.7 %fusion.63 = (f32[2,256]{1,0:T(2,128)S(1)}, f32[2,256,2304]{2,1,0:T(8,128)S(1)}) fusion(f32[256,2304]{1,0:T(8,128)} %get-tuple-element.210, f32[2]{0:T(128)S(1)} %get-tuple-element.209, bf16[256,2,64]{0,2,1:T(8,128)(2,1)S(1)} %bitcast.166, bf16[2304,2,64]{0,2,1:T(8,128)(2,1)S(1)} %bitcast.162), kind=kOutput, calls=%fused_computation.61.clone.1 | convolution fusion | flops 155713024 | bytes 7735304 | tf_op jit(solution)/shard_map/while/body/eval_jaxpr/while/body/eval_jaxpr/qgd,kgd->gqk/dot_general | solution.py:40
  195.9 1.3 constant_dynamic-slice_fusion.5
  198.6 2.6 %fusion.63 = (f32[2,256]{1,0:T(2,128)S(1)}, f32[2,256,2304]{2,1,0:T(8,128)S(1)}) fusion(f32[256,2304]{1,0:T(8,128)} %get-tuple-element.210, f32[2]{0:T(128)S(1)} %get-tuple-element.209, bf16[256,2,64]{0,2,1:T(8,128)(2,1)S(1)} %bitcast.166, bf16[2304,2,64]{0,2,1:T(8,128)(2,1)S(1)} %bitcast.162), kind=kOutput, calls=%fused_computation.61.clone.1 | convolution fusion | flops 155713024 | bytes 7735304 | tf_op jit(solution)/shard_map/while/body/eval_jaxpr/while/body/eval_jaxpr/qgd,kgd->gqk/dot_general | solution.py:40
  203.0 1.3 constant_dynamic-slice_fusion.5
  205.7 2.7 %fusion.63 = (f32[2,256]{1,0:T(2,128)S(1)}, f32[2,256,2304]{2,1,0:T(8,128)S(1)}) fusion(f32[256,2304]{1,0:T(8,128)} %get-tuple-element.210, f32[2]{0:T(128)S(1)} %get-tuple-element.209, bf16[256,2,64]{0,2,1:T(8,128)(2,1)S(1)} %bitcast.166, bf16[2304,2,64]{0,2,1:T(8,128)(2,1)S(1)} %bitcast.162), kind=kOutput, calls=%fused_computation.61.clone.1 | convolution fusion | flops 155713024 | bytes 7735304 | tf_op jit(solution)/shard_map/while/body/eval_jaxpr/while/body/eval_jaxpr/qgd,kgd->gqk/dot_general | solution.py:40
  210.1 1.3 constant_dynamic-slice_fusion.5
  212.8 2.6 %fusion.63 = (f32[2,256]{1,0:T(2,128)S(1)}, f32[2,256,2304]{2,1,0:T(8,128)S(1)}) fusion(f32[256,2304]{1,0:T(8,128)} %get-tuple-element.210, f32[2]{0:T(128)S(1)} %get-tuple-element.209, bf16[256,2,64]{0,2,1:T(8,128)(2,1)S(1)} %bitcast.166, bf16[2304,2,64]{0,2,1:T(8,128)(2,1)S(1)} %bitcast.162), kind=kOutput, calls=%fused_computation.61.clone.1 | convolution fusion | flops 155713024 | bytes 7735304 | tf_op jit(solution)/shard_map/while/body/eval_jaxpr/while/body/eval_jaxpr/qgd,kgd->gqk/dot_general | solution.py:40
  217.2 1.3 constant_dynamic-slice_fusion.5
  219.9 2.7 %fusion.63 = (f32[2,256]{1,0:T(2,128)S(1)}, f32[2,256,2304]{2,1,0:T(8,128)S(1)}) fusion(f32[256,2304]{1,0:T(8,128)} %get-tuple-element.210, f32[2]{0:T(128)S(1)} %get-tuple-element.209, bf16[256,2,64]{0,2,1:T(8,128)(2,1)S(1)} %bitcast.166, bf16[2304,2,64]{0,2,1:T(8,128)(2,1)S(1)} %bitcast.162), kind=kOutput, calls=%fused_computation.61.clone.1 | convolution fusion | flops 155713024 | bytes 7735304 | tf_op jit(solution)/shard_map/while/body/eval_jaxpr/while/body/eval_jaxpr/qgd,kgd->gqk/dot_general | solution.py:40
  224.3 1.3 constant_dynamic-slice_fusion.5
  226.9 2.6 %fusion.63 = (f32[2,256]{1,0:T(2,128)S(1)}, f32[2,256,2304]{2,1,0:T(8,128)S(1)}) fusion(f32[256,2304]{1,0:T(8,128)} %get-tuple-element.210, f32[2]{0:T(128)S(1)} %get-tuple-element.209, bf16[256,2,64]{0,2,1:T(8,128)(2,1)S(1)} %bitcast.166, bf16[2304,2,64]{0,2,1:T(8,128)(2,1)S(1)} %bitcast.162), kind=kOutput, calls=%fused_computation.61.clone.1 | convolution fusion | flops 155713024 | bytes 7735304 | tf_op jit(solution)/shard_map/while/body/eval_jaxpr/while/body/eval_jaxpr/qgd,kgd->gqk/dot_general | solution.py:40
  231.3 31.1 %all_to_all.64 = bf16[16,256,128]{1,2,0:T(8,128)(2,1)S(1)} all-to-all(bf16[16,256,128]{1,2,0:T(8,128)(2,1)S(1)} %get-tuple-element.63), channel_id=1, replica_groups=mesh['seq'=16,'batch'=2] {'seq'}, dimensions={0} | all-to-all | bytes 2097152 | tf_op jit(solution)/shard_map/all_to_all | solution.py:86
  262.4 1.4 copy.59
  (195 shorter events, 84.9 us)
Async XLA Ops:
  0.0 9.8 %copy-start.23 = (s32[5]{0:T(128)S(1)}, s32[5]{0:T(128)}, u32[]{:S(2)}) copy-start(s32[5]{0:T(128)} %param.12) | copy-start | bytes 64
  0.0 16.7 %copy-start.10 = (bf16[256,2048]{1,0:T(8,128)(2,1)S(1)}, bf16[256,2048]{1,0:T(8,128)(2,1)}, u32[]{:S(2)}) copy-start(bf16[256,2048]{1,0:T(8,128)(2,1)} %param.8) | copy-start | bytes 3145732
  2.4 15.7 %copy-start.11 = (bf16[256,2048]{1,0:T(8,128)(2,1)S(1)}, bf16[256,2048]{1,0:T(8,128)(2,1)}, u32[]{:S(2)}) copy-start(bf16[256,2048]{1,0:T(8,128)(2,1)} %param.9) | copy-start | bytes 3145732
  2.4 30.6 %all-to-all-start = ((bf16[256,16,128]{0,2,1:T(8,128)(2,1)}), bf16[256,16,128]{0,2,1:T(8,128)(2,1)S(1)}, u32[]{:S(2)}, u32[]{:S(2)}) async-start(bf16[256,16,128]{0,2,1:T(8,128)(2,1)} %bitcast.6), calls=%async_computation | async-start | bytes 2097152 | tf_op jit(solution)/shard_map/all_to_all | solution.py:61
  9.8 12.1 %copy-start.3 = (bf16[3,256,256]{2,1,0:T(8,128)(2,1)S(1)}, bf16[3,256,256]{2,1,0:T(8,128)(2,1)}, u32[]{:S(2)}) copy-start(bf16[3,256,256]{2,1,0:T(8,128)(2,1)} %param.11) | copy-start | bytes 1179652
  19.4 3.1 %copy-start.24 = (f32[32]{0:T(128)S(1)}, f32[32]{0:T(128)}, u32[]{:S(2)}) copy-start(f32[32]{0:T(128)} %param.13) | copy-start | bytes 388
  33.0 29.7 %all-to-all-start.2 = ((bf16[256,16,128]{0,2,1:T(8,128)(2,1)}), bf16[256,16,128]{0,2,1:T(8,128)(2,1)S(1)}, u32[]{:S(2)}, u32[]{:S(2)}) async-start(bf16[256,16,128]{0,2,1:T(8,128)(2,1)} %bitcast.20), calls=%async_computation.2 | async-start | bytes 2097152 | tf_op jit(solution)/shard_map/all_to_all | solution.py:60
  62.7 55.2 %all-to-all-start.1 = ((bf16[256,16,128]{0,2,1:T(8,128)(2,1)}), bf16[256,16,128]{0,2,1:T(8,128)(2,1)}, u32[]{:S(2)}, u32[]{:S(2)}) async-start(bf16[256,16,128]{0,2,1:T(8,128)(2,1)} %bitcast.18), calls=%async_computation.1 | async-start | bytes 2097152 | tf_op jit(solution)/shard_map/all_to_all | solution.py:59
  70.3 1.9 copy-start.9
  70.3 1.9 copy-start.14
  71.4 2.8 %copy-start.6 = (bf16[13,256,128]{1,2,0:T(8,128)(2,1)S(1)}, bf16[13,256,128]{1,2,0:T(8,128)(2,1)}, u32[]{:S(2)}) copy-start(bf16[13,256,128]{1,2,0:T(8,128)(2,1)} %get-tuple-element.117) | copy-start | bytes 2555908
  71.4 2.8 %copy-start.16 = (bf16[3,256,128]{1,2,0:T(8,128)(2,1)S(1)}, bf16[3,256,128]{1,2,0:T(8,128)(2,1)}, u32[]{:S(2)}) copy-start(bf16[3,256,128]{1,2,0:T(8,128)(2,1)} %get-tuple-element.119) | copy-start | bytes 589828
  73.2 2.1 copy-start.2
  73.2 2.1 copy-start.20
  74.2 2.2 copy-start
  74.2 2.2 copy-start.22
  76.4 2.1 copy-start.21
  77.5 2.2 copy-start.1
  77.5 2.2 copy-start.18
  78.6 2.2 copy-start.5
  78.6 2.2 copy-start.15
  79.7 2.1 copy-start.8
  79.7 2.1 copy-start.13
  96.5 0.9 copy-start.19
  99.8 2.1 copy-start.17
  100.8 2.1 copy-start.4
  101.9 2.1 copy-start.7
  105.1 12.8 %copy-start.12 = (bf16[16,256,128]{1,2,0:T(8,128)(2,1)S(1)}, bf16[16,256,128]{1,2,0:T(8,128)(2,1)}, u32[]{:S(2)}) copy-start(bf16[16,256,128]{1,2,0:T(8,128)(2,1)} %custom-call.3) | copy-start | bytes 3145732
where the time goes:
time: 267 us; the launch traced here: 264 us
  local copies, waits for them, and re-layouts  93.7 us (35%)
  matrix products  57.5 us (22%)
  other arithmetic  33.4 us (13%)
  blocking collectives  31.1 us (12%)
  starting transfers between devices  20.4 us (8%)
  waiting for transfers between devices  17.6 us (7%)
  between operations  9.56 us (4%)
    dynamic_slice x64, local copies, waits for them, and re-layouts, per_device(): results = lax.map(per_block, (query_blocks, shifted_keys, shifted_values))  42.7 us
    dot_general x16, matrix products, per_group(): jnp.einsum('qgd,kgd->gqk', query_one, key_one, preferred_element_type=jnp...  42.4 us
    all_to_all x1, blocking collectives, per_device(): lax.all_to_all(local_rows, 'seq', split_axis=0, concat_axis=1, tiled=True)  31.1 us
    unnamed x18, other arithmetic  17.9 us
    dot_general x16, matrix products, per_group(): jnp.einsum('gqk,kgd->qgd', weights, value_one, preferred_element_type=jnp...  15.1 us
    all_to_all x1, waiting for transfers between devices, per_device(): lax.all_to_all(key_rows, 'seq', split_axis=1, concat_axis=0, tiled=True)  14.6 us
    another operation x1, local copies, waits for them, and re-layouts, per_device(): jnp.stack([jnp.roll(key_blocks, -offset, axis=0) for offset in range(-WIN...  12.8 us
    another operation x1, local copies, waits for them, and re-layouts, per_device(): jnp.stack([jnp.roll(value_blocks, -offset, axis=0) for offset in range(-W...  12.6 us
  transfers between devices with their start and end apart: 3, of which 2 were waited for; matrix products, arithmetic and copies ran while one was open for 25% of the time, Pallas kernels for 0%

commit v1 on v0

v1 whole, which is shorter than its diff:
```python
import functools

import jax
import jax.numpy as jnp
from jax import lax
from jax.experimental import pallas as pl
from jax.experimental.pallas import tpu as pltpu
from jax.sharding import PartitionSpec as P

LANES = 128


def bias_kernel(win, buckets, tile_ref, out_ref):
    step = pl.program_id(0)
    tile = tile_ref[0].astype(jnp.float32)

    @pl.when(step < win)
    def _():
        out_ref[0] = tile.T

    @pl.when(step >= win)
    def _():
        out_ref[0] = tile


def bias_window(bias_tiles, buckets):
    win = buckets.shape[0] - 1
    block_len = bias_tiles.shape[1]
    grid_spec = pltpu.PrefetchScalarGridSpec(
        num_scalar_prefetch=1,
        grid=(2 * win + 1,),
        in_specs=[
            pl.BlockSpec(
                (1, block_len, block_len), lambda t, b: (b[jnp.abs(t - win)], 0, 0)
            )
        ],
        out_specs=pl.BlockSpec((1, block_len, block_len), lambda t, b: (t, 0, 0)),
    )
    return pl.pallas_call(
        functools.partial(bias_kernel, win),
        grid_spec=grid_spec,
        out_shape=jax.ShapeDtypeStruct((2 * win + 1, block_len, block_len), jnp.float32),
        name="bias_window",
    )(buckets, bias_tiles)


def pack_kernel(groups, *refs):
    count = sum(len(g) for g in groups)
    ins, outs = refs[:count], refs[count:]
    at = 0
    for group, out in zip(groups, outs):
        for slot in range(len(group)):
            out[0, slot] = ins[at][...]
            at += 1


def pack(arrays, groups, plane, name):
    rows = arrays[0].shape[0]
    flat = [item for group in groups for item in group]
    in_specs = [
        pl.BlockSpec((rows, LANES), functools.partial(lambda c, p: (0, plane * c + p), chunk))
        for _, chunk in flat
    ]
    out_specs = [
        pl.BlockSpec((1, len(g), rows, LANES), lambda p: (p, 0, 0, 0)) for g in groups
    ]
    out_shape = [
        jax.ShapeDtypeStruct((plane, len(g), rows, LANES), arrays[0].dtype) for g in groups
    ]
    size = sum(len(g) for g in groups) * plane * rows * LANES * 4
    return pl.pallas_call(
        functools.partial(pack_kernel, groups),
        grid=(plane,),
        in_specs=in_specs,
        out_specs=out_specs,
        out_shape=out_shape,
        cost_estimate=pl.CostEstimate(flops=0, bytes_accessed=size, transcendentals=0),
        name=name,
    )(*[arrays[a] for a, _ in flat])


def attention_kernel(
    win, heads, scale, slopes, q_ref, up_ref, own_ref, down_ref, bias_ref, out_ref,
    kv, scores, sems,
):
    step = pl.program_id(0)
    plane = own_ref.shape[0]
    rows = q_ref.shape[2]
    head_width = LANES // heads

    @pl.when(step == 0)
    def _():
        copies = [
            pltpu.make_async_copy(ref, kv.at[pl.ds(plane * at, plane)], sems.at[at])
            for at, ref in enumerate((up_ref, own_ref, down_ref))
        ]
        for copy in copies:
            copy.start()
        for copy in copies:
            copy.wait()

    base = step + plane - win
    query = q_ref[0, 0] * jnp.asarray(scale, q_ref.dtype)
    lane = lax.broadcasted_iota(jnp.int32, (1, LANES), 1) // head_width
    tiles = 2 * win + 1
    result = jnp.zeros((rows, LANES), jnp.float32)
    for head in range(heads):
        slope = slopes[head]
        mine = lane == head
        one = jnp.where(mine, query, jnp.zeros_like(query))
        best = None
        for t in range(tiles):
            keys = kv[base + t, 0]
            tile = lax.dot_general(
                one, keys, (((1,), (1,)), ((), ())), preferred_element_type=jnp.float32
            )
            tile = tile + slope * bias_ref[t]
            scores[:, t * rows:(t + 1) * rows] = tile
            for at in range(0, rows, LANES):
                part = tile[:, at:at + LANES]
                best = part if best is None else jnp.maximum(best, part)
        peak = jnp.max(best, axis=1, keepdims=True)
        total = jnp.zeros((rows, LANES), jnp.float32)
        acc = jnp.zeros((rows, LANES), jnp.float32)
        for t in range(tiles):
            raised = jnp.exp(scores[:, t * rows:(t + 1) * rows] - peak)
            for at in range(0, rows, LANES):
                total = total + raised[:, at:at + LANES]
            acc = acc + jnp.dot(
                raised.astype(q_ref.dtype), kv[base + t, 1], preferred_element_type=jnp.float32
            )
        acc = acc / jnp.sum(total, axis=1, keepdims=True)
        result = jnp.where(mine, acc, result)
    out_ref[0] = result.astype(out_ref.dtype)


def attention(query, chunk, up, own, down, bias, slopes, head_width):
    plane, _, rows, _ = query.shape
    tiles = bias.shape[0]
    win = tiles // 2
    heads = LANES // head_width
    any_spec = pl.BlockSpec(memory_space=pl.ANY)
    pairs = plane * tiles * heads * rows * rows
    grid_spec = pltpu.PrefetchScalarGridSpec(
        num_scalar_prefetch=1,
        grid=(plane,),
        in_specs=[
            pl.BlockSpec((1, 1, rows, LANES), lambda i, s: (i, chunk, 0, 0)),
            any_spec, any_spec, any_spec,
            pl.BlockSpec(bias.shape, lambda i, s: (0, 0, 0), pipeline_mode=pl.Buffered(1)),
        ],
        out_specs=pl.BlockSpec((1, rows, LANES), lambda i, s: (i, 0, 0)),
        scratch_shapes=[
            pltpu.VMEM((3 * plane, 2, rows, LANES), query.dtype),
            pltpu.VMEM((rows, tiles * rows), jnp.float32),
            pltpu.SemaphoreType.DMA((3,)),
        ],
    )
    return pl.pallas_call(
        functools.partial(attention_kernel, win, heads, head_width ** -0.5),
        grid_spec=grid_spec,
        out_shape=jax.ShapeDtypeStruct((plane, rows, LANES), query.dtype),
        cost_estimate=pl.CostEstimate(
            flops=4 * pairs * LANES, bytes_accessed=8 << 20, transcendentals=pairs
        ),
        compiler_params=pltpu.CompilerParams(vmem_limit_bytes=32 << 20),
        name="attention",
    )(slopes, query, up, own, down, bias)


def unpack_kernel(count, *refs):
    out = refs[count]
    for at in range(count):
        out[:, at * LANES:(at + 1) * LANES] = refs[at][0]


def unpack(parts):
    plane, rows, _ = parts[0].shape
    return jnp.concatenate([p.transpose(1, 0, 2).reshape(rows, plane * LANES) for p in parts], axis=1)


def per_device(queries, key_rows, values, bias_tiles, buckets, slopes):
    count = lax.axis_size("seq")
    plane = buckets.shape[0] - 1
    width = queries.shape[1]
    head_width = width // slopes.shape[0]
    chunks = width // (plane * LANES)
    heads = LANES // head_width
    planes = [[g * plane + p for p in range(plane)] for g in range(count // plane)]
    onward = [(i, (i + plane) % count) for i in range(count)]
    back = [(i, (i - plane) % count) for i in range(count)]

    def swap(x):
        return lax.all_to_all(
            x, "seq", split_axis=0, concat_axis=0, tiled=True, axis_index_groups=planes
        )

    def up(x):
        return lax.ppermute(x, "seq", onward)

    def down(x):
        return lax.ppermute(x, "seq", back)

    place = lax.axis_index("seq") % plane
    local_slopes = lax.dynamic_slice_in_dim(
        slopes.reshape(chunks, plane, heads), place, 1, 1
    )[:, 0]

    (first,) = pack((key_rows, values), [[(0, 0), (1, 0)]], plane, "pack_first")
    raw_up, raw_down = up(first), down(first)
    rest = pack(
        (queries, key_rows, values),
        [[(1, c), (2, c)] for c in range(1, chunks)] + [[(0, c) for c in range(chunks)]],
        plane,
        "pack_rest",
    )
    own = [None] + [swap(x) for x in rest[:-1]]
    query = swap(rest[-1])
    own[0] = swap(first)
    bias = bias_window(bias_tiles, buckets)
    ups = [swap(raw_up)] + [up(x) for x in own[1:]]
    downs = [swap(raw_down)] + [down(x) for x in own[1:]]
    parts = [
        swap(attention(query, c, ups[c], own[c], downs[c], bias, local_slopes[c], head_width))
        for c in range(chunks)
    ]
    return unpack(parts)


def solution(mesh):
    rows = P(("batch", "seq"), None)
    return jax.shard_map(
        per_device,
        mesh=mesh,
        in_specs=(rows, rows, rows, P(), P(), P()),
        out_specs=rows,
        check_vma=False,
    )
```

time: 267 us -> 200 us (0.75)
  local copies, waits for them, and re-layouts: 93.7 us -> 16.2 us
  Pallas kernels: 0 us -> 59.6 us
  matrix products: 57.5 us -> 0 us
  starting transfers between devices: 20.4 us -> 60.5 us
  other arithmetic: 33.4 us -> 0.07 us
  between operations: 9.56 us -> 0.17 us
  blocking collectives: 31.1 us -> 38 us
  waiting for transfers between devices: 17.6 us -> 22.2 us
    pallas_call x0 -> x7, Pallas kernels: none -> 59.6 us  [the longest x4 45.7 us: attention(): pl.pallas_call(functools.partial(attention_kernel, win, heads, head_width...]
    dot_general x32 -> x0, matrix products: 57.5 us -> none  [the longest x16 42.4 us: per_group(): jnp.einsum('qgd,kgd->gqk', query_one, key_one, preferred_element_type=jnp...]
    dynamic_slice x65 -> x0, local copies, waits for them, and re-layouts: 42.8 us -> none  [the longest x64 42.7 us: per_device(): results = lax.map(per_block, (query_blocks, shifted_keys, shifted_values))]
    another operation x2 -> x0, local copies, waits for them, and re-layouts: 25.4 us -> none  [the longest x1 12.8 us: per_device(): jnp.stack([jnp.roll(key_blocks, -offset, axis=0) for offset in range(-WIN...]
    ppermute x0 -> x8, starting transfers between devices: none -> 24.8 us  [the longest x4 21.6 us: down(): return lax.ppermute(x, 'seq', back)]
    unnamed x18 -> x0, other arithmetic: 17.9 us -> none
    ppermute x0 -> x8, waiting for transfers between devices: none -> 15.5 us  [the longest x4 12.6 us: up(): return lax.ppermute(x, 'seq', onward)]
    all_to_all x3 -> x8, starting transfers between devices: 20.4 us -> 35.7 us  [swap(): lax.all_to_all(x, 'seq', split_axis=0, concat_axis=0, tiled=True, axis_in...]
  transfers between devices with their start and end apart: 3 -> 16, of which waited for: 2 -> 4; matrix products, arithmetic and copies ran while one was open for 25% -> 2% of each run, Pallas kernels for 0% -> 28%
where the time goes in v1:
time: 200 us; the launch traced here: 197 us
  starting transfers between devices  60.5 us (30%)
  Pallas kernels  59.6 us (30%)
  blocking collectives  38 us (19%)
  waiting for transfers between devices  22.2 us (11%)
  local copies, waits for them, and re-layouts  16.2 us (8%)
    pallas_call x4, Pallas kernels, attention(): pl.pallas_call(functools.partial(attention_kernel, win, heads, head_width...  45.7 us
    all_to_all x3, blocking collectives, swap(): lax.all_to_all(x, 'seq', split_axis=0, concat_axis=0, tiled=True, axis_in...  38 us
    all_to_all x8, starting transfers between devices, swap(): lax.all_to_all(x, 'seq', split_axis=0, concat_axis=0, tiled=True, axis_in...  35.7 us
    ppermute x4, starting transfers between devices, down(): return lax.ppermute(x, 'seq', back)  21.6 us
    ppermute x4, waiting for transfers between devices, up(): return lax.ppermute(x, 'seq', onward)  12.6 us
    unnamed x32, local copies, waits for them, and re-layouts  11.3 us
    pallas_call x2, Pallas kernels, pack(): pl.pallas_call(functools.partial(pack_kernel, groups), grid=(plane,), in_...  7.08 us
    pallas_call x1, Pallas kernels, bias_window(): pl.pallas_call(functools.partial(bias_kernel, win), grid_spec=grid_spec,...  6.89 us
  transfers between devices with their start and end apart: 16, of which 4 were waited for; matrix products, arithmetic and copies ran while one was open for 2% of the time, Pallas kernels for 28%

profile of v1, /device:TPU:1, one launch (start us, length us, event | category | flops | bytes accessed | tf_op | source)
XLA Modules:
  0.0 196.8 jit_solution(5790571721738773151)
XLA Ops:
  0.0 4.0 %pack_rest.1 = (bf16[4,2,256,128]{3,2,1,0:T(8,128)(2,1)}, bf16[4,2,256,128]{3,2,1,0:T(8,128)(2,1)}, bf16[4,2,256,128]{3,2,1,0:T(8,128)(2,1)}, bf16[4,4,256,128]{3,2,1,0:T(8,128)(2,1)}) custom-call(bf16[256,2048]{1,0:T(8,128)(2,1)} %refs_0_.3, bf16[256,2048]{1,0:T(8,128)(2,1)} %refs_1_.3, bf16[256,2048]{1,0:T(8,128)(2,1)} %refs_0_.3, ...), custom_call_target="tpu_custom_call" | custom-call | bytes 5242880 | tf_op jit(solution)/shard_map/pack_rest/pallas_call | solution.py:71
  4.0 12.0 %all_to_all.55.own_ref = bf16[4,2,256,128]{3,2,1,0:T(8,128)(2,1)S(1)} all-to-all(bf16[4,2,256,128]{3,2,1,0:T(8,128)(2,1)} %get-tuple-element.12), channel_id=1, replica_groups={{0,2,4,6},{8,10,12,14},{16,18,20,22},{24,26,28,30},{1,3,5,7},{9,11,13,1..., dimensions={0} | all-to-all | bytes 1048576 | tf_op jit(solution)/shard_map/all_to_all | solution.py:194
  16.0 13.0 %all_to_all.56.own_ref = bf16[4,2,256,128]{3,2,1,0:T(8,128)(2,1)} all-to-all(bf16[4,2,256,128]{3,2,1,0:T(8,128)(2,1)} %get-tuple-element.11), channel_id=1, replica_groups={{0,2,4,6},{8,10,12,14},{16,18,20,22},{24,26,28,30},{1,3,5,7},{9,11,13,1..., dimensions={0} | all-to-all | bytes 1048576 | tf_op jit(solution)/shard_map/all_to_all | solution.py:194
  29.0 5.1 %all-to-all-start.5 = ((bf16[4,2,256,128]{3,2,1,0:T(8,128)(2,1)}), bf16[4,2,256,128]{3,2,1,0:T(8,128)(2,1)}, u32[]{:S(2)}, u32[]{:S(2)}) async-start(bf16[4,2,256,128]{3,2,1,0:T(8,128)(2,1)} %get-tuple-element.10), calls=%async_computation.5 | async-start | bytes 1048576 | tf_op jit(solution)/shard_map/all_to_all | solution.py:194
  34.2 3.1 %pack_first.1 = bf16[4,2,256,128]{3,2,1,0:T(8,128)(2,1)} custom-call(bf16[256,2048]{1,0:T(8,128)(2,1)} %refs_0_.3, bf16[256,2048]{1,0:T(8,128)(2,1)} %refs_1_.3), custom_call_target="tpu_custom_call" | custom-call | bytes 1048576 | tf_op jit(solution)/shard_map/pack_first/pallas_call | solution.py:71
  37.2 4.9 %all-to-all-done.5.own_ref = bf16[4,2,256,128]{3,2,1,0:T(8,128)(2,1)} async-done(((bf16[4,2,256,128]{3,2,1,0:T(8,128)(2,1)}), bf16[4,2,256,128]{3,2,1,0:T(8,128)(2,1)}, u32[]{:S(2)}, u32[]{:S(2)}) %all-to-all-start.5) | async-done | bytes 524320 | tf_op jit(solution)/shard_map/all_to_all | solution.py:194
  42.1 12.9 %all_to_all.57.own_ref = bf16[4,2,256,128]{3,2,1,0:T(8,128)(2,1)} all-to-all(bf16[4,2,256,128]{3,2,1,0:T(8,128)(2,1)} %pack_first.1), channel_id=1, replica_groups={{0,2,4,6},{8,10,12,14},{16,18,20,22},{24,26,28,30},{1,3,5,7},{9,11,13,1..., dimensions={0} | all-to-all | bytes 1048576 | tf_op jit(solution)/shard_map/all_to_all | solution.py:194
  55.1 4.7 %all-to-all-start = ((bf16[4,4,256,128]{3,2,1,0:T(8,128)(2,1)}), bf16[4,4,256,128]{3,2,1,0:T(8,128)(2,1)S(1)}, u32[]{:S(2)}, u32[]{:S(2)}) async-start(bf16[4,4,256,128]{3,2,1,0:T(8,128)(2,1)} %get-tuple-element.9), calls=%async_computation | async-start | bytes 2097152 | tf_op jit(solution)/shard_map/all_to_all | solution.py:194
  59.7 2.0 %collective-permute-start = (bf16[4,2,256,128]{3,2,1,0:T(8,128)(2,1)}, bf16[4,2,256,128]{3,2,1,0:T(8,128)(2,1)}, u32[]{:S(2)}, u32[]{:S(2)}) collective-permute-start(bf16[4,2,256,128]{3,2,1,0:T(8,128)(2,1)} %pack_first.1), channel_id=1, source_target_pairs={{0,8},{2,10},{4,12},{6,14},{8,16},{10,18},{12,20},{14,22},{16,24},... | collective-permute-start | bytes 1572872 | tf_op jit(solution)/shard_map/ppermute | solution.py:199
  61.7 2.0 %collective-permute-start.1 = (bf16[4,2,256,128]{3,2,1,0:T(8,128)(2,1)}, bf16[4,2,256,128]{3,2,1,0:T(8,128)(2,1)}, u32[]{:S(2)}, u32[]{:S(2)}) collective-permute-start(bf16[4,2,256,128]{3,2,1,0:T(8,128)(2,1)} %pack_first.1), channel_id=1, source_target_pairs={{0,24},{2,26},{4,28},{6,30},{8,0},{10,2},{12,4},{14,6},{16,8},{18,... | collective-permute-start | bytes 1572872 | tf_op jit(solution)/shard_map/ppermute | solution.py:202
  63.7 12.6 %collective-permute-done = bf16[4,2,256,128]{3,2,1,0:T(8,128)(2,1)} collective-permute-done((bf16[4,2,256,128]{3,2,1,0:T(8,128)(2,1)}, bf16[4,2,256,128]{3,2,1,0:T(8,128)(2,1)}, u32[]{:S(2)}, u32[]{:S(2)}) %collective-permute-start) | collective-permute-done | bytes 524320 | tf_op jit(solution)/shard_map/ppermute | solution.py:199
  76.3 4.4 %all-to-all-start.1 = ((bf16[4,2,256,128]{3,2,1,0:T(8,128)(2,1)}), bf16[4,2,256,128]{3,2,1,0:T(8,128)(2,1)S(1)}, u32[]{:S(2)}, u32[]{:S(2)}) async-start(bf16[4,2,256,128]{3,2,1,0:T(8,128)(2,1)} %collective-permute-done), calls=%async_computation.1 | async-start | bytes 1048576 | tf_op jit(solution)/shard_map/all_to_all | solution.py:194
  80.7 12.9 %collective-permute-start.7 = (bf16[4,2,256,128]{3,2,1,0:T(8,128)(2,1)S(1)}, bf16[4,2,256,128]{3,2,1,0:T(8,128)(2,1)S(1)}, u32[]{:S(2)}, u32[]{:S(2)}) collective-permute-start(bf16[4,2,256,128]{3,2,1,0:T(8,128)(2,1)S(1)} %all_to_all.55.own_ref), channel_id=1, source_target_pairs={{0,24},{2,26},{4,28},{6,30},{8,0},{10,2},{12,4},{14,6},{16,8},{18,... | collective-permute-start | bytes 1572872 | tf_op jit(solution)/shard_map/ppermute | solution.py:202
  93.6 3.3 %collective-permute-start.5 = (bf16[4,2,256,128]{3,2,1,0:T(8,128)(2,1)}, bf16[4,2,256,128]{3,2,1,0:T(8,128)(2,1)}, u32[]{:S(2)}, u32[]{:S(2)}) collective-permute-start(bf16[4,2,256,128]{3,2,1,0:T(8,128)(2,1)} %all_to_all.56.own_ref), channel_id=1, source_target_pairs={{0,24},{2,26},{4,28},{6,30},{8,0},{10,2},{12,4},{14,6},{16,8},{18,... | collective-permute-start | bytes 1572872 | tf_op jit(solution)/shard_map/ppermute | solution.py:202
  96.9 5.1 %all-to-all-start.3 = ((bf16[4,2,256,128]{3,2,1,0:T(8,128)(2,1)}), bf16[4,2,256,128]{3,2,1,0:T(8,128)(2,1)}, u32[]{:S(2)}, u32[]{:S(2)}) async-start(bf16[4,2,256,128]{3,2,1,0:T(8,128)(2,1)} %collective-permute-done.1), calls=%async_computation.3 | async-start | bytes 1048576 | tf_op jit(solution)/shard_map/all_to_all | solution.py:194
  101.9 0.1 reshape.23
  102.0 6.9 %bias_window.1.bias_ref = f32[9,256,256]{2,1,0:T(8,128)} custom-call(s32[5]{0:T(128)} %buckets.1, bf16[3,256,256]{2,1,0:T(8,128)(2,1)} %tile_ref.1), custom_call_target="tpu_custom_call" | custom-call | tf_op jit(solution)/shard_map/bias_window/pallas_call | solution.py:39
  108.9 1.2 collective-permute-start.2
  110.2 0.8 copy-done.11
  110.9 3.4 %collective-permute-start.3 = (bf16[4,2,256,128]{3,2,1,0:T(8,128)(2,1)}, bf16[4,2,256,128]{3,2,1,0:T(8,128)(2,1)}, u32[]{:S(2)}, u32[]{:S(2)}) collective-permute-start(bf16[4,2,256,128]{3,2,1,0:T(8,128)(2,1)} %all-to-all-done.5.own_ref), channel_id=1, source_target_pairs={{0,24},{2,26},{4,28},{6,30},{8,0},{10,2},{12,4},{14,6},{16,8},{18,... | collective-permute-start | bytes 1572872 | tf_op jit(solution)/shard_map/ppermute | solution.py:202
  114.4 0.9 copy-done.13
  115.2 1.7 copy-done
  116.9 1.0 copy-done.6
  117.9 1.0 copy-done.12
  119.0 1.0 copy-done.14
  120.0 10.5 %attention.7 = bf16[4,256,128]{2,1,0:T(8,128)(2,1)S(1)} custom-call(f32[2]{0:T(128)S(1)} %get-tuple-element.16.slopes, bf16[4,4,256,128]{3,2,1,0:T(8,128)(2,1)S(1)} %all-to-all-done.q_ref, bf16[4,2,256,128]{3,2,1,0:T(8,128)(2,1)S(1)} %copy-done.12, bf16[4,2,256,128]{3,2,1,0:T(8,128)(2,1)S(1)} %copy-done.6, bf16[4,2,256,128]{3,2,1,0:T(8,128)(2,1)S(1)} %copy-done.14, ...), custom_call_target="tpu_custom_call" | custom-call | flops 2415919104 | bytes 8388608 | tf_op jit(solution)/shard_map/attention/pallas_call | solution.py:159
  130.5 0.0 copy-start.7
  130.5 0.7 copy-done.7
  131.2 4.4 %all-to-all-start.10 = ((bf16[4,256,128]{2,1,0:T(8,128)(2,1)}), bf16[4,256,128]{2,1,0:T(8,128)(2,1)}, u32[]{:S(2)}, u32[]{:S(2)}) async-start(bf16[4,256,128]{2,1,0:T(8,128)(2,1)} %copy-done.7), calls=%async_computation.10 | async-start | bytes 524288 | tf_op jit(solution)/shard_map/all_to_all | solution.py:194
  135.6 11.8 %attention.6 = bf16[4,256,128]{2,1,0:T(8,128)(2,1)S(1)} custom-call(f32[2]{0:T(128)S(1)} %get-tuple-element.14.slopes, bf16[4,4,256,128]{3,2,1,0:T(8,128)(2,1)S(1)} %all-to-all-done.q_ref, bf16[4,2,256,128]{3,2,1,0:T(8,128)(2,1)} %collective-permute-done.4.up_ref, bf16[4,2,256,128]{3,2,1,0:T(8,128)(2,1)} %all_to_all.56.own_ref, ...), custom_call_target="tpu_custom_call" | custom-call | flops 2415919104 | bytes 8388608 | tf_op jit(solution)/shard_map/attention/pallas_call | solution.py:159
  147.4 0.7 copy-done.8
  148.1 4.1 %all-to-all-start.8 = ((bf16[4,256,128]{2,1,0:T(8,128)(2,1)}), bf16[4,256,128]{2,1,0:T(8,128)(2,1)}, u32[]{:S(2)}, u32[]{:S(2)}) async-start(bf16[4,256,128]{2,1,0:T(8,128)(2,1)} %copy-done.8), calls=%async_computation.8 | async-start | bytes 524288 | tf_op jit(solution)/shard_map/all_to_all | solution.py:194
  152.2 3.0 %collective-permute-done.3.down_ref = bf16[4,2,256,128]{3,2,1,0:T(8,128)(2,1)} collective-permute-done((bf16[4,2,256,128]{3,2,1,0:T(8,128)(2,1)}, bf16[4,2,256,128]{3,2,1,0:T(8,128)(2,1)}, u32[]{:S(2)}, u32[]{:S(2)}) %collective-permute-start.3) | collective-permute-done | bytes 524320 | tf_op jit(solution)/shard_map/ppermute | solution.py:202
  155.2 11.8 %attention.5 = bf16[4,256,128]{2,1,0:T(8,128)(2,1)S(1)} custom-call(f32[2]{0:T(128)S(1)} %get-tuple-element.15.slopes, bf16[4,4,256,128]{3,2,1,0:T(8,128)(2,1)S(1)} %all-to-all-done.q_ref, bf16[4,2,256,128]{3,2,1,0:T(8,128)(2,1)} %collective-permute-done.2.up_ref, bf16[4,2,256,128]{3,2,1,0:T(8,128)(2,1)} %all-to-all-done.5.own_ref, ...), custom_call_target="tpu_custom_call" | custom-call | flops 2415919104 | bytes 8388608 | tf_op jit(solution)/shard_map/attention/pallas_call | solution.py:159
  167.0 0.7 copy-done.9
  167.7 4.4 %all-to-all-start.6 = ((bf16[4,256,128]{2,1,0:T(8,128)(2,1)}), bf16[4,256,128]{2,1,0:T(8,128)(2,1)}, u32[]{:S(2)}, u32[]{:S(2)}) async-start(bf16[4,256,128]{2,1,0:T(8,128)(2,1)} %copy-done.9), calls=%async_computation.6 | async-start | bytes 524288 | tf_op jit(solution)/shard_map/all_to_all | solution.py:194
  172.1 1.0 copy-done.2
  173.2 1.0 copy-done.4
  174.2 11.5 %attention.4 = bf16[4,256,128]{2,1,0:T(8,128)(2,1)S(1)} custom-call(f32[2]{0:T(128)S(1)} %get-tuple-element.13.slopes, bf16[4,4,256,128]{3,2,1,0:T(8,128)(2,1)S(1)} %all-to-all-done.q_ref, bf16[4,2,256,128]{3,2,1,0:T(8,128)(2,1)S(1)} %copy-done.4, bf16[4,2,256,128]{3,2,1,0:T(8,128)(2,1)S(1)} %copy-done.2, bf16[4,2,256,128]{3,2,1,0:T(8,128)(2,1)} %all-to-all-done.3.down_ref, ...), custom_call_target="tpu_custom_call" | custom-call | flops 2415919104 | bytes 8388608 | tf_op jit(solution)/shard_map/attention/pallas_call | solution.py:159
  185.8 0.7 copy-done.10
  186.5 3.6 %all-to-all-start.4 = ((bf16[4,256,128]{2,1,0:T(8,128)(2,1)}), bf16[4,256,128]{2,1,0:T(8,128)(2,1)S(1)}, u32[]{:S(2)}, u32[]{:S(2)}) async-start(bf16[4,256,128]{2,1,0:T(8,128)(2,1)} %copy-done.10), calls=%async_computation.4 | async-start | bytes 524288 | tf_op jit(solution)/shard_map/all_to_all | solution.py:194
  190.1 1.1 copy.10
  191.2 1.1 copy.9
  192.3 1.1 copy.8
  193.3 1.8 all-to-all-done.4
  195.1 0.1 copy.7
  195.3 0.1 pad_maximum_fusion
  195.3 1.4 copy.11
  (34 shorter events, 0.1 us)
Async XLA Ops:
  16.0 64.6 %copy-start.5 = (bf16[4,2,256,128]{3,2,1,0:T(8,128)(2,1)}, bf16[4,2,256,128]{3,2,1,0:T(8,128)(2,1)S(1)}, u32[]{:S(2)}) copy-start(bf16[4,2,256,128]{3,2,1,0:T(8,128)(2,1)S(1)} %all_to_all.55.own_ref) | copy-start | bytes 1572868
  29.0 13.1 %all-to-all-start.5 = ((bf16[4,2,256,128]{3,2,1,0:T(8,128)(2,1)}), bf16[4,2,256,128]{3,2,1,0:T(8,128)(2,1)}, u32[]{:S(2)}, u32[]{:S(2)}) async-start(bf16[4,2,256,128]{3,2,1,0:T(8,128)(2,1)} %get-tuple-element.10), calls=%async_computation.5 | async-start | bytes 1048576 | tf_op jit(solution)/shard_map/all_to_all | solution.py:194
  55.1 46.9 %copy-start.15 = (f32[32]{0:T(128)S(1)}, f32[32]{0:T(128)}, u32[]{:S(2)}) copy-start(f32[32]{0:T(128)} %param.11) | copy-start | bytes 388
  55.1 21.2 %all-to-all-start = ((bf16[4,4,256,128]{3,2,1,0:T(8,128)(2,1)}), bf16[4,4,256,128]{3,2,1,0:T(8,128)(2,1)S(1)}, u32[]{:S(2)}, u32[]{:S(2)}) async-start(bf16[4,4,256,128]{3,2,1,0:T(8,128)(2,1)} %get-tuple-element.9), calls=%async_computation | async-start | bytes 2097152 | tf_op jit(solution)/shard_map/all_to_all | solution.py:194
  59.7 16.6 %collective-permute-start = (bf16[4,2,256,128]{3,2,1,0:T(8,128)(2,1)}, bf16[4,2,256,128]{3,2,1,0:T(8,128)(2,1)}, u32[]{:S(2)}, u32[]{:S(2)}) collective-permute-start(bf16[4,2,256,128]{3,2,1,0:T(8,128)(2,1)} %pack_first.1), channel_id=1, source_target_pairs={{0,8},{2,10},{4,12},{6,14},{8,16},{10,18},{12,20},{14,22},{16,24},... | collective-permute-start | bytes 1572872 | tf_op jit(solution)/shard_map/ppermute | solution.py:199
  61.7 35.2 %collective-permute-start.1 = (bf16[4,2,256,128]{3,2,1,0:T(8,128)(2,1)}, bf16[4,2,256,128]{3,2,1,0:T(8,128)(2,1)}, u32[]{:S(2)}, u32[]{:S(2)}) collective-permute-start(bf16[4,2,256,128]{3,2,1,0:T(8,128)(2,1)} %pack_first.1), channel_id=1, source_target_pairs={{0,24},{2,26},{4,28},{6,30},{8,0},{10,2},{12,4},{14,6},{16,8},{18,... | collective-permute-start | bytes 1572872 | tf_op jit(solution)/shard_map/ppermute | solution.py:202
  63.7 46.4 %collective-permute-start.6 = (bf16[4,2,256,128]{3,2,1,0:T(8,128)(2,1)S(1)}, bf16[4,2,256,128]{3,2,1,0:T(8,128)(2,1)S(1)}, u32[]{:S(2)}, u32[]{:S(2)}) collective-permute-start(bf16[4,2,256,128]{3,2,1,0:T(8,128)(2,1)S(1)} %all_to_all.55.own_ref), channel_id=1, source_target_pairs={{0,8},{2,10},{4,12},{6,14},{8,16},{10,18},{12,20},{14,22},{16,24},... | collective-permute-start | bytes 1572872 | tf_op jit(solution)/shard_map/ppermute | solution.py:199
  76.3 20.6 %all-to-all-start.1 = ((bf16[4,2,256,128]{3,2,1,0:T(8,128)(2,1)}), bf16[4,2,256,128]{3,2,1,0:T(8,128)(2,1)S(1)}, u32[]{:S(2)}, u32[]{:S(2)}) async-start(bf16[4,2,256,128]{3,2,1,0:T(8,128)(2,1)} %collective-permute-done), calls=%async_computation.1 | async-start | bytes 1048576 | tf_op jit(solution)/shard_map/all_to_all | solution.py:194
  80.7 33.6 %collective-permute-start.7 = (bf16[4,2,256,128]{3,2,1,0:T(8,128)(2,1)S(1)}, bf16[4,2,256,128]{3,2,1,0:T(8,128)(2,1)S(1)}, u32[]{:S(2)}, u32[]{:S(2)}) collective-permute-start(bf16[4,2,256,128]{3,2,1,0:T(8,128)(2,1)S(1)} %all_to_all.55.own_ref), channel_id=1, source_target_pairs={{0,24},{2,26},{4,28},{6,30},{8,0},{10,2},{12,4},{14,6},{16,8},{18,... | collective-permute-start | bytes 1572872 | tf_op jit(solution)/shard_map/ppermute | solution.py:202
  93.6 42.0 %collective-permute-start.4 = (bf16[4,2,256,128]{3,2,1,0:T(8,128)(2,1)}, bf16[4,2,256,128]{3,2,1,0:T(8,128)(2,1)}, u32[]{:S(2)}, u32[]{:S(2)}) collective-permute-start(bf16[4,2,256,128]{3,2,1,0:T(8,128)(2,1)} %all_to_all.56.own_ref), channel_id=1, source_target_pairs={{0,8},{2,10},{4,12},{6,14},{8,16},{10,18},{12,20},{14,22},{16,24},... | collective-permute-start | bytes 1572872 | tf_op jit(solution)/shard_map/ppermute | solution.py:199
  93.6 42.0 %collective-permute-start.5 = (bf16[4,2,256,128]{3,2,1,0:T(8,128)(2,1)}, bf16[4,2,256,128]{3,2,1,0:T(8,128)(2,1)}, u32[]{:S(2)}, u32[]{:S(2)}) collective-permute-start(bf16[4,2,256,128]{3,2,1,0:T(8,128)(2,1)} %all_to_all.56.own_ref), channel_id=1, source_target_pairs={{0,24},{2,26},{4,28},{6,30},{8,0},{10,2},{12,4},{14,6},{16,8},{18,... | collective-permute-start | bytes 1572872 | tf_op jit(solution)/shard_map/ppermute | solution.py:202
  96.9 17.5 %copy-start.3 = (bf16[4,2,256,128]{3,2,1,0:T(8,128)(2,1)}, bf16[4,2,256,128]{3,2,1,0:T(8,128)(2,1)S(1)}, u32[]{:S(2)}) copy-start(bf16[4,2,256,128]{3,2,1,0:T(8,128)(2,1)S(1)} %all-to-all-done.1.up_ref) | copy-start | bytes 1572868
  96.9 34.4 %all-to-all-start.3 = ((bf16[4,2,256,128]{3,2,1,0:T(8,128)(2,1)}), bf16[4,2,256,128]{3,2,1,0:T(8,128)(2,1)}, u32[]{:S(2)}, u32[]{:S(2)}) async-start(bf16[4,2,256,128]{3,2,1,0:T(8,128)(2,1)} %collective-permute-done.1), calls=%async_computation.3 | async-start | bytes 1048576 | tf_op jit(solution)/shard_map/all_to_all | solution.py:194
  108.9 43.3 %collective-permute-start.2 = (bf16[4,2,256,128]{3,2,1,0:T(8,128)(2,1)}, bf16[4,2,256,128]{3,2,1,0:T(8,128)(2,1)}, u32[]{:S(2)}, u32[]{:S(2)}) collective-permute-start(bf16[4,2,256,128]{3,2,1,0:T(8,128)(2,1)} %all-to-all-done.5.own_ref), channel_id=1, source_target_pairs={{0,8},{2,10},{4,12},{6,14},{8,16},{10,18},{12,20},{14,22},{16,24},... | collective-permute-start | bytes 1572872 | tf_op jit(solution)/shard_map/ppermute | solution.py:199
  110.2 0.8 copy-start.11
  110.9 44.2 %collective-permute-start.3 = (bf16[4,2,256,128]{3,2,1,0:T(8,128)(2,1)}, bf16[4,2,256,128]{3,2,1,0:T(8,128)(2,1)}, u32[]{:S(2)}, u32[]{:S(2)}) collective-permute-start(bf16[4,2,256,128]{3,2,1,0:T(8,128)(2,1)} %all-to-all-done.5.own_ref), channel_id=1, source_target_pairs={{0,24},{2,26},{4,28},{6,30},{8,0},{10,2},{12,4},{14,6},{16,8},{18,... | collective-permute-start | bytes 1572872 | tf_op jit(solution)/shard_map/ppermute | solution.py:202
  114.3 0.9 copy-start.13
  115.2 1.7 copy-start
  116.9 1.0 copy-start.6
  117.9 1.0 copy-start.12
  119.0 1.0 copy-start.14
  120.0 15.6 %copy-start.1 = (f32[9,256,256]{2,1,0:T(8,128)S(1)}, f32[9,256,256]{2,1,0:T(8,128)}, u32[]{:S(2)}) copy-start(f32[9,256,256]{2,1,0:T(8,128)} %bias_window.1.bias_ref) | copy-start | bytes 7077892
  130.5 0.7 copy-start.7
  131.2 16.9 %all-to-all-start.10 = ((bf16[4,256,128]{2,1,0:T(8,128)(2,1)}), bf16[4,256,128]{2,1,0:T(8,128)(2,1)}, u32[]{:S(2)}, u32[]{:S(2)}) async-start(bf16[4,256,128]{2,1,0:T(8,128)(2,1)} %copy-done.7), calls=%async_computation.10 | async-start | bytes 524288 | tf_op jit(solution)/shard_map/all_to_all | solution.py:194
  147.4 0.7 copy-start.8
  148.1 19.6 %all-to-all-start.8 = ((bf16[4,256,128]{2,1,0:T(8,128)(2,1)}), bf16[4,256,128]{2,1,0:T(8,128)(2,1)}, u32[]{:S(2)}, u32[]{:S(2)}) async-start(bf16[4,256,128]{2,1,0:T(8,128)(2,1)} %copy-done.8), calls=%async_computation.8 | async-start | bytes 524288 | tf_op jit(solution)/shard_map/all_to_all | solution.py:194
  167.0 0.7 copy-start.9
  167.7 18.8 %all-to-all-start.6 = ((bf16[4,256,128]{2,1,0:T(8,128)(2,1)}), bf16[4,256,128]{2,1,0:T(8,128)(2,1)}, u32[]{:S(2)}, u32[]{:S(2)}) async-start(bf16[4,256,128]{2,1,0:T(8,128)(2,1)} %copy-done.9), calls=%async_computation.6 | async-start | bytes 524288 | tf_op jit(solution)/shard_map/all_to_all | solution.py:194
  172.1 1.0 copy-start.2
  173.2 1.0 copy-start.4
  185.7 0.7 copy-start.10
  186.5 8.6 %all-to-all-start.4 = ((bf16[4,256,128]{2,1,0:T(8,128)(2,1)}), bf16[4,256,128]{2,1,0:T(8,128)(2,1)S(1)}, u32[]{:S(2)}, u32[]{:S(2)}) async-start(bf16[4,256,128]{2,1,0:T(8,128)(2,1)} %copy-done.10), calls=%async_computation.4 | async-start | bytes 524288 | tf_op jit(solution)/shard_map/all_to_all | solution.py:194

commit v2 on v0

v2 whole, which is shorter than its diff:
```python
import functools

import jax
import jax.numpy as jnp
from jax import lax
from jax.experimental import pallas as pl
from jax.experimental.pallas import tpu as pltpu
from jax.sharding import PartitionSpec as P


LANES = 128
FULL = 67043328
ANY = pl.BlockSpec(memory_space=pl.ANY)
SMEM = pl.BlockSpec(memory_space=pltpu.SMEM)
PARAMS = pltpu.CompilerParams(vmem_limit_bytes=FULL)


def bias_kernel(win, buckets, tile_ref, near_ref, far_ref):
    for t in range(-win, win + 1):
        tile = tile_ref[buckets[abs(t)]].astype(jnp.float32)
        if t < win:
            near_ref[t + win] = tile.T if t < 0 else tile
        if t > 0:
            far_ref[t - 1] = tile


def bias_window(bias_tiles, buckets):
    win = buckets.shape[0] - 1
    side = bias_tiles.shape[1]
    vmem = pl.BlockSpec(memory_space=pltpu.VMEM)
    return pl.pallas_call(
        functools.partial(bias_kernel, win),
        in_specs=[SMEM, vmem],
        out_specs=[vmem, vmem],
        out_shape=[
            jax.ShapeDtypeStruct((2 * win, side, side), jnp.float32),
            jax.ShapeDtypeStruct((win, side, side), jnp.float32),
        ],
        compiler_params=PARAMS,
        name="bias_window",
    )(buckets, bias_tiles)


def columns(place, chunk, plane):
    return pl.ds(pl.multiple_of((place + chunk * plane) * LANES, LANES), LANES)


def pack_kernel(plane, groups, names, place_ref, *refs):
    ins, outs = refs[:len(names)], refs[len(names):-3]
    held, sem_in, sem_out = refs[-3:]
    place = place_ref[0]
    width = plane * LANES
    slots = sorted({item for group in groups for item in group})
    loads, stores = {}, []
    for at, (array, chunk) in enumerate(slots):
        loads[array, chunk] = copy = pltpu.make_async_copy(
            ins[names.index(array)].at[:, pl.ds(chunk * width, width)], held.at[at], sem_in.at[at]
        )
        copy.start()
    waited = set()
    for g, group in enumerate(groups):
        for slot, item in enumerate(group):
            if item not in waited:
                loads[item].wait()
                waited.add(item)
            for k in range(plane):
                copy = pltpu.make_async_copy(
                    held.at[slots.index(item), :, columns(place ^ k, 0, plane)],
                    outs[g * plane + k].at[slot],
                    sem_out.at[len(stores)],
                )
                copy.start()
                stores.append(copy)
    for copy in stores:
        copy.wait()


def pack(arrays, groups, plane, place):
    names = list(arrays)
    first = arrays[names[0]]
    rows = first.shape[0]
    slots = len({item for g in groups for item in g})
    stores = plane * sum(len(g) for g in groups)
    outs = pl.pallas_call(
        functools.partial(pack_kernel, plane, groups, names),
        in_specs=[SMEM] + [ANY] * len(names),
        out_specs=[ANY] * (plane * len(groups)),
        out_shape=[
            jax.ShapeDtypeStruct((len(g), rows, LANES), first.dtype)
            for g in groups for _ in range(plane)
        ],
        scratch_shapes=[
            pltpu.VMEM((slots, rows, plane * LANES), first.dtype),
            pltpu.SemaphoreType.DMA((slots,)),
            pltpu.SemaphoreType.DMA((stores,)),
        ],
        cost_estimate=pl.CostEstimate(
            flops=0, bytes_accessed=stores * rows * LANES * 4, transcendentals=0
        ),
        compiler_params=PARAMS,
    )(place, *arrays.values())
    return [outs[g * plane:(g + 1) * plane] for g in range(len(groups))]


def unpack_kernel(plane, chunk0, chunks, count, place_ref, *refs):
    ins, (out, held, sem_in, sem_out) = refs[:count * plane], refs[-4:]
    place = place_ref[0]
    width = plane * LANES
    at, loads = 0, []
    for group in range(count):
        for chunk in range(ins[group * plane].shape[0]):
            for k in range(plane):
                copy = pltpu.make_async_copy(
                    ins[group * plane + k].at[chunk],
                    held.at[at, :, columns(place ^ k, 0, plane)],
                    sem_in.at[at, k],
                )
                copy.start()
                loads.append(copy)
            at += 1
    stores = []
    for at in range(chunks):
        for copy in loads[at * plane:(at + 1) * plane]:
            copy.wait()
        copy = pltpu.make_async_copy(
            held.at[at], out.at[:, pl.ds((chunk0 + at) * width, width)], sem_out.at[at]
        )
        copy.start()
        stores.append(copy)
    for copy in stores:
        copy.wait()


def unpack(place, groups, chunk0, total, into):
    plane = len(groups[0])
    chunks = sum(g[0].shape[0] for g in groups)
    _, rows, _ = groups[0][0].shape
    dtype = groups[0][0].dtype
    flat = [x for g in groups for x in g]
    extra = [] if into is None else [into]
    return pl.pallas_call(
        functools.partial(unpack_kernel, plane, chunk0, chunks, len(groups)),
        in_specs=[SMEM] + [ANY] * (len(flat) + len(extra)),
        out_specs=ANY,
        out_shape=jax.ShapeDtypeStruct((rows, total * plane * LANES), dtype),
        scratch_shapes=[
            pltpu.VMEM((chunks, rows, plane * LANES), dtype),
            pltpu.SemaphoreType.DMA((chunks, plane)),
            pltpu.SemaphoreType.DMA((chunks,)),
        ],
        input_output_aliases={} if into is None else {1 + len(flat): 0},
        cost_estimate=pl.CostEstimate(
            flops=0, bytes_accessed=chunks * rows * plane * LANES * 4, transcendentals=0
        ),
        compiler_params=PARAMS,
    )(place, *flat, *extra)


def scores(query, tiles, slope, store):
    best = None
    for at, (keys, _, bias) in enumerate(tiles):
        tile = lax.dot_general(
            query, keys[...], (((1,), (1,)), ((), ())), preferred_element_type=jnp.float32
        )
        tile = tile + slope * bias[...]
        store[at] = tile
        for lane in range(0, tile.shape[1], LANES):
            part = tile[:, lane:lane + LANES]
            best = part if best is None else jnp.maximum(best, part)
    return jnp.broadcast_to(jnp.max(best, axis=1, keepdims=True), best.shape)


def weigh(tiles, peak, store, dtype):
    acc = None
    for at, (_, values, _) in enumerate(tiles):
        raised = jnp.concatenate(
            [
                jnp.exp(store[at, :, lane:lane + LANES] - peak).astype(dtype)
                for lane in range(0, store.shape[2], LANES)
            ],
            axis=1,
        )
        part = jnp.dot(raised, values[...], preferred_element_type=jnp.float32)
        acc = part if acc is None else acc + part
    return acc


def lanes_of(head_width, head):
    return lax.broadcasted_iota(jnp.int32, (1, LANES), 1) // head_width == head


def near_kernel(win, plane, chunk0, head_width, place_ref, slopes, *refs):
    qs = refs[:plane]
    uks, uvs = refs[plane:2 * plane], refs[2 * plane:3 * plane]
    oks, ovs = refs[3 * plane:4 * plane], refs[4 * plane:5 * plane]
    bias, acc_ref, peak_ref, store, keys, ones, query = refs[5 * plane:]
    place = place_ref[0]
    heads = LANES // head_width
    chunk, head = pl.program_id(0) + chunk0, pl.program_id(1)
    dtype = keys.dtype
    slope = slopes[(chunk * plane + place) * heads + head]
    mine = lanes_of(head_width, head)
    scale = jnp.asarray(head_width ** -0.5, dtype)
    for k in range(plane):
        at = place ^ k
        query[at] = jnp.where(mine, qs[k][0] * scale, jnp.zeros((), dtype))
        ones[at] = jnp.where(mine, uvs[k][0], jnp.ones((), dtype))
        ones[plane + at] = jnp.where(mine, ovs[k][0], jnp.ones((), dtype))
        keys[at] = uks[k][0]
        keys[plane + at] = oks[k][0]
    for i in range(plane):
        tiles = []
        for b in range(2 * plane):
            offset = b - plane - i
            if offset >= -win:
                tiles.append((keys.at[b], ones.at[b], bias.at[offset + win]))
        slot = store.at[i % 2]
        peak = scores(query[i], tiles, slope, slot)
        peak_ref[0, 0, i] = peak
        acc_ref[0, 0, i] = weigh(tiles, peak, slot, dtype)


def near(place, slopes, qs, ups, owns, bias, chunk0, chunks, total, head_width):
    plane = len(qs)
    _, rows, _ = qs[0].shape
    win = bias.shape[0] // 2
    heads = LANES // head_width
    block = (1, rows, LANES)
    pairs = chunks * heads * rows * rows * (plane * plane + plane * (plane + 1) // 2)
    key_spec = pl.BlockSpec(block, lambda c, h: (c, 0, 0))
    value_spec = pl.BlockSpec(block, lambda c, h: (chunks + c, 0, 0))
    query_spec = pl.BlockSpec(block, lambda c, h: (chunk0 + c, 0, 0))
    own_key = pl.BlockSpec(block, lambda c, h: (chunk0 + c, 0, 0))
    own_value = pl.BlockSpec(block, lambda c, h: (total + chunk0 + c, 0, 0))
    out = (chunks, heads, plane, rows, LANES)
    out_spec = pl.BlockSpec((1, 1) + out[2:], lambda c, h: (c, h, 0, 0, 0))
    return pl.pallas_call(
        functools.partial(near_kernel, win, plane, chunk0, head_width),
        grid=(chunks, heads),
        in_specs=[SMEM, SMEM] + [query_spec] * plane + [key_spec] * plane + [value_spec] * plane
        + [own_key] * plane + [own_value] * plane
        + [pl.BlockSpec(bias.shape, lambda c, h: (0, 0, 0), pipeline_mode=pl.Buffered(1))],
        out_specs=[out_spec, out_spec],
        out_shape=[jax.ShapeDtypeStruct(out, jnp.float32)] * 2,
        scratch_shapes=[
            pltpu.VMEM((2, 2 * win, rows, rows), jnp.float32),
            pltpu.VMEM((2 * plane, rows, LANES), qs[0].dtype),
            pltpu.VMEM((2 * plane, rows, LANES), qs[0].dtype),
            pltpu.VMEM((plane, rows, LANES), qs[0].dtype),
        ],
        cost_estimate=pl.CostEstimate(
            flops=4 * pairs * LANES, bytes_accessed=chunks * (4 << 20), transcendentals=pairs
        ),
        compiler_params=PARAMS,
        name="near",
    )(place, slopes, *qs, *ups, *ups, *owns, *owns, bias)


def far_kernel(win, plane, chunk0, head_width, place_ref, slopes, *refs):
    qs, dks, dvs = (refs[n * plane:(n + 1) * plane] for n in range(3))
    bias, acc_ref, peak_ref = refs[3 * plane:3 * plane + 3]
    outs = refs[3 * plane + 3:4 * plane + 3]
    store, keys, ones, query, held = refs[4 * plane + 3:]
    place = place_ref[0]
    heads = LANES // head_width
    chunk = pl.program_id(0) + chunk0
    dtype = keys.dtype
    scale = jnp.asarray(head_width ** -0.5, dtype)
    for k in range(plane):
        at = place ^ k
        keys[at] = dks[k][0]
        for head in range(heads):
            mine = lanes_of(head_width, head)
            query[head, at] = jnp.where(mine, qs[k][0] * scale, jnp.zeros((), dtype))
            ones[head, at] = jnp.where(mine, dvs[k][0], jnp.ones((), dtype))
    for i in range(plane):
        upper = lower = None
        for head in range(heads):
            slope = slopes[(chunk * plane + place) * heads + head]
            tiles = [
                (keys.at[b], ones.at[head, b], bias.at[b + plane - i - 1])
                for b in range(plane) if b + plane - i <= win
            ]
            slot = store.at[(i * heads + head) % store.shape[0]]
            before = peak_ref[0, head, i]
            peak = jnp.maximum(scores(query[head, i], tiles, slope, slot), before)
            acc = weigh(tiles, peak, slot, dtype) + acc_ref[0, head, i] * jnp.exp(before - peak)
            if upper is None:
                upper, lower = acc, acc
            else:
                mine = lanes_of(head_width, head)
                beside = lanes_of(head_width, head - 1)
                upper = jnp.where(mine, acc, upper)
                lower = jnp.where(beside, acc, lower)
        lower = pltpu.roll(lower, head_width, 1)
        held[i ^ place] = (upper / lower).astype(dtype)
    for k in range(plane):
        outs[k][0] = held[k]


def far(place, slopes, qs, downs, bias, before, chunk0, chunks, head_width):
    plane = len(qs)
    _, rows, _ = qs[0].shape
    win = bias.shape[0]
    heads = LANES // head_width
    block = (1, rows, LANES)
    pairs = chunks * heads * rows * rows * (plane * (plane + 1) // 2)
    acc, peak, base = before
    key_spec = pl.BlockSpec(block, lambda c: (c, 0, 0))
    value_spec = pl.BlockSpec(block, lambda c: (chunks + c, 0, 0))
    query_spec = pl.BlockSpec(block, lambda c: (chunk0 + c, 0, 0))
    near_spec = pl.BlockSpec(
        (1, heads, plane, rows, LANES), lambda c: (chunk0 - base + c, 0, 0, 0, 0)
    )
    return pl.pallas_call(
        functools.partial(far_kernel, win, plane, chunk0, head_width),
        grid=(chunks,),
        in_specs=[SMEM, SMEM] + [query_spec] * plane + [key_spec] * plane + [value_spec] * plane
        + [pl.BlockSpec(bias.shape, lambda c: (0, 0, 0), pipeline_mode=pl.Buffered(1))]
        + [near_spec, near_spec],
        out_specs=[key_spec] * plane,
        out_shape=[jax.ShapeDtypeStruct((chunks, rows, LANES), qs[0].dtype)] * plane,
        scratch_shapes=[
            pltpu.VMEM((2 * heads, win, rows, rows), jnp.float32),
            pltpu.VMEM((plane, rows, LANES), qs[0].dtype),
            pltpu.VMEM((heads, plane, rows, LANES), qs[0].dtype),
            pltpu.VMEM((heads, plane, rows, LANES), qs[0].dtype),
            pltpu.VMEM((plane, rows, LANES), qs[0].dtype),
        ],
        cost_estimate=pl.CostEstimate(
            flops=4 * pairs * LANES, bytes_accessed=chunks * (4 << 20), transcendentals=pairs
        ),
        compiler_params=PARAMS,
        name="far",
    )(place, slopes, *qs, *downs, *downs, bias, acc, peak)


def per_device(queries, key_rows, values, bias_tiles, buckets, slopes):
    count = lax.axis_size("seq")
    plane = buckets.shape[0] - 1
    width = queries.shape[1]
    head_width = width // slopes.shape[0]
    chunks = width // (plane * LANES)

    def send(arrays, step):
        out = []
        for k, x in enumerate(arrays):
            if k == 0 and step == 0:
                out.append(x)
                continue
            pairs = [(i, ((i + step * plane) % count) ^ k) for i in range(count)]
            out.append(lax.ppermute(x, "seq", pairs))
        return out

    place = (lax.axis_index("seq") % plane).astype(jnp.int32).reshape(1)
    data = dict(q=queries, k=key_rows, v=values)

    def kv(start, size):
        span = range(start, start + size)
        return [("k", c) for c in span] + [("v", c) for c in span]

    groups = [(0, chunks - 2), (chunks - 2, 1), (chunks - 1, 1)]
    kv_only = dict(k=key_rows, v=values)
    (packed,) = pack(kv_only, [kv(0, chunks)], plane, place)
    rest = pack(data, [[("q", c) for c in range(chunks)]] + [kv(*g) for g in groups], plane, place)
    ups = send(packed, 1)
    qs = send(rest[0], 0)
    owns = send(packed, 0)
    near_bias, far_bias = bias_window(bias_tiles, buckets)
    downs = [send(x, -1) for x in rest[1:]]
    sums = near(place, slopes, qs, ups, owns, near_bias, 0, chunks, chunks, head_width)
    back = []
    for g, (start, size) in enumerate(groups):
        outs = far(place, slopes, qs, downs[g], far_bias, (*sums, 0), start, size, head_width)
        back.append(send(outs, 0))
    most = unpack(place, back[:1], 0, chunks, None)
    return unpack(place, back[1:], chunks - 2, chunks, most)


def solution(mesh):
    rows = P(("batch", "seq"), None)
    return jax.shard_map(
        per_device,
        mesh=mesh,
        in_specs=(rows, rows, rows, P(), P(), P()),
        out_specs=rows,
        check_vma=False,
    )
```

time: 267 us -> 182 us (0.68)
  local copies, waits for them, and re-layouts: 93.7 us -> 0 us
  Pallas kernels: 0 us -> 66.4 us
  matrix products: 57.5 us -> 0 us
  starting transfers between devices: 20.4 us -> 62.3 us
  waiting for transfers between devices: 17.6 us -> 52 us
  other arithmetic: 33.4 us -> 0 us
  blocking collectives: 31.1 us -> 0 us
  between operations: 9.56 us -> 0.31 us
    pallas_call x0 -> x9, Pallas kernels: none -> 66.4 us  [the longest x1 31 us: near(): pl.pallas_call(functools.partial(near_kernel, win, plane, chunk0, head_wi...]
    ppermute x0 -> x31, starting transfers between devices: none -> 62.3 us  [send(): out.append(lax.ppermute(x, 'seq', pairs))]
    dot_general x32 -> x0, matrix products: 57.5 us -> none  [the longest x16 42.4 us: per_group(): jnp.einsum('qgd,kgd->gqk', query_one, key_one, preferred_element_type=jnp...]
    ppermute x0 -> x31, waiting for transfers between devices: none -> 52 us  [send(): out.append(lax.ppermute(x, 'seq', pairs))]
    dynamic_slice x65 -> x0, local copies, waits for them, and re-layouts: 42.8 us -> none  [the longest x64 42.7 us: per_device(): results = lax.map(per_block, (query_blocks, shifted_keys, shifted_values))]
    all_to_all x1 -> x0, blocking collectives: 31.1 us -> none  [per_device(): lax.all_to_all(local_rows, 'seq', split_axis=0, concat_axis=1, tiled=True)]
    another operation x2 -> x0, local copies, waits for them, and re-layouts: 25.4 us -> none  [the longest x1 12.8 us: per_device(): jnp.stack([jnp.roll(key_blocks, -offset, axis=0) for offset in range(-WIN...]
    all_to_all x3 -> x0, starting transfers between devices: 20.4 us -> none  [the longest x1 7.44 us: per_device(): lax.all_to_all(values, 'seq', split_axis=1, concat_axis=0, tiled=True)]
  transfers between devices with their start and end apart: 3 -> 31, of which waited for: 2 -> 6; matrix products, arithmetic and copies ran while one was open for 25% -> 0% of each run, Pallas kernels for 0% -> 34%
where the time goes in v2:
time: 182 us; the launch traced here: 181 us
  Pallas kernels  66.4 us (36%)
  starting transfers between devices  62.3 us (34%)
  waiting for transfers between devices  52 us (29%)
    ppermute x31, starting transfers between devices, send(): out.append(lax.ppermute(x, 'seq', pairs))  62.3 us
    ppermute x31, waiting for transfers between devices, send(): out.append(lax.ppermute(x, 'seq', pairs))  52 us
    pallas_call x1, Pallas kernels, near(): pl.pallas_call(functools.partial(near_kernel, win, plane, chunk0, head_wi...  31 us
    pallas_call x3, Pallas kernels, far(): pl.pallas_call(functools.partial(far_kernel, win, plane, chunk0, head_wid...  22.7 us
    pallas_call x2, Pallas kernels, pack(): pl.pallas_call(functools.partial(pack_kernel, plane, groups, names), in_s...  6.05 us
    pallas_call x2, Pallas kernels, unpack(): pl.pallas_call(functools.partial(unpack_kernel, plane, chunk0, chunks, le...  3.69 us
  transfers between devices with their start and end apart: 31, of which 6 were waited for; matrix products, arithmetic and copies ran while one was open for 0% of the time, Pallas kernels for 34%

profile of v2, /device:TPU:1, one launch (start us, length us, event | category | flops | bytes accessed | tf_op | source)
XLA Modules:
  0.0 181.0 jit_solution(7210223775013097139)
XLA Ops:
  0.0 3.4 %shard_map.64 = (bf16[4,256,128]{2,1,0:T(8,128)(2,1)}, bf16[4,256,128]{2,1,0:T(8,128)(2,1)}, bf16[4,256,128]{2,1,0:T(8,128)(2,1)}, bf16[4,256,128]{2,1,0:T(8,128...) custom-call(s32[1]{0:T(128)} %bitcast.place_ref, ...), custom_call_target="tpu_custom_call" | custom-call | bytes 6291456 | tf_op jit(solution)/shard_map/pallas_call | solution.py:84
  3.4 4.2 %collective-permute-start.3 = (bf16[2,256,128]{2,1,0:T(8,128)(2,1)}, bf16[2,256,128]{2,1,0:T(8,128)(2,1)}, u32[]{:S(2)}, u32[]{:S(2)}) collective-permute-start(bf16[2,256,128]{2,1,0:T(8,128)(2,1)} %get-tuple-element.45), channel_id=1, source_target_pairs={{0,24},{2,26},{4,28},{6,30},{8,0},{10,2},{12,4},{14,6},{16,8},{18,... | collective-permute-start | bytes 393224 | tf_op jit(solution)/shard_map/ppermute | solution.py:352
  7.6 1.0 collective-permute-start.4
  8.6 0.0 collective-permute-start
  8.6 1.2 collective-permute-start.1
  9.8 2.6 %shard_map.65 = (bf16[8,256,128]{2,1,0:T(8,128)(2,1)}, bf16[8,256,128]{2,1,0:T(8,128)(2,1)}, bf16[8,256,128]{2,1,0:T(8,128)(2,1)}, bf16[8,256,128]{2,1,0:T(8,128)(2,1)}) custom-call(s32[1]{0:T(128)} %bitcast.place_ref, bf16[256,2048]{1,0:T(8,128)(2,1)} %refs_0_.3, bf16[256,2048]{1,0:T(8,128)(2,1)} %refs_1_.3), custom_call_target="tpu_custom_call" | custom-call | bytes 4194304 | tf_op jit(solution)/shard_map/pallas_call | solution.py:84
  12.5 1.3 collective-permute-start.7
  13.8 1.1 collective-permute-start.11
  14.9 2.9 %collective-permute-start.17 = (bf16[2,256,128]{2,1,0:T(8,128)(2,1)}, bf16[2,256,128]{2,1,0:T(8,128)(2,1)}, u32[]{:S(2)}, u32[]{:S(2)}) collective-permute-start(bf16[2,256,128]{2,1,0:T(8,128)(2,1)} %get-tuple-element.61), channel_id=1, source_target_pairs={{0,24},{2,26},{4,28},{6,30},{8,0},{10,2},{12,4},{14,6},{16,8},{18,... | collective-permute-start | bytes 393224 | tf_op jit(solution)/shard_map/ppermute | solution.py:352
  17.9 13.5 %collective-permute-done.17.refs_4_.refs_8_ = bf16[2,256,128]{2,1,0:T(8,128)(2,1)} collective-permute-done((bf16[2,256,128]{2,1,0:T(8,128)(2,1)}, bf16[2,256,128]{2,1,0:T(8,128)(2,1)}, u32[]{:S(2)}, u32[]{:S(2)}) %collective-permute-start.17) | collective-permute-done | bytes 131104 | tf_op jit(solution)/shard_map/ppermute | solution.py:352
  31.4 0.5 collective-permute-start.2
  31.9 0.0 collective-permute-done.refs_1_
  31.9 1.7 collective-permute-start.24
  33.6 0.0 collective-permute-done.1.refs_2_
  33.6 0.0 collective-permute-start.25
  33.6 6.7 %collective-permute-done.2.refs_3_ = bf16[4,256,128]{2,1,0:T(8,128)(2,1)} collective-permute-done((bf16[4,256,128]{2,1,0:T(8,128)(2,1)}, bf16[4,256,128]{2,1,0:T(8,128)(2,1)}, u32[]{:S(2)}, u32[]{:S(2)}) %collective-permute-start.2) | collective-permute-done | bytes 262176 | tf_op jit(solution)/shard_map/ppermute | solution.py:352
  40.4 0.3 collective-permute-start.8
  40.6 0.0 collective-permute-done.24.refs_4_.refs_8_
  40.6 0.7 collective-permute-start.12
  41.3 4.9 %collective-permute-done.25.refs_5_.refs_9_ = bf16[4,256,128]{2,1,0:T(8,128)(2,1)} collective-permute-done((bf16[4,256,128]{2,1,0:T(8,128)(2,1)}, bf16[4,256,128]{2,1,0:T(8,128)(2,1)}, u32[]{:S(2)}, u32[]{:S(2)}) %collective-permute-start.25) | collective-permute-done | bytes 262176 | tf_op jit(solution)/shard_map/ppermute | solution.py:352
  46.2 23.4 %collective-permute-start.9 = (bf16[8,256,128]{2,1,0:T(8,128)(2,1)}, bf16[8,256,128]{2,1,0:T(8,128)(2,1)}, u32[]{:S(2)}, u32[]{:S(2)}) collective-permute-start(bf16[8,256,128]{2,1,0:T(8,128)(2,1)} %get-tuple-element.52), channel_id=1, source_target_pairs={{0,12},{2,14},{4,8},{6,10},{8,20},{10,22},{12,16},{14,18},{16,28},... | collective-permute-start | bytes 1572872 | tf_op jit(solution)/shard_map/ppermute | solution.py:352
  69.6 0.0 collective-permute-done.7.refs_4_.refs_8_
  69.6 0.0 collective-permute-start.13
  69.6 0.1 collective-permute-start.10
  69.7 3.0 %bias_window.1 = (f32[8,256,256]{2,1,0:T(8,128)}, f32[4,256,256]{2,1,0:T(8,128)}) custom-call(s32[5]{0:T(128)} %buckets.1, bf16[3,256,256]{2,1,0:T(8,128)(2,1)} %tile_ref.1), custom_call_target="tpu_custom_call" | custom-call | tf_op jit(solution)/shard_map/bias_window/pallas_call | solution.py:31
  72.6 4.6 %collective-permute-start.18 = (bf16[2,256,128]{2,1,0:T(8,128)(2,1)}, bf16[2,256,128]{2,1,0:T(8,128)(2,1)}, u32[]{:S(2)}, u32[]{:S(2)}) collective-permute-start(bf16[2,256,128]{2,1,0:T(8,128)(2,1)} %get-tuple-element.62), channel_id=1, source_target_pairs={{0,26},{2,24},{4,30},{6,28},{8,2},{10,0},{12,6},{14,4},{16,10},{18... | collective-permute-start | bytes 393224 | tf_op jit(solution)/shard_map/ppermute | solution.py:352
  77.2 0.0 collective-permute-done.12.refs_14_.refs_18_
  77.2 1.1 collective-permute-start.19
  78.3 3.2 %collective-permute-done.9.refs_6_.refs_10_ = bf16[8,256,128]{2,1,0:T(8,128)(2,1)} collective-permute-done((bf16[8,256,128]{2,1,0:T(8,128)(2,1)}, bf16[8,256,128]{2,1,0:T(8,128)(2,1)}, u32[]{:S(2)}, u32[]{:S(2)}) %collective-permute-start.9) | collective-permute-done | bytes 524320 | tf_op jit(solution)/shard_map/ppermute | solution.py:352
  81.5 0.0 collective-permute-start.20
  81.5 22.0 %collective-permute-done.13.refs_15_.refs_19_ = bf16[8,256,128]{2,1,0:T(8,128)(2,1)} collective-permute-done((bf16[8,256,128]{2,1,0:T(8,128)(2,1)}, bf16[8,256,128]{2,1,0:T(8,128)(2,1)}, u32[]{:S(2)}, u32[]{:S(2)}) %collective-permute-start.13) | collective-permute-done | bytes 524320 | tf_op jit(solution)/shard_map/ppermute | solution.py:352
  103.5 31.0 %near.1 = (f32[4,2,4,256,128]{4,3,2,1,0:T(8,128)}, f32[4,2,4,256,128]{4,3,2,1,0:T(8,128)}) custom-call(s32[1]{0:T(128)} %bitcast.place_ref, f32[32]{0:T(128)} %slopes.7, bf16[4,256,128]{2,1,0:T(8,128)(2,1)} %get-tuple-element.41.refs_0_, bf16[4,256,128]{2,1,0:T(8,128)(2,1)} %collective-permute-done.refs_1_, ...), custom_call_target="tpu_custom_call" | custom-call | flops 6979321856 | bytes 16777216 | tf_op jit(solution)/shard_map/near/pallas_call | solution.py:237
  134.6 11.0 %collective-permute-start.5 = (bf16[2,256,128]{2,1,0:T(8,128)(2,1)}, bf16[2,256,128]{2,1,0:T(8,128)(2,1)}, u32[]{:S(2)}, u32[]{:S(2)}) collective-permute-start(bf16[2,256,128]{2,1,0:T(8,128)(2,1)} %get-tuple-element.47), channel_id=1, source_target_pairs={{0,28},{2,30},{4,24},{6,26},{8,4},{10,6},{12,0},{14,2},{16,12},{18... | collective-permute-start | bytes 393224 | tf_op jit(solution)/shard_map/ppermute | solution.py:352
  145.5 0.7 collective-permute-start.6
  146.2 9.9 %far.5 = (bf16[2,256,128]{2,1,0:T(8,128)(2,1)}, bf16[2,256,128]{2,1,0:T(8,128)(2,1)}, bf16[2,256,128]{2,1,0:T(8,128)(2,1)}, bf16[2,256,128]{2,1,0:T(8,128)(2,1)}) custom-call(s32[1]{0:T(128)} %bitcast.place_ref, f32[32]{0:T(128)} %slopes.7, bf16[4,256,128]{2,1,0:T(8,128)(2,1)} %get-tuple-element.41.refs_0_, ...), custom_call_target="tpu_custom_call" | custom-call | flops 1342177280 | bytes 8388608 | tf_op jit(solution)/shard_map/far/pallas_call | solution.py:315
  156.1 0.2 collective-permute-start.28
  156.3 0.1 collective-permute-start.29
  156.4 1.9 %collective-permute-start.30 = (bf16[2,256,128]{2,1,0:T(8,128)(2,1)}, bf16[2,256,128]{2,1,0:T(8,128)(2,1)}, u32[]{:S(2)}, u32[]{:S(2)}) collective-permute-start(bf16[2,256,128]{2,1,0:T(8,128)(2,1)} %get-tuple-element.76), channel_id=1, source_target_pairs={{0,6},{2,4},{4,2},{6,0},{8,14},{10,12},{12,10},{14,8},{16,22},{18,... | collective-permute-start | bytes 393224 | tf_op jit(solution)/shard_map/ppermute | solution.py:352
  158.3 6.4 %far.4 = (bf16[1,256,128]{2,1,0:T(8,128)(2,1)}, bf16[1,256,128]{2,1,0:T(8,128)(2,1)}, bf16[1,256,128]{2,1,0:T(8,128)(2,1)}, bf16[1,256,128]{2,1,0:T(8,128)(2,1)}) custom-call(s32[1]{0:T(128)} %bitcast.place_ref, f32[32]{0:T(128)} %slopes.7, bf16[4,256,128]{2,1,0:T(8,128)(2,1)} %get-tuple-element.41.refs_0_, ...), custom_call_target="tpu_custom_call" | custom-call | flops 671088640 | bytes 4194304 | tf_op jit(solution)/shard_map/far/pallas_call | solution.py:315
  164.7 0.1 collective-permute-start.21
  164.8 0.1 collective-permute-start.22
  164.9 6.4 %far.3 = (bf16[1,256,128]{2,1,0:T(8,128)(2,1)}, bf16[1,256,128]{2,1,0:T(8,128)(2,1)}, bf16[1,256,128]{2,1,0:T(8,128)(2,1)}, bf16[1,256,128]{2,1,0:T(8,128)(2,1)}) custom-call(s32[1]{0:T(128)} %bitcast.place_ref, f32[32]{0:T(128)} %slopes.7, bf16[4,256,128]{2,1,0:T(8,128)(2,1)} %get-tuple-element.41.refs_0_, ...), custom_call_target="tpu_custom_call" | custom-call | flops 671088640 | bytes 4194304 | tf_op jit(solution)/shard_map/far/pallas_call | solution.py:315
  171.3 2.1 %collective-permute-start.23 = (bf16[1,256,128]{2,1,0:T(8,128)(2,1)}, bf16[1,256,128]{2,1,0:T(8,128)(2,1)}, u32[]{:S(2)}, u32[]{:S(2)}) collective-permute-start(bf16[1,256,128]{2,1,0:T(8,128)(2,1)} %get-tuple-element.68), channel_id=1, source_target_pairs={{0,6},{2,4},{4,2},{6,0},{8,14},{10,12},{12,10},{14,8},{16,22},{18,... | collective-permute-start | bytes 196616 | tf_op jit(solution)/shard_map/ppermute | solution.py:352
  173.4 0.2 collective-permute-start.15
  173.6 1.9 %collective-permute-start.16 = (bf16[1,256,128]{2,1,0:T(8,128)(2,1)}, bf16[1,256,128]{2,1,0:T(8,128)(2,1)}, u32[]{:S(2)}, u32[]{:S(2)}) collective-permute-start(bf16[1,256,128]{2,1,0:T(8,128)(2,1)} %get-tuple-element.60), channel_id=1, source_target_pairs={{0,6},{2,4},{4,2},{6,0},{8,14},{10,12},{12,10},{14,8},{16,22},{18,... | collective-permute-start | bytes 196616 | tf_op jit(solution)/shard_map/ppermute | solution.py:352
  175.5 1.8 %shard_map.66.refs_8_ = bf16[256,2048]{1,0:T(8,128)(2,1)} custom-call(s32[1]{0:T(128)} %bitcast.place_ref, bf16[2,256,128]{2,1,0:T(8,128)(2,1)} %get-tuple-element.73.refs_0_, bf16[2,256,128]{2,1,0:T(8,128)(2,1)} %collective-permute-done.28.refs_1_, bf16[2,256,128]{2,1,0:T(8,128)(2,1)} %collective-permute-done.29.refs_2_, ...), custom_call_target="tpu_custom_call" | custom-call | bytes 1048576 | tf_op jit(solution)/shard_map/pallas_call | solution.py:141
  177.4 1.6 collective-permute-done.16.refs_3_
  179.0 1.8 %shard_map.67 = bf16[256,2048]{1,0:T(8,128)(2,1)} custom-call(s32[1]{0:T(128)} %bitcast.place_ref, bf16[1,256,128]{2,1,0:T(8,128)(2,1)} %get-tuple-element.57.refs_0_, bf16[1,256,128]{2,1,0:T(8,128)(2,1)} %collective-permute-done.14.refs_1_, bf16[1,256,128]{2,1,0:T(8,128)(2,1)} %collective-permute-done.15.refs_2_, ...), custom_call_target="tpu_custom_call", output_to_operand_aliasing={{}: (9, {})} | custom-call | bytes 1048576 | tf_op jit(solution)/shard_map/pallas_call | solution.py:141
  (23 shorter events, 0.1 us)
Async XLA Ops:
  3.4 10.4 %collective-permute-start.3 = (bf16[2,256,128]{2,1,0:T(8,128)(2,1)}, bf16[2,256,128]{2,1,0:T(8,128)(2,1)}, u32[]{:S(2)}, u32[]{:S(2)}) collective-permute-start(bf16[2,256,128]{2,1,0:T(8,128)(2,1)} %get-tuple-element.45), channel_id=1, source_target_pairs={{0,24},{2,26},{4,28},{6,30},{8,0},{10,2},{12,4},{14,6},{16,8},{18,... | collective-permute-start | bytes 393224 | tf_op jit(solution)/shard_map/ppermute | solution.py:352
  7.6 7.3 %collective-permute-start.4 = (bf16[2,256,128]{2,1,0:T(8,128)(2,1)}, bf16[2,256,128]{2,1,0:T(8,128)(2,1)}, u32[]{:S(2)}, u32[]{:S(2)}) collective-permute-start(bf16[2,256,128]{2,1,0:T(8,128)(2,1)} %get-tuple-element.46), channel_id=1, source_target_pairs={{0,26},{2,24},{4,30},{6,28},{8,2},{10,0},{12,6},{14,4},{16,10},{18... | collective-permute-start | bytes 393224 | tf_op jit(solution)/shard_map/ppermute | solution.py:352
  8.6 23.3 %collective-permute-start = (bf16[4,256,128]{2,1,0:T(8,128)(2,1)}, bf16[4,256,128]{2,1,0:T(8,128)(2,1)}, u32[]{:S(2)}, u32[]{:S(2)}) collective-permute-start(bf16[4,256,128]{2,1,0:T(8,128)(2,1)} %get-tuple-element.42), channel_id=1, source_target_pairs={{0,2},{2,0},{4,6},{6,4},{8,10},{10,8},{12,14},{14,12},{16,18},{18,... | collective-permute-start | bytes 786440 | tf_op jit(solution)/shard_map/ppermute | solution.py:352
  8.6 25.0 %collective-permute-start.1 = (bf16[4,256,128]{2,1,0:T(8,128)(2,1)}, bf16[4,256,128]{2,1,0:T(8,128)(2,1)}, u32[]{:S(2)}, u32[]{:S(2)}) collective-permute-start(bf16[4,256,128]{2,1,0:T(8,128)(2,1)} %get-tuple-element.43), channel_id=1, source_target_pairs={{0,4},{2,6},{4,0},{6,2},{8,12},{10,14},{12,8},{14,10},{16,20},{18,... | collective-permute-start | bytes 786440 | tf_op jit(solution)/shard_map/ppermute | solution.py:352
  12.5 57.1 %collective-permute-start.7 = (bf16[8,256,128]{2,1,0:T(8,128)(2,1)}, bf16[8,256,128]{2,1,0:T(8,128)(2,1)}, u32[]{:S(2)}, u32[]{:S(2)}) collective-permute-start(bf16[8,256,128]{2,1,0:T(8,128)(2,1)} %get-tuple-element.50.refs_12_.refs_16_), channel_id=1, source_target_pairs={{0,8},{2,10},{4,12},{6,14},{8,16},{10,18},{12,20},{14,22},{16,24},... | collective-permute-start | bytes 1572872 | tf_op jit(solution)/shard_map/ppermute | solution.py:352
  13.8 55.8 %collective-permute-start.11 = (bf16[8,256,128]{2,1,0:T(8,128)(2,1)}, bf16[8,256,128]{2,1,0:T(8,128)(2,1)}, u32[]{:S(2)}, u32[]{:S(2)}) collective-permute-start(bf16[8,256,128]{2,1,0:T(8,128)(2,1)} %get-tuple-element.51), channel_id=1, source_target_pairs={{0,2},{2,0},{4,6},{6,4},{8,10},{10,8},{12,14},{14,12},{16,18},{18,... | collective-permute-start | bytes 1572872 | tf_op jit(solution)/shard_map/ppermute | solution.py:352
  14.9 16.5 %collective-permute-start.17 = (bf16[2,256,128]{2,1,0:T(8,128)(2,1)}, bf16[2,256,128]{2,1,0:T(8,128)(2,1)}, u32[]{:S(2)}, u32[]{:S(2)}) collective-permute-start(bf16[2,256,128]{2,1,0:T(8,128)(2,1)} %get-tuple-element.61), channel_id=1, source_target_pairs={{0,24},{2,26},{4,28},{6,30},{8,0},{10,2},{12,4},{14,6},{16,8},{18,... | collective-permute-start | bytes 393224 | tf_op jit(solution)/shard_map/ppermute | solution.py:352
  31.4 9.0 %collective-permute-start.2 = (bf16[4,256,128]{2,1,0:T(8,128)(2,1)}, bf16[4,256,128]{2,1,0:T(8,128)(2,1)}, u32[]{:S(2)}, u32[]{:S(2)}) collective-permute-start(bf16[4,256,128]{2,1,0:T(8,128)(2,1)} %get-tuple-element.44), channel_id=1, source_target_pairs={{0,6},{2,4},{4,2},{6,0},{8,14},{10,12},{12,10},{14,8},{16,22},{18,... | collective-permute-start | bytes 786440 | tf_op jit(solution)/shard_map/ppermute | solution.py:352
  31.9 8.7 %collective-permute-start.24 = (bf16[4,256,128]{2,1,0:T(8,128)(2,1)}, bf16[4,256,128]{2,1,0:T(8,128)(2,1)}, u32[]{:S(2)}, u32[]{:S(2)}) collective-permute-start(bf16[4,256,128]{2,1,0:T(8,128)(2,1)} %get-tuple-element.69), channel_id=1, source_target_pairs={{0,24},{2,26},{4,28},{6,30},{8,0},{10,2},{12,4},{14,6},{16,8},{18,... | collective-permute-start | bytes 786440 | tf_op jit(solution)/shard_map/ppermute | solution.py:352
  33.6 12.6 %collective-permute-start.25 = (bf16[4,256,128]{2,1,0:T(8,128)(2,1)}, bf16[4,256,128]{2,1,0:T(8,128)(2,1)}, u32[]{:S(2)}, u32[]{:S(2)}) collective-permute-start(bf16[4,256,128]{2,1,0:T(8,128)(2,1)} %get-tuple-element.70), channel_id=1, source_target_pairs={{0,26},{2,24},{4,30},{6,28},{8,2},{10,0},{12,6},{14,4},{16,10},{18... | collective-permute-start | bytes 786440 | tf_op jit(solution)/shard_map/ppermute | solution.py:352
  40.4 32.3 %collective-permute-start.8 = (bf16[8,256,128]{2,1,0:T(8,128)(2,1)}, bf16[8,256,128]{2,1,0:T(8,128)(2,1)}, u32[]{:S(2)}, u32[]{:S(2)}) collective-permute-start(bf16[8,256,128]{2,1,0:T(8,128)(2,1)} %get-tuple-element.51), channel_id=1, source_target_pairs={{0,10},{2,8},{4,14},{6,12},{8,18},{10,16},{12,22},{14,20},{16,26},... | collective-permute-start | bytes 1572872 | tf_op jit(solution)/shard_map/ppermute | solution.py:352
  40.6 36.5 %collective-permute-start.12 = (bf16[8,256,128]{2,1,0:T(8,128)(2,1)}, bf16[8,256,128]{2,1,0:T(8,128)(2,1)}, u32[]{:S(2)}, u32[]{:S(2)}) collective-permute-start(bf16[8,256,128]{2,1,0:T(8,128)(2,1)} %get-tuple-element.52), channel_id=1, source_target_pairs={{0,4},{2,6},{4,0},{6,2},{8,12},{10,14},{12,8},{14,10},{16,20},{18,... | collective-permute-start | bytes 1572872 | tf_op jit(solution)/shard_map/ppermute | solution.py:352
  46.2 35.3 %collective-permute-start.9 = (bf16[8,256,128]{2,1,0:T(8,128)(2,1)}, bf16[8,256,128]{2,1,0:T(8,128)(2,1)}, u32[]{:S(2)}, u32[]{:S(2)}) collective-permute-start(bf16[8,256,128]{2,1,0:T(8,128)(2,1)} %get-tuple-element.52), channel_id=1, source_target_pairs={{0,12},{2,14},{4,8},{6,10},{8,20},{10,22},{12,16},{14,18},{16,28},... | collective-permute-start | bytes 1572872 | tf_op jit(solution)/shard_map/ppermute | solution.py:352
  69.6 33.9 %collective-permute-start.13 = (bf16[8,256,128]{2,1,0:T(8,128)(2,1)}, bf16[8,256,128]{2,1,0:T(8,128)(2,1)}, u32[]{:S(2)}, u32[]{:S(2)}) collective-permute-start(bf16[8,256,128]{2,1,0:T(8,128)(2,1)} %get-tuple-element.53), channel_id=1, source_target_pairs={{0,6},{2,4},{4,2},{6,0},{8,14},{10,12},{12,10},{14,8},{16,22},{18,... | collective-permute-start | bytes 1572872 | tf_op jit(solution)/shard_map/ppermute | solution.py:352
  69.6 33.9 %collective-permute-start.10 = (bf16[8,256,128]{2,1,0:T(8,128)(2,1)}, bf16[8,256,128]{2,1,0:T(8,128)(2,1)}, u32[]{:S(2)}, u32[]{:S(2)}) collective-permute-start(bf16[8,256,128]{2,1,0:T(8,128)(2,1)} %get-tuple-element.53), channel_id=1, source_target_pairs={{0,14},{2,12},{4,10},{6,8},{8,22},{10,20},{12,18},{14,16},{16,30},... | collective-permute-start | bytes 1572872 | tf_op jit(solution)/shard_map/ppermute | solution.py:352
  72.6 83.5 %collective-permute-start.18 = (bf16[2,256,128]{2,1,0:T(8,128)(2,1)}, bf16[2,256,128]{2,1,0:T(8,128)(2,1)}, u32[]{:S(2)}, u32[]{:S(2)}) collective-permute-start(bf16[2,256,128]{2,1,0:T(8,128)(2,1)} %get-tuple-element.62), channel_id=1, source_target_pairs={{0,26},{2,24},{4,30},{6,28},{8,2},{10,0},{12,6},{14,4},{16,10},{18... | collective-permute-start | bytes 393224 | tf_op jit(solution)/shard_map/ppermute | solution.py:352
  77.2 79.1 %collective-permute-start.19 = (bf16[2,256,128]{2,1,0:T(8,128)(2,1)}, bf16[2,256,128]{2,1,0:T(8,128)(2,1)}, u32[]{:S(2)}, u32[]{:S(2)}) collective-permute-start(bf16[2,256,128]{2,1,0:T(8,128)(2,1)} %get-tuple-element.63), channel_id=1, source_target_pairs={{0,28},{2,30},{4,24},{6,26},{8,4},{10,6},{12,0},{14,2},{16,12},{18... | collective-permute-start | bytes 393224 | tf_op jit(solution)/shard_map/ppermute | solution.py:352
  81.5 74.9 %collective-permute-start.20 = (bf16[2,256,128]{2,1,0:T(8,128)(2,1)}, bf16[2,256,128]{2,1,0:T(8,128)(2,1)}, u32[]{:S(2)}, u32[]{:S(2)}) collective-permute-start(bf16[2,256,128]{2,1,0:T(8,128)(2,1)} %get-tuple-element.64), channel_id=1, source_target_pairs={{0,30},{2,28},{4,26},{6,24},{8,6},{10,4},{12,2},{14,0},{16,14},{18... | collective-permute-start | bytes 393224 | tf_op jit(solution)/shard_map/ppermute | solution.py:352
  103.5 31.0 %collective-permute-start.26 = (bf16[4,256,128]{2,1,0:T(8,128)(2,1)}, bf16[4,256,128]{2,1,0:T(8,128)(2,1)}, u32[]{:S(2)}, u32[]{:S(2)}) collective-permute-start(bf16[4,256,128]{2,1,0:T(8,128)(2,1)} %get-tuple-element.71), channel_id=1, source_target_pairs={{0,28},{2,30},{4,24},{6,26},{8,4},{10,6},{12,0},{14,2},{16,12},{18... | collective-permute-start | bytes 786440 | tf_op jit(solution)/shard_map/ppermute | solution.py:352
  103.5 42.0 %collective-permute-start.27 = (bf16[4,256,128]{2,1,0:T(8,128)(2,1)}, bf16[4,256,128]{2,1,0:T(8,128)(2,1)}, u32[]{:S(2)}, u32[]{:S(2)}) collective-permute-start(bf16[4,256,128]{2,1,0:T(8,128)(2,1)} %get-tuple-element.72), channel_id=1, source_target_pairs={{0,30},{2,28},{4,26},{6,24},{8,6},{10,4},{12,2},{14,0},{16,14},{18... | collective-permute-start | bytes 786440 | tf_op jit(solution)/shard_map/ppermute | solution.py:352
  134.6 30.2 %collective-permute-start.5 = (bf16[2,256,128]{2,1,0:T(8,128)(2,1)}, bf16[2,256,128]{2,1,0:T(8,128)(2,1)}, u32[]{:S(2)}, u32[]{:S(2)}) collective-permute-start(bf16[2,256,128]{2,1,0:T(8,128)(2,1)} %get-tuple-element.47), channel_id=1, source_target_pairs={{0,28},{2,30},{4,24},{6,26},{8,4},{10,6},{12,0},{14,2},{16,12},{18... | collective-permute-start | bytes 393224 | tf_op jit(solution)/shard_map/ppermute | solution.py:352
  145.5 19.3 %collective-permute-start.6 = (bf16[2,256,128]{2,1,0:T(8,128)(2,1)}, bf16[2,256,128]{2,1,0:T(8,128)(2,1)}, u32[]{:S(2)}, u32[]{:S(2)}) collective-permute-start(bf16[2,256,128]{2,1,0:T(8,128)(2,1)} %get-tuple-element.48), channel_id=1, source_target_pairs={{0,30},{2,28},{4,26},{6,24},{8,6},{10,4},{12,2},{14,0},{16,14},{18... | collective-permute-start | bytes 393224 | tf_op jit(solution)/shard_map/ppermute | solution.py:352
  156.1 17.3 %collective-permute-start.28 = (bf16[2,256,128]{2,1,0:T(8,128)(2,1)}, bf16[2,256,128]{2,1,0:T(8,128)(2,1)}, u32[]{:S(2)}, u32[]{:S(2)}) collective-permute-start(bf16[2,256,128]{2,1,0:T(8,128)(2,1)} %get-tuple-element.74), channel_id=1, source_target_pairs={{0,2},{2,0},{4,6},{6,4},{8,10},{10,8},{12,14},{14,12},{16,18},{18,... | collective-permute-start | bytes 393224 | tf_op jit(solution)/shard_map/ppermute | solution.py:352
  156.3 17.1 %collective-permute-start.29 = (bf16[2,256,128]{2,1,0:T(8,128)(2,1)}, bf16[2,256,128]{2,1,0:T(8,128)(2,1)}, u32[]{:S(2)}, u32[]{:S(2)}) collective-permute-start(bf16[2,256,128]{2,1,0:T(8,128)(2,1)} %get-tuple-element.75), channel_id=1, source_target_pairs={{0,4},{2,6},{4,0},{6,2},{8,12},{10,14},{12,8},{14,10},{16,20},{18,... | collective-permute-start | bytes 393224 | tf_op jit(solution)/shard_map/ppermute | solution.py:352
  156.4 17.2 %collective-permute-start.30 = (bf16[2,256,128]{2,1,0:T(8,128)(2,1)}, bf16[2,256,128]{2,1,0:T(8,128)(2,1)}, u32[]{:S(2)}, u32[]{:S(2)}) collective-permute-start(bf16[2,256,128]{2,1,0:T(8,128)(2,1)} %get-tuple-element.76), channel_id=1, source_target_pairs={{0,6},{2,4},{4,2},{6,0},{8,14},{10,12},{12,10},{14,8},{16,22},{18,... | collective-permute-start | bytes 393224 | tf_op jit(solution)/shard_map/ppermute | solution.py:352
  164.7 6.6 %collective-permute-start.21 = (bf16[1,256,128]{2,1,0:T(8,128)(2,1)}, bf16[1,256,128]{2,1,0:T(8,128)(2,1)}, u32[]{:S(2)}, u32[]{:S(2)}) collective-permute-start(bf16[1,256,128]{2,1,0:T(8,128)(2,1)} %get-tuple-element.66), channel_id=1, source_target_pairs={{0,2},{2,0},{4,6},{6,4},{8,10},{10,8},{12,14},{14,12},{16,18},{18,... | collective-permute-start | bytes 196616 | tf_op jit(solution)/shard_map/ppermute | solution.py:352
  164.8 12.6 %collective-permute-start.22 = (bf16[1,256,128]{2,1,0:T(8,128)(2,1)}, bf16[1,256,128]{2,1,0:T(8,128)(2,1)}, u32[]{:S(2)}, u32[]{:S(2)}) collective-permute-start(bf16[1,256,128]{2,1,0:T(8,128)(2,1)} %get-tuple-element.67), channel_id=1, source_target_pairs={{0,4},{2,6},{4,0},{6,2},{8,12},{10,14},{12,8},{14,10},{16,20},{18,... | collective-permute-start | bytes 196616 | tf_op jit(solution)/shard_map/ppermute | solution.py:352
  171.3 6.1 %collective-permute-start.23 = (bf16[1,256,128]{2,1,0:T(8,128)(2,1)}, bf16[1,256,128]{2,1,0:T(8,128)(2,1)}, u32[]{:S(2)}, u32[]{:S(2)}) collective-permute-start(bf16[1,256,128]{2,1,0:T(8,128)(2,1)} %get-tuple-element.68), channel_id=1, source_target_pairs={{0,6},{2,4},{4,2},{6,0},{8,14},{10,12},{12,10},{14,8},{16,22},{18,... | collective-permute-start | bytes 196616 | tf_op jit(solution)/shard_map/ppermute | solution.py:352
  173.4 4.0 %collective-permute-start.14 = (bf16[1,256,128]{2,1,0:T(8,128)(2,1)}, bf16[1,256,128]{2,1,0:T(8,128)(2,1)}, u32[]{:S(2)}, u32[]{:S(2)}) collective-permute-start(bf16[1,256,128]{2,1,0:T(8,128)(2,1)} %get-tuple-element.58), channel_id=1, source_target_pairs={{0,2},{2,0},{4,6},{6,4},{8,10},{10,8},{12,14},{14,12},{16,18},{18,... | collective-permute-start | bytes 196616 | tf_op jit(solution)/shard_map/ppermute | solution.py:352
  173.4 4.0 %collective-permute-start.15 = (bf16[1,256,128]{2,1,0:T(8,128)(2,1)}, bf16[1,256,128]{2,1,0:T(8,128)(2,1)}, u32[]{:S(2)}, u32[]{:S(2)}) collective-permute-start(bf16[1,256,128]{2,1,0:T(8,128)(2,1)} %get-tuple-element.59), channel_id=1, source_target_pairs={{0,4},{2,6},{4,0},{6,2},{8,12},{10,14},{12,8},{14,10},{16,20},{18,... | collective-permute-start | bytes 196616 | tf_op jit(solution)/shard_map/ppermute | solution.py:352
  173.6 5.4 %collective-permute-start.16 = (bf16[1,256,128]{2,1,0:T(8,128)(2,1)}, bf16[1,256,128]{2,1,0:T(8,128)(2,1)}, u32[]{:S(2)}, u32[]{:S(2)}) collective-permute-start(bf16[1,256,128]{2,1,0:T(8,128)(2,1)} %get-tuple-element.60), channel_id=1, source_target_pairs={{0,6},{2,4},{4,2},{6,0},{8,14},{10,12},{12,10},{14,8},{16,22},{18,... | collective-permute-start | bytes 196616 | tf_op jit(solution)/shard_map/ppermute | solution.py:352

commit v3 on v2

--- a/solution.py
+++ b/solution.py
@@ -220,7 +220,7 @@
         acc_ref[0, 0, i] = weigh(tiles, peak, slot, dtype)
 
 
-def near(place, slopes, qs, ups, owns, bias, chunk0, chunks, total, head_width):
+def near(place, slopes, qs, ups, owns, bias, chunk0, chunks, head_width):
     plane = len(qs)
     _, rows, _ = qs[0].shape
     win = bias.shape[0] // 2
@@ -230,15 +230,13 @@
     key_spec = pl.BlockSpec(block, lambda c, h: (c, 0, 0))
     value_spec = pl.BlockSpec(block, lambda c, h: (chunks + c, 0, 0))
     query_spec = pl.BlockSpec(block, lambda c, h: (chunk0 + c, 0, 0))
-    own_key = pl.BlockSpec(block, lambda c, h: (chunk0 + c, 0, 0))
-    own_value = pl.BlockSpec(block, lambda c, h: (total + chunk0 + c, 0, 0))
     out = (chunks, heads, plane, rows, LANES)
     out_spec = pl.BlockSpec((1, 1) + out[2:], lambda c, h: (c, h, 0, 0, 0))
     return pl.pallas_call(
         functools.partial(near_kernel, win, plane, chunk0, head_width),
         grid=(chunks, heads),
         in_specs=[SMEM, SMEM] + [query_spec] * plane + [key_spec] * plane + [value_spec] * plane
-        + [own_key] * plane + [own_value] * plane
+        + [key_spec] * plane + [value_spec] * plane
         + [pl.BlockSpec(bias.shape, lambda c, h: (0, 0, 0), pipeline_mode=pl.Buffered(1))],
         out_specs=[out_spec, out_spec],
         out_shape=[jax.ShapeDtypeStruct(out, jnp.float32)] * 2,
@@ -305,12 +303,12 @@
     heads = LANES // head_width
     block = (1, rows, LANES)
     pairs = chunks * heads * rows * rows * (plane * (plane + 1) // 2)
-    acc, peak, base = before
+    acc, peak = before
     key_spec = pl.BlockSpec(block, lambda c: (c, 0, 0))
     value_spec = pl.BlockSpec(block, lambda c: (chunks + c, 0, 0))
     query_spec = pl.BlockSpec(block, lambda c: (chunk0 + c, 0, 0))
     near_spec = pl.BlockSpec(
-        (1, heads, plane, rows, LANES), lambda c: (chunk0 - base + c, 0, 0, 0, 0)
+        (1, heads, plane, rows, LANES), lambda c: (c, 0, 0, 0, 0)
     )
     return pl.pallas_call(
         functools.partial(far_kernel, win, plane, chunk0, head_width),
@@ -342,15 +340,16 @@
     head_width = width // slopes.shape[0]
     chunks = width // (plane * LANES)
 
-    def send(arrays, step):
-        out = []
-        for k, x in enumerate(arrays):
-            if k == 0 and step == 0:
-                out.append(x)
-                continue
-            pairs = [(i, ((i + step * plane) % count) ^ k) for i in range(count)]
+    def send(arrays):
+        out = list(arrays[:1])
+        for k, x in enumerate(arrays[1:], 1):
+            pairs = [(i, i ^ k) for i in range(count)]
             out.append(lax.ppermute(x, "seq", pairs))
         return out
+
+    def shift(arrays, step):
+        pairs = [(i, (i + step * plane) % count) for i in range(count)]
+        return [lax.ppermute(x, "seq", pairs) for x in arrays]
 
     place = (lax.axis_index("seq") % plane).astype(jnp.int32).reshape(1)
     data = dict(q=queries, k=key_rows, v=values)
@@ -359,22 +358,22 @@
         span = range(start, start + size)
         return [("k", c) for c in span] + [("v", c) for c in span]
 
-    groups = [(0, chunks - 2), (chunks - 2, 1), (chunks - 1, 1)]
-    kv_only = dict(k=key_rows, v=values)
-    (packed,) = pack(kv_only, [kv(0, chunks)], plane, place)
-    rest = pack(data, [[("q", c) for c in range(chunks)]] + [kv(*g) for g in groups], plane, place)
-    ups = send(packed, 1)
-    qs = send(rest[0], 0)
-    owns = send(packed, 0)
+    groups = [(0, chunks - 1), (chunks - 1, 1)]
+    (first,) = pack(dict(k=key_rows, v=values), [kv(*groups[0])], plane, place)
+    second, query = pack(data, [kv(*groups[1]), [("q", c) for c in range(chunks)]], plane, place)
+    owns = [send(x) for x in (first, second)]
+    qs = send(query)
     near_bias, far_bias = bias_window(bias_tiles, buckets)
-    downs = [send(x, -1) for x in rest[1:]]
-    sums = near(place, slopes, qs, ups, owns, near_bias, 0, chunks, chunks, head_width)
-    back = []
+    ups = [shift(x, 1) for x in owns]
+    downs = [shift(x, -1) for x in owns]
+    sums, back = [], []
     for g, (start, size) in enumerate(groups):
-        outs = far(place, slopes, qs, downs[g], far_bias, (*sums, 0), start, size, head_width)
-        back.append(send(outs, 0))
+        sums.append(near(place, slopes, qs, ups[g], owns[g], near_bias, start, size, head_width))
+    for g, (start, size) in enumerate(groups):
+        outs = far(place, slopes, qs, downs[g], far_bias, sums[g], start, size, head_width)
+        back.append(send(outs))
     most = unpack(place, back[:1], 0, chunks, None)
-    return unpack(place, back[1:], chunks - 2, chunks, most)
+    return unpack(place, back[1:], chunks - 1, chunks, most)
 
 
 def solution(mesh):

time: 182 us -> 160 us (0.88)
  starting transfers between devices: 62.3 us -> 39.5 us
  waiting for transfers between devices: 52 us -> 53.9 us
    ppermute x31 -> x15, starting transfers between devices: 62.3 us -> 20 us  [send(): out.append(lax.ppermute(x, 'seq', pairs))]
    ppermute x0 -> x16, waiting for transfers between devices: none -> 22.6 us  [shift(): return [lax.ppermute(x, 'seq', pairs) for x in arrays]]
    ppermute x31 -> x15, waiting for transfers between devices: 52 us -> 31.4 us  [send(): out.append(lax.ppermute(x, 'seq', pairs))]
    ppermute x0 -> x16, starting transfers between devices: none -> 19.4 us  [shift(): return [lax.ppermute(x, 'seq', pairs) for x in arrays]]
    pallas_call x1 -> x2, Pallas kernels: 31 us -> 33.8 us  [near(): pl.pallas_call(functools.partial(near_kernel, win, plane, chunk0, head_wi...]
    pallas_call x3 -> x2, Pallas kernels: 22.7 us -> 19.9 us  [far(): pl.pallas_call(functools.partial(far_kernel, win, plane, chunk0, head_wid...]
  transfers between devices with their start and end apart: 31 -> 31, of which waited for: 6 -> 8; matrix products, arithmetic and copies ran while one was open for 0% -> 0% of each run, Pallas kernels for 34% -> 38%
where the time goes in v3:
time: 160 us; the launch traced here: 159 us
  Pallas kernels  65.3 us (41%)
  waiting for transfers between devices  53.9 us (34%)
  starting transfers between devices  39.5 us (25%)
    pallas_call x2, Pallas kernels, near(): pl.pallas_call(functools.partial(near_kernel, win, plane, chunk0, head_wi...  33.8 us
    ppermute x15, waiting for transfers between devices, send(): out.append(lax.ppermute(x, 'seq', pairs))  31.4 us
    ppermute x16, waiting for transfers between devices, shift(): return [lax.ppermute(x, 'seq', pairs) for x in arrays]  22.6 us
    ppermute x15, starting transfers between devices, send(): out.append(lax.ppermute(x, 'seq', pairs))  20 us
    pallas_call x2, Pallas kernels, far(): pl.pallas_call(functools.partial(far_kernel, win, plane, chunk0, head_wid...  19.9 us
    ppermute x16, starting transfers between devices, shift(): return [lax.ppermute(x, 'seq', pairs) for x in arrays]  19.4 us
    pallas_call x2, Pallas kernels, pack(): pl.pallas_call(functools.partial(pack_kernel, plane, groups, names), in_s...  5.01 us
    pallas_call x2, Pallas kernels, unpack(): pl.pallas_call(functools.partial(unpack_kernel, plane, chunk0, chunks, le...  3.66 us
  transfers between devices with their start and end apart: 31, of which 8 were waited for; matrix products, arithmetic and copies ran while one was open for 0% of the time, Pallas kernels for 38%

profile of v3, /device:TPU:1, one launch (start us, length us, event | category | flops | bytes accessed | tf_op | source)
XLA Modules:
  0.0 159.0 jit_solution(6892865120225606995)
XLA Ops:
  0.0 2.7 %shard_map.64 = (bf16[2,256,128]{2,1,0:T(8,128)(2,1)}, bf16[2,256,128]{2,1,0:T(8,128)(2,1)}, bf16[2,256,128]{2,1,0:T(8,128)(2,1)}, bf16[2,256,128]{2,1,0:T(8,128...) custom-call(s32[1]{0:T(128)} %bitcast.place_ref, ...), custom_call_target="tpu_custom_call" | custom-call | bytes 3145728 | tf_op jit(solution)/shard_map/pallas_call | solution.py:84
  2.7 0.1 collective-permute-start.4
  2.8 2.7 %collective-permute-start.6 = (bf16[2,256,128]{2,1,0:T(8,128)(2,1)}, bf16[2,256,128]{2,1,0:T(8,128)(2,1)}, u32[]{:S(2)}, u32[]{:S(2)}) collective-permute-start(bf16[2,256,128]{2,1,0:T(8,128)(2,1)} %get-tuple-element.37), channel_id=1, source_target_pairs={{0,4},{2,6},{4,0},{6,2},{8,12},{10,14},{12,8},{14,10},{16,20},{18,... | collective-permute-start | bytes 393224 | tf_op jit(solution)/shard_map/ppermute | solution.py:347
  5.5 2.3 %shard_map.65 = (bf16[6,256,128]{2,1,0:T(8,128)(2,1)}, bf16[6,256,128]{2,1,0:T(8,128)(2,1)}, bf16[6,256,128]{2,1,0:T(8,128)(2,1)}, bf16[6,256,128]{2,1,0:T(8,128)(2,1)}) custom-call(s32[1]{0:T(128)} %bitcast.place_ref, bf16[256,2048]{1,0:T(8,128)(2,1)} %refs_0_.3, bf16[256,2048]{1,0:T(8,128)(2,1)} %refs_1_.3), custom_call_target="tpu_custom_call" | custom-call | bytes 3145728 | tf_op jit(solution)/shard_map/pallas_call | solution.py:84
  7.8 0.4 collective-permute-start.18
  8.2 0.0 collective-permute-start.20
  8.2 1.8 %collective-permute-start.22 = (bf16[6,256,128]{2,1,0:T(8,128)(2,1)}, bf16[6,256,128]{2,1,0:T(8,128)(2,1)}, u32[]{:S(2)}, u32[]{:S(2)}) collective-permute-start(bf16[6,256,128]{2,1,0:T(8,128)(2,1)} %get-tuple-element.50), channel_id=1, source_target_pairs={{0,6},{2,4},{4,2},{6,0},{8,14},{10,12},{12,10},{14,8},{16,22},{18,... | collective-permute-start | bytes 1179656 | tf_op jit(solution)/shard_map/ppermute | solution.py:347
  10.0 0.0 collective-permute-start.8
  10.0 0.0 collective-permute-done.6.refs_14_.refs_18_
  10.0 0.4 collective-permute-start
  10.4 20.2 %collective-permute-done.8.refs_15_.refs_19_ = bf16[2,256,128]{2,1,0:T(8,128)(2,1)} collective-permute-done((bf16[2,256,128]{2,1,0:T(8,128)(2,1)}, bf16[2,256,128]{2,1,0:T(8,128)(2,1)}, u32[]{:S(2)}, u32[]{:S(2)}) %collective-permute-start.8) | collective-permute-done | bytes 131104 | tf_op jit(solution)/shard_map/ppermute | solution.py:347
  30.6 0.1 collective-permute-start.1
  30.7 1.5 collective-permute-start.24
  32.2 1.3 collective-permute-start.25
  33.5 1.3 collective-permute-start.26
  34.8 0.1 collective-permute-start.27
  34.8 3.9 %collective-permute-done.1.refs_2_ = bf16[4,256,128]{2,1,0:T(8,128)(2,1)} collective-permute-done((bf16[4,256,128]{2,1,0:T(8,128)(2,1)}, bf16[4,256,128]{2,1,0:T(8,128)(2,1)}, u32[]{:S(2)}, u32[]{:S(2)}) %collective-permute-start.1) | collective-permute-done | bytes 262176 | tf_op jit(solution)/shard_map/ppermute | solution.py:347
  38.7 0.9 collective-permute-start.2
  39.6 3.0 %bias_window.1 = (f32[8,256,256]{2,1,0:T(8,128)}, f32[4,256,256]{2,1,0:T(8,128)}) custom-call(s32[5]{0:T(128)} %buckets.1, bf16[3,256,256]{2,1,0:T(8,128)(2,1)} %tile_ref.1), custom_call_target="tpu_custom_call" | custom-call | tf_op jit(solution)/shard_map/bias_window/pallas_call | solution.py:31
  42.5 5.1 %collective-permute-done.2.refs_3_ = bf16[4,256,128]{2,1,0:T(8,128)(2,1)} collective-permute-done((bf16[4,256,128]{2,1,0:T(8,128)(2,1)}, bf16[4,256,128]{2,1,0:T(8,128)(2,1)}, u32[]{:S(2)}, u32[]{:S(2)}) %collective-permute-start.2) | collective-permute-done | bytes 262176 | tf_op jit(solution)/shard_map/ppermute | solution.py:347
  47.7 3.3 %collective-permute-start.17 = (bf16[6,256,128]{2,1,0:T(8,128)(2,1)}, bf16[6,256,128]{2,1,0:T(8,128)(2,1)}, u32[]{:S(2)}, u32[]{:S(2)}) collective-permute-start(bf16[6,256,128]{2,1,0:T(8,128)(2,1)} %get-tuple-element.47.refs_12_.refs_16_), channel_id=1, source_target_pairs={{0,24},{2,26},{4,28},{6,30},{8,0},{10,2},{12,4},{14,6},{16,8},{18,... | collective-permute-start | bytes 1179656 | tf_op jit(solution)/shard_map/ppermute | solution.py:352
  51.0 1.0 collective-permute-done.25.refs_5_.refs_9_
  52.0 2.3 %collective-permute-start.19 = (bf16[6,256,128]{2,1,0:T(8,128)(2,1)}, bf16[6,256,128]{2,1,0:T(8,128)(2,1)}, u32[]{:S(2)}, u32[]{:S(2)}) collective-permute-start(bf16[6,256,128]{2,1,0:T(8,128)(2,1)} %collective-permute-done.18.refs_13_.refs_17_), channel_id=1, source_target_pairs={{0,24},{2,26},{4,28},{6,30},{8,0},{10,2},{12,4},{14,6},{16,8},{18,... | collective-permute-start | bytes 1179656 | tf_op jit(solution)/shard_map/ppermute | solution.py:352
  54.3 6.2 %collective-permute-done.26.refs_6_.refs_10_ = bf16[6,256,128]{2,1,0:T(8,128)(2,1)} collective-permute-done((bf16[6,256,128]{2,1,0:T(8,128)(2,1)}, bf16[6,256,128]{2,1,0:T(8,128)(2,1)}, u32[]{:S(2)}, u32[]{:S(2)}) %collective-permute-start.26) | collective-permute-done | bytes 393248 | tf_op jit(solution)/shard_map/ppermute | solution.py:352
  60.5 1.2 collective-permute-start.21
  61.7 7.2 %collective-permute-done.27.refs_7_.refs_11_ = bf16[6,256,128]{2,1,0:T(8,128)(2,1)} collective-permute-done((bf16[6,256,128]{2,1,0:T(8,128)(2,1)}, bf16[6,256,128]{2,1,0:T(8,128)(2,1)}, u32[]{:S(2)}, u32[]{:S(2)}) %collective-permute-start.27) | collective-permute-done | bytes 393248 | tf_op jit(solution)/shard_map/ppermute | solution.py:352
  68.9 1.4 collective-permute-start.23
  70.3 23.9 %near.3 = (f32[3,2,4,256,128]{4,3,2,1,0:T(8,128)}, f32[3,2,4,256,128]{4,3,2,1,0:T(8,128)}) custom-call(s32[1]{0:T(128)} %bitcast.place_ref, f32[32]{0:T(128)} %slopes.7, bf16[4,256,128]{2,1,0:T(8,128)(2,1)} %get-tuple-element.31.refs_0_, bf16[4,256,128]{2,1,0:T(8,128)(2,1)} %collective-permute-done.refs_1_, ...), custom_call_target="tpu_custom_call" | custom-call | flops 5234491392 | bytes 12582912 | tf_op jit(solution)/shard_map/near/pallas_call | solution.py:235
  94.3 0.1 collective-permute-start.3
  94.4 1.4 collective-permute-start.11
  95.8 1.9 %collective-permute-start.5 = (bf16[2,256,128]{2,1,0:T(8,128)(2,1)}, bf16[2,256,128]{2,1,0:T(8,128)(2,1)}, u32[]{:S(2)}, u32[]{:S(2)}) collective-permute-start(bf16[2,256,128]{2,1,0:T(8,128)(2,1)} %collective-permute-done.4.refs_13_.refs_17_), channel_id=1, source_target_pairs={{0,24},{2,26},{4,28},{6,30},{8,0},{10,2},{12,4},{14,6},{16,8},{18,... | collective-permute-start | bytes 393224 | tf_op jit(solution)/shard_map/ppermute | solution.py:352
  97.7 0.1 collective-permute-start.12
  97.7 8.1 %collective-permute-done.23.refs_7_.refs_11_ = bf16[6,256,128]{2,1,0:T(8,128)(2,1)} collective-permute-done((bf16[6,256,128]{2,1,0:T(8,128)(2,1)}, bf16[6,256,128]{2,1,0:T(8,128)(2,1)}, u32[]{:S(2)}, u32[]{:S(2)}) %collective-permute-start.23) | collective-permute-done | bytes 393248 | tf_op jit(solution)/shard_map/ppermute | solution.py:352
  105.9 0.3 collective-permute-start.13
  106.2 13.5 %far.3 = (bf16[3,256,128]{2,1,0:T(8,128)(2,1)}, bf16[3,256,128]{2,1,0:T(8,128)(2,1)}, bf16[3,256,128]{2,1,0:T(8,128)(2,1)}, bf16[3,256,128]{2,1,0:T(8,128)(2,1)}) custom-call(s32[1]{0:T(128)} %bitcast.place_ref, f32[32]{0:T(128)} %slopes.7, bf16[4,256,128]{2,1,0:T(8,128)(2,1)} %get-tuple-element.31.refs_0_, ...), custom_call_target="tpu_custom_call" | custom-call | flops 2013265920 | bytes 12582912 | tf_op jit(solution)/shard_map/far/pallas_call | solution.py:313
  119.7 3.0 %collective-permute-start.7 = (bf16[2,256,128]{2,1,0:T(8,128)(2,1)}, bf16[2,256,128]{2,1,0:T(8,128)(2,1)}, u32[]{:S(2)}, u32[]{:S(2)}) collective-permute-start(bf16[2,256,128]{2,1,0:T(8,128)(2,1)} %collective-permute-done.6.refs_14_.refs_18_), channel_id=1, source_target_pairs={{0,24},{2,26},{4,28},{6,30},{8,0},{10,2},{12,4},{14,6},{16,8},{18,... | collective-permute-start | bytes 393224 | tf_op jit(solution)/shard_map/ppermute | solution.py:352
  122.7 0.3 collective-permute-start.9
  122.9 9.9 %collective-permute-start.28 = (bf16[3,256,128]{2,1,0:T(8,128)(2,1)}, bf16[3,256,128]{2,1,0:T(8,128)(2,1)}, u32[]{:S(2)}, u32[]{:S(2)}) collective-permute-start(bf16[3,256,128]{2,1,0:T(8,128)(2,1)} %get-tuple-element.54), channel_id=1, source_target_pairs={{0,2},{2,0},{4,6},{6,4},{8,10},{10,8},{12,14},{14,12},{16,18},{18,... | collective-permute-start | bytes 589832 | tf_op jit(solution)/shard_map/ppermute | solution.py:347
  132.8 1.2 collective-permute-start.29
  134.1 0.5 collective-permute-start.30
  134.5 9.9 %near.2 = (f32[1,2,4,256,128]{4,3,2,1,0:T(8,128)}, f32[1,2,4,256,128]{4,3,2,1,0:T(8,128)}) custom-call(s32[1]{0:T(128)} %bitcast.place_ref, f32[32]{0:T(128)} %slopes.7, bf16[4,256,128]{2,1,0:T(8,128)(2,1)} %get-tuple-element.31.refs_0_, bf16[4,256,128]{2,1,0:T(8,128)(2,1)} %collective-permute-done.refs_1_, ...), custom_call_target="tpu_custom_call" | custom-call | flops 1744830464 | bytes 4194304 | tf_op jit(solution)/shard_map/near/pallas_call | solution.py:235
  144.5 6.4 %far.2 = (bf16[1,256,128]{2,1,0:T(8,128)(2,1)}, bf16[1,256,128]{2,1,0:T(8,128)(2,1)}, bf16[1,256,128]{2,1,0:T(8,128)(2,1)}, bf16[1,256,128]{2,1,0:T(8,128)(2,1)}) custom-call(s32[1]{0:T(128)} %bitcast.place_ref, f32[32]{0:T(128)} %slopes.7, bf16[4,256,128]{2,1,0:T(8,128)(2,1)} %get-tuple-element.31.refs_0_, ...), custom_call_target="tpu_custom_call" | custom-call | flops 671088640 | bytes 4194304 | tf_op jit(solution)/shard_map/far/pallas_call | solution.py:313
  150.9 0.2 collective-permute-start.14
  151.1 1.2 collective-permute-start.15
  152.3 0.8 collective-permute-start.16
  153.0 2.0 %shard_map.66.refs_4_ = bf16[256,2048]{1,0:T(8,128)(2,1)} custom-call(s32[1]{0:T(128)} %bitcast.place_ref, bf16[3,256,128]{2,1,0:T(8,128)(2,1)} %get-tuple-element.53.refs_0_, bf16[3,256,128]{2,1,0:T(8,128)(2,1)} %collective-permute-done.28.refs_1_, bf16[3,256,128]{2,1,0:T(8,128)(2,1)} %collective-permute-done.29.refs_2_, ...), custom_call_target="tpu_custom_call" | custom-call | bytes 1572864 | tf_op jit(solution)/shard_map/pallas_call | solution.py:141
  155.1 2.1 %collective-permute-done.16.refs_3_ = bf16[1,256,128]{2,1,0:T(8,128)(2,1)} collective-permute-done((bf16[1,256,128]{2,1,0:T(8,128)(2,1)}, bf16[1,256,128]{2,1,0:T(8,128)(2,1)}, u32[]{:S(2)}, u32[]{:S(2)}) %collective-permute-start.16) | collective-permute-done | bytes 65568 | tf_op jit(solution)/shard_map/ppermute | solution.py:347
  157.1 1.7 %shard_map.67 = bf16[256,2048]{1,0:T(8,128)(2,1)} custom-call(s32[1]{0:T(128)} %bitcast.place_ref, bf16[1,256,128]{2,1,0:T(8,128)(2,1)} %get-tuple-element.43.refs_0_, bf16[1,256,128]{2,1,0:T(8,128)(2,1)} %collective-permute-done.14.refs_1_, bf16[1,256,128]{2,1,0:T(8,128)(2,1)} %collective-permute-done.15.refs_2_, ...), custom_call_target="tpu_custom_call", output_to_operand_aliasing={{}: (5, {})} | custom-call | bytes 524288 | tf_op jit(solution)/shard_map/pallas_call | solution.py:141
  (23 shorter events, 0.1 us)
Async XLA Ops:
  2.7 7.3 %collective-permute-start.4 = (bf16[2,256,128]{2,1,0:T(8,128)(2,1)}, bf16[2,256,128]{2,1,0:T(8,128)(2,1)}, u32[]{:S(2)}, u32[]{:S(2)}) collective-permute-start(bf16[2,256,128]{2,1,0:T(8,128)(2,1)} %get-tuple-element.36), channel_id=1, source_target_pairs={{0,2},{2,0},{4,6},{6,4},{8,10},{10,8},{12,14},{14,12},{16,18},{18,... | collective-permute-start | bytes 393224 | tf_op jit(solution)/shard_map/ppermute | solution.py:347
  2.8 7.2 %collective-permute-start.6 = (bf16[2,256,128]{2,1,0:T(8,128)(2,1)}, bf16[2,256,128]{2,1,0:T(8,128)(2,1)}, u32[]{:S(2)}, u32[]{:S(2)}) collective-permute-start(bf16[2,256,128]{2,1,0:T(8,128)(2,1)} %get-tuple-element.37), channel_id=1, source_target_pairs={{0,4},{2,6},{4,0},{6,2},{8,12},{10,14},{12,8},{14,10},{16,20},{18,... | collective-permute-start | bytes 393224 | tf_op jit(solution)/shard_map/ppermute | solution.py:347
  7.8 24.4 %collective-permute-start.18 = (bf16[6,256,128]{2,1,0:T(8,128)(2,1)}, bf16[6,256,128]{2,1,0:T(8,128)(2,1)}, u32[]{:S(2)}, u32[]{:S(2)}) collective-permute-start(bf16[6,256,128]{2,1,0:T(8,128)(2,1)} %get-tuple-element.48), channel_id=1, source_target_pairs={{0,2},{2,0},{4,6},{6,4},{8,10},{10,8},{12,14},{14,12},{16,18},{18,... | collective-permute-start | bytes 1179656 | tf_op jit(solution)/shard_map/ppermute | solution.py:347
  8.2 25.3 %collective-permute-start.20 = (bf16[6,256,128]{2,1,0:T(8,128)(2,1)}, bf16[6,256,128]{2,1,0:T(8,128)(2,1)}, u32[]{:S(2)}, u32[]{:S(2)}) collective-permute-start(bf16[6,256,128]{2,1,0:T(8,128)(2,1)} %get-tuple-element.49), channel_id=1, source_target_pairs={{0,4},{2,6},{4,0},{6,2},{8,12},{10,14},{12,8},{14,10},{16,20},{18,... | collective-permute-start | bytes 1179656 | tf_op jit(solution)/shard_map/ppermute | solution.py:347
  8.2 26.5 %collective-permute-start.22 = (bf16[6,256,128]{2,1,0:T(8,128)(2,1)}, bf16[6,256,128]{2,1,0:T(8,128)(2,1)}, u32[]{:S(2)}, u32[]{:S(2)}) collective-permute-start(bf16[6,256,128]{2,1,0:T(8,128)(2,1)} %get-tuple-element.50), channel_id=1, source_target_pairs={{0,6},{2,4},{4,2},{6,0},{8,14},{10,12},{12,10},{14,8},{16,22},{18,... | collective-permute-start | bytes 1179656 | tf_op jit(solution)/shard_map/ppermute | solution.py:347
  10.0 20.6 %collective-permute-start.8 = (bf16[2,256,128]{2,1,0:T(8,128)(2,1)}, bf16[2,256,128]{2,1,0:T(8,128)(2,1)}, u32[]{:S(2)}, u32[]{:S(2)}) collective-permute-start(bf16[2,256,128]{2,1,0:T(8,128)(2,1)} %get-tuple-element.38), channel_id=1, source_target_pairs={{0,6},{2,4},{4,2},{6,0},{8,14},{10,12},{12,10},{14,8},{16,22},{18,... | collective-permute-start | bytes 393224 | tf_op jit(solution)/shard_map/ppermute | solution.py:347
  10.0 20.6 %collective-permute-start = (bf16[4,256,128]{2,1,0:T(8,128)(2,1)}, bf16[4,256,128]{2,1,0:T(8,128)(2,1)}, u32[]{:S(2)}, u32[]{:S(2)}) collective-permute-start(bf16[4,256,128]{2,1,0:T(8,128)(2,1)} %get-tuple-element.32), channel_id=1, source_target_pairs={{0,2},{2,0},{4,6},{6,4},{8,10},{10,8},{12,14},{14,12},{16,18},{18,... | collective-permute-start | bytes 786440 | tf_op jit(solution)/shard_map/ppermute | solution.py:347
  30.6 8.1 %collective-permute-start.1 = (bf16[4,256,128]{2,1,0:T(8,128)(2,1)}, bf16[4,256,128]{2,1,0:T(8,128)(2,1)}, u32[]{:S(2)}, u32[]{:S(2)}) collective-permute-start(bf16[4,256,128]{2,1,0:T(8,128)(2,1)} %get-tuple-element.33), channel_id=1, source_target_pairs={{0,4},{2,6},{4,0},{6,2},{8,12},{10,14},{12,8},{14,10},{16,20},{18,... | collective-permute-start | bytes 786440 | tf_op jit(solution)/shard_map/ppermute | solution.py:347
  30.7 20.3 %collective-permute-start.24 = (bf16[6,256,128]{2,1,0:T(8,128)(2,1)}, bf16[6,256,128]{2,1,0:T(8,128)(2,1)}, u32[]{:S(2)}, u32[]{:S(2)}) collective-permute-start(bf16[6,256,128]{2,1,0:T(8,128)(2,1)} %get-tuple-element.47.refs_12_.refs_16_), channel_id=1, source_target_pairs={{0,8},{2,10},{4,12},{6,14},{8,16},{10,18},{12,20},{14,22},{16,24},... | collective-permute-start | bytes 1179656 | tf_op jit(solution)/shard_map/ppermute | solution.py:352
  32.2 19.8 %collective-permute-start.25 = (bf16[6,256,128]{2,1,0:T(8,128)(2,1)}, bf16[6,256,128]{2,1,0:T(8,128)(2,1)}, u32[]{:S(2)}, u32[]{:S(2)}) collective-permute-start(bf16[6,256,128]{2,1,0:T(8,128)(2,1)} %collective-permute-done.18.refs_13_.refs_17_), channel_id=1, source_target_pairs={{0,8},{2,10},{4,12},{6,14},{8,16},{10,18},{12,20},{14,22},{16,24},... | collective-permute-start | bytes 1179656 | tf_op jit(solution)/shard_map/ppermute | solution.py:352
  33.5 27.0 %collective-permute-start.26 = (bf16[6,256,128]{2,1,0:T(8,128)(2,1)}, bf16[6,256,128]{2,1,0:T(8,128)(2,1)}, u32[]{:S(2)}, u32[]{:S(2)}) collective-permute-start(bf16[6,256,128]{2,1,0:T(8,128)(2,1)} %collective-permute-done.20.refs_14_.refs_18_), channel_id=1, source_target_pairs={{0,8},{2,10},{4,12},{6,14},{8,16},{10,18},{12,20},{14,22},{16,24},... | collective-permute-start | bytes 1179656 | tf_op jit(solution)/shard_map/ppermute | solution.py:352
  34.8 34.1 %collective-permute-start.27 = (bf16[6,256,128]{2,1,0:T(8,128)(2,1)}, bf16[6,256,128]{2,1,0:T(8,128)(2,1)}, u32[]{:S(2)}, u32[]{:S(2)}) collective-permute-start(bf16[6,256,128]{2,1,0:T(8,128)(2,1)} %collective-permute-done.22.refs_15_.refs_19_), channel_id=1, source_target_pairs={{0,8},{2,10},{4,12},{6,14},{8,16},{10,18},{12,20},{14,22},{16,24},... | collective-permute-start | bytes 1179656 | tf_op jit(solution)/shard_map/ppermute | solution.py:352
  38.7 9.0 %collective-permute-start.2 = (bf16[4,256,128]{2,1,0:T(8,128)(2,1)}, bf16[4,256,128]{2,1,0:T(8,128)(2,1)}, u32[]{:S(2)}, u32[]{:S(2)}) collective-permute-start(bf16[4,256,128]{2,1,0:T(8,128)(2,1)} %get-tuple-element.34), channel_id=1, source_target_pairs={{0,6},{2,4},{4,2},{6,0},{8,14},{10,12},{12,10},{14,8},{16,22},{18,... | collective-permute-start | bytes 786440 | tf_op jit(solution)/shard_map/ppermute | solution.py:347
  47.7 46.7 %collective-permute-start.17 = (bf16[6,256,128]{2,1,0:T(8,128)(2,1)}, bf16[6,256,128]{2,1,0:T(8,128)(2,1)}, u32[]{:S(2)}, u32[]{:S(2)}) collective-permute-start(bf16[6,256,128]{2,1,0:T(8,128)(2,1)} %get-tuple-element.47.refs_12_.refs_16_), channel_id=1, source_target_pairs={{0,24},{2,26},{4,28},{6,30},{8,0},{10,2},{12,4},{14,6},{16,8},{18,... | collective-permute-start | bytes 1179656 | tf_op jit(solution)/shard_map/ppermute | solution.py:352
  51.0 43.2 %collective-permute-start.10 = (bf16[2,256,128]{2,1,0:T(8,128)(2,1)}, bf16[2,256,128]{2,1,0:T(8,128)(2,1)}, u32[]{:S(2)}, u32[]{:S(2)}) collective-permute-start(bf16[2,256,128]{2,1,0:T(8,128)(2,1)} %get-tuple-element.35.refs_12_.refs_16_), channel_id=1, source_target_pairs={{0,8},{2,10},{4,12},{6,14},{8,16},{10,18},{12,20},{14,22},{16,24},... | collective-permute-start | bytes 393224 | tf_op jit(solution)/shard_map/ppermute | solution.py:352
  52.0 43.8 %collective-permute-start.19 = (bf16[6,256,128]{2,1,0:T(8,128)(2,1)}, bf16[6,256,128]{2,1,0:T(8,128)(2,1)}, u32[]{:S(2)}, u32[]{:S(2)}) collective-permute-start(bf16[6,256,128]{2,1,0:T(8,128)(2,1)} %collective-permute-done.18.refs_13_.refs_17_), channel_id=1, source_target_pairs={{0,24},{2,26},{4,28},{6,30},{8,0},{10,2},{12,4},{14,6},{16,8},{18,... | collective-permute-start | bytes 1179656 | tf_op jit(solution)/shard_map/ppermute | solution.py:352
  60.5 37.2 %collective-permute-start.21 = (bf16[6,256,128]{2,1,0:T(8,128)(2,1)}, bf16[6,256,128]{2,1,0:T(8,128)(2,1)}, u32[]{:S(2)}, u32[]{:S(2)}) collective-permute-start(bf16[6,256,128]{2,1,0:T(8,128)(2,1)} %collective-permute-done.20.refs_14_.refs_18_), channel_id=1, source_target_pairs={{0,24},{2,26},{4,28},{6,30},{8,0},{10,2},{12,4},{14,6},{16,8},{18,... | collective-permute-start | bytes 1179656 | tf_op jit(solution)/shard_map/ppermute | solution.py:352
  68.9 37.0 %collective-permute-start.23 = (bf16[6,256,128]{2,1,0:T(8,128)(2,1)}, bf16[6,256,128]{2,1,0:T(8,128)(2,1)}, u32[]{:S(2)}, u32[]{:S(2)}) collective-permute-start(bf16[6,256,128]{2,1,0:T(8,128)(2,1)} %collective-permute-done.22.refs_15_.refs_19_), channel_id=1, source_target_pairs={{0,24},{2,26},{4,28},{6,30},{8,0},{10,2},{12,4},{14,6},{16,8},{18,... | collective-permute-start | bytes 1179656 | tf_op jit(solution)/shard_map/ppermute | solution.py:352
  94.3 25.4 %collective-permute-start.3 = (bf16[2,256,128]{2,1,0:T(8,128)(2,1)}, bf16[2,256,128]{2,1,0:T(8,128)(2,1)}, u32[]{:S(2)}, u32[]{:S(2)}) collective-permute-start(bf16[2,256,128]{2,1,0:T(8,128)(2,1)} %get-tuple-element.35.refs_12_.refs_16_), channel_id=1, source_target_pairs={{0,24},{2,26},{4,28},{6,30},{8,0},{10,2},{12,4},{14,6},{16,8},{18,... | collective-permute-start | bytes 393224 | tf_op jit(solution)/shard_map/ppermute | solution.py:352
  94.4 28.3 %collective-permute-start.11 = (bf16[2,256,128]{2,1,0:T(8,128)(2,1)}, bf16[2,256,128]{2,1,0:T(8,128)(2,1)}, u32[]{:S(2)}, u32[]{:S(2)}) collective-permute-start(bf16[2,256,128]{2,1,0:T(8,128)(2,1)} %collective-permute-done.4.refs_13_.refs_17_), channel_id=1, source_target_pairs={{0,8},{2,10},{4,12},{6,14},{8,16},{10,18},{12,20},{14,22},{16,24},... | collective-permute-start | bytes 393224 | tf_op jit(solution)/shard_map/ppermute | solution.py:352
  95.8 38.3 %collective-permute-start.5 = (bf16[2,256,128]{2,1,0:T(8,128)(2,1)}, bf16[2,256,128]{2,1,0:T(8,128)(2,1)}, u32[]{:S(2)}, u32[]{:S(2)}) collective-permute-start(bf16[2,256,128]{2,1,0:T(8,128)(2,1)} %collective-permute-done.4.refs_13_.refs_17_), channel_id=1, source_target_pairs={{0,24},{2,26},{4,28},{6,30},{8,0},{10,2},{12,4},{14,6},{16,8},{18,... | collective-permute-start | bytes 393224 | tf_op jit(solution)/shard_map/ppermute | solution.py:352
  97.7 25.3 %collective-permute-start.12 = (bf16[2,256,128]{2,1,0:T(8,128)(2,1)}, bf16[2,256,128]{2,1,0:T(8,128)(2,1)}, u32[]{:S(2)}, u32[]{:S(2)}) collective-permute-start(bf16[2,256,128]{2,1,0:T(8,128)(2,1)} %collective-permute-done.6.refs_14_.refs_18_), channel_id=1, source_target_pairs={{0,8},{2,10},{4,12},{6,14},{8,16},{10,18},{12,20},{14,22},{16,24},... | collective-permute-start | bytes 393224 | tf_op jit(solution)/shard_map/ppermute | solution.py:352
  105.9 27.0 %collective-permute-start.13 = (bf16[2,256,128]{2,1,0:T(8,128)(2,1)}, bf16[2,256,128]{2,1,0:T(8,128)(2,1)}, u32[]{:S(2)}, u32[]{:S(2)}) collective-permute-start(bf16[2,256,128]{2,1,0:T(8,128)(2,1)} %collective-permute-done.8.refs_15_.refs_19_), channel_id=1, source_target_pairs={{0,8},{2,10},{4,12},{6,14},{8,16},{10,18},{12,20},{14,22},{16,24},... | collective-permute-start | bytes 393224 | tf_op jit(solution)/shard_map/ppermute | solution.py:352
  119.7 24.8 %collective-permute-start.7 = (bf16[2,256,128]{2,1,0:T(8,128)(2,1)}, bf16[2,256,128]{2,1,0:T(8,128)(2,1)}, u32[]{:S(2)}, u32[]{:S(2)}) collective-permute-start(bf16[2,256,128]{2,1,0:T(8,128)(2,1)} %collective-permute-done.6.refs_14_.refs_18_), channel_id=1, source_target_pairs={{0,24},{2,26},{4,28},{6,30},{8,0},{10,2},{12,4},{14,6},{16,8},{18,... | collective-permute-start | bytes 393224 | tf_op jit(solution)/shard_map/ppermute | solution.py:352
  122.7 21.8 %collective-permute-start.9 = (bf16[2,256,128]{2,1,0:T(8,128)(2,1)}, bf16[2,256,128]{2,1,0:T(8,128)(2,1)}, u32[]{:S(2)}, u32[]{:S(2)}) collective-permute-start(bf16[2,256,128]{2,1,0:T(8,128)(2,1)} %collective-permute-done.8.refs_15_.refs_19_), channel_id=1, source_target_pairs={{0,24},{2,26},{4,28},{6,30},{8,0},{10,2},{12,4},{14,6},{16,8},{18,... | collective-permute-start | bytes 393224 | tf_op jit(solution)/shard_map/ppermute | solution.py:352
  122.9 29.3 %collective-permute-start.28 = (bf16[3,256,128]{2,1,0:T(8,128)(2,1)}, bf16[3,256,128]{2,1,0:T(8,128)(2,1)}, u32[]{:S(2)}, u32[]{:S(2)}) collective-permute-start(bf16[3,256,128]{2,1,0:T(8,128)(2,1)} %get-tuple-element.54), channel_id=1, source_target_pairs={{0,2},{2,0},{4,6},{6,4},{8,10},{10,8},{12,14},{14,12},{16,18},{18,... | collective-permute-start | bytes 589832 | tf_op jit(solution)/shard_map/ppermute | solution.py:347
  132.8 20.2 %collective-permute-start.29 = (bf16[3,256,128]{2,1,0:T(8,128)(2,1)}, bf16[3,256,128]{2,1,0:T(8,128)(2,1)}, u32[]{:S(2)}, u32[]{:S(2)}) collective-permute-start(bf16[3,256,128]{2,1,0:T(8,128)(2,1)} %get-tuple-element.55), channel_id=1, source_target_pairs={{0,4},{2,6},{4,0},{6,2},{8,12},{10,14},{12,8},{14,10},{16,20},{18,... | collective-permute-start | bytes 589832 | tf_op jit(solution)/shard_map/ppermute | solution.py:347
  134.1 19.0 %collective-permute-start.30 = (bf16[3,256,128]{2,1,0:T(8,128)(2,1)}, bf16[3,256,128]{2,1,0:T(8,128)(2,1)}, u32[]{:S(2)}, u32[]{:S(2)}) collective-permute-start(bf16[3,256,128]{2,1,0:T(8,128)(2,1)} %get-tuple-element.56), channel_id=1, source_target_pairs={{0,6},{2,4},{4,2},{6,0},{8,14},{10,12},{12,10},{14,8},{16,22},{18,... | collective-permute-start | bytes 589832 | tf_op jit(solution)/shard_map/ppermute | solution.py:347
  150.9 4.2 %collective-permute-start.14 = (bf16[1,256,128]{2,1,0:T(8,128)(2,1)}, bf16[1,256,128]{2,1,0:T(8,128)(2,1)}, u32[]{:S(2)}, u32[]{:S(2)}) collective-permute-start(bf16[1,256,128]{2,1,0:T(8,128)(2,1)} %get-tuple-element.44), channel_id=1, source_target_pairs={{0,2},{2,0},{4,6},{6,4},{8,10},{10,8},{12,14},{14,12},{16,18},{18,... | collective-permute-start | bytes 196616 | tf_op jit(solution)/shard_map/ppermute | solution.py:347
  151.1 4.0 %collective-permute-start.15 = (bf16[1,256,128]{2,1,0:T(8,128)(2,1)}, bf16[1,256,128]{2,1,0:T(8,128)(2,1)}, u32[]{:S(2)}, u32[]{:S(2)}) collective-permute-start(bf16[1,256,128]{2,1,0:T(8,128)(2,1)} %get-tuple-element.45), channel_id=1, source_target_pairs={{0,4},{2,6},{4,0},{6,2},{8,12},{10,14},{12,8},{14,10},{16,20},{18,... | collective-permute-start | bytes 196616 | tf_op jit(solution)/shard_map/ppermute | solution.py:347
  152.3 4.9 %collective-permute-start.16 = (bf16[1,256,128]{2,1,0:T(8,128)(2,1)}, bf16[1,256,128]{2,1,0:T(8,128)(2,1)}, u32[]{:S(2)}, u32[]{:S(2)}) collective-permute-start(bf16[1,256,128]{2,1,0:T(8,128)(2,1)} %get-tuple-element.46), channel_id=1, source_target_pairs={{0,6},{2,4},{4,2},{6,0},{8,14},{10,12},{12,10},{14,8},{16,22},{18,... | collective-permute-start | bytes 196616 | tf_op jit(solution)/shard_map/ppermute | solution.py:347

commit v4 on v3

--- a/solution.py
+++ b/solution.py
@@ -19,9 +19,9 @@
     for t in range(-win, win + 1):
         tile = tile_ref[buckets[abs(t)]].astype(jnp.float32)
         if t < win:
-            near_ref[t + win] = tile.T if t < 0 else tile
+            near_ref[t + win] = tile if t < 0 else tile.T
         if t > 0:
-            far_ref[t - 1] = tile
+            far_ref[t - 1] = tile.T
 
 
 def bias_window(bias_tiles, buckets):
@@ -156,68 +156,90 @@
     )(place, *flat, *extra)
 
 
-def scores(query, tiles, slope, store):
+LOG2E = 1.4426950408889634
+
+
+SUB = 8
+
+
+def attend(query, keys, bias, store):
+    rows = query.shape[0]
     best = None
-    for at, (keys, _, bias) in enumerate(tiles):
+    for t, tile_bias in enumerate(bias):
         tile = lax.dot_general(
-            query, keys[...], (((1,), (1,)), ((), ())), preferred_element_type=jnp.float32
+            keys[pl.ds(t * rows, rows), :], query, (((1,), (1,)), ((), ())),
+            preferred_element_type=jnp.float32,
         )
-        tile = tile + slope * bias[...]
-        store[at] = tile
-        for lane in range(0, tile.shape[1], LANES):
-            part = tile[:, lane:lane + LANES]
-            best = part if best is None else jnp.maximum(best, part)
-    return jnp.broadcast_to(jnp.max(best, axis=1, keepdims=True), best.shape)
-
-
-def weigh(tiles, peak, store, dtype):
+        tile = tile * LOG2E + tile_bias[...]
+        store[pl.ds(t * rows, rows), :] = tile
+        part = jnp.max(tile.reshape(rows // SUB, SUB, rows), axis=0)
+        best = part if best is None else jnp.maximum(best, part)
+    return jnp.broadcast_to(jnp.max(best, axis=0, keepdims=True), best.shape)
+
+
+def weigh(values, peak, count, store):
+    rows = store.shape[1]
     acc = None
-    for at, (_, values, _) in enumerate(tiles):
-        raised = jnp.concatenate(
-            [
-                jnp.exp(store[at, :, lane:lane + LANES] - peak).astype(dtype)
-                for lane in range(0, store.shape[2], LANES)
-            ],
-            axis=1,
+    for t in range(count):
+        tile = store[pl.ds(t * rows, rows), :].reshape(rows // SUB, SUB, rows)
+        raised = jnp.exp2(tile - peak[None]).reshape(rows, rows).astype(values.dtype)
+        part = jnp.dot(
+            values[:, pl.ds(t * rows, rows)], raised, preferred_element_type=jnp.float32
         )
-        part = jnp.dot(raised, values[...], preferred_element_type=jnp.float32)
         acc = part if acc is None else acc + part
     return acc
 
 
 def lanes_of(head_width, head):
     return lax.broadcasted_iota(jnp.int32, (1, LANES), 1) // head_width == head
+
+
+def turned(values, head, head_width):
+    flat = values.astype(jnp.float32).T
+    return flat[head * head_width:(head + 1) * head_width].astype(values.dtype)
 
 
 def near_kernel(win, plane, chunk0, head_width, place_ref, slopes, *refs):
     qs = refs[:plane]
     uks, uvs = refs[plane:2 * plane], refs[2 * plane:3 * plane]
     oks, ovs = refs[3 * plane:4 * plane], refs[4 * plane:5 * plane]
-    bias, acc_ref, peak_ref, store, keys, ones, query = refs[5 * plane:]
+    bias, out_ref, store, keys, flat, query, scaled = refs[5 * plane:]
     place = place_ref[0]
     heads = LANES // head_width
-    chunk, head = pl.program_id(0) + chunk0, pl.program_id(1)
+    chunk = pl.program_id(0) + chunk0
     dtype = keys.dtype
-    slope = slopes[(chunk * plane + place) * heads + head]
-    mine = lanes_of(head_width, head)
+    rows = query.shape[2]
     scale = jnp.asarray(head_width ** -0.5, dtype)
     for k in range(plane):
         at = place ^ k
-        query[at] = jnp.where(mine, qs[k][0] * scale, jnp.zeros((), dtype))
-        ones[at] = jnp.where(mine, uvs[k][0], jnp.ones((), dtype))
-        ones[plane + at] = jnp.where(mine, ovs[k][0], jnp.ones((), dtype))
-        keys[at] = uks[k][0]
-        keys[plane + at] = oks[k][0]
-    for i in range(plane):
-        tiles = []
-        for b in range(2 * plane):
-            offset = b - plane - i
-            if offset >= -win:
-                tiles.append((keys.at[b], ones.at[b], bias.at[offset + win]))
-        slot = store.at[i % 2]
-        peak = scores(query[i], tiles, slope, slot)
-        peak_ref[0, 0, i] = peak
-        acc_ref[0, 0, i] = weigh(tiles, peak, slot, dtype)
+        for base, ks, vs in ((0, uks, uvs), (plane, oks, ovs)):
+            span = pl.ds(pl.multiple_of((base + at) * rows, rows), rows)
+            keys[span, :] = ks[k][0]
+            for head in range(heads):
+                flat[head, :head_width, span] = turned(vs[k][0], head, head_width)
+        for head in range(heads):
+            query[head, at] = jnp.where(
+                lanes_of(head_width, head), qs[k][0] * scale, jnp.zeros((), dtype)
+            )
+    for head in range(heads):
+        flat[head, head_width:, :] = jnp.ones((2 * SUB, flat.shape[2]), dtype)
+
+    def one(head, _):
+        slope = slopes[(chunk * plane + place) * heads + head] * LOG2E
+        for t in range(2 * win):
+            scaled[t] = bias[t] * slope
+        for i in range(plane):
+            first = max(0, i + plane - win)
+            count = 2 * plane - first
+            tiles = [scaled.at[b - plane - i + win] for b in range(first, 2 * plane)]
+            span = pl.ds(first * rows, count * rows)
+            peak = attend(query[head, i], keys.at[span], tiles, store.at[i % 2])
+            acc = weigh(flat.at[head, :, span], peak, count, store.at[i % 2])
+            out_ref[0, head, i, :head_width + SUB] = acc[:head_width + SUB]
+            out_ref[0, head, i, head_width + SUB:] = peak
+        return 0
+
+    lax.fori_loop(0, heads, one, 0)
 
 
 def near(place, slopes, qs, ups, owns, bias, chunk0, chunks, head_width):
@@ -227,24 +249,25 @@
     heads = LANES // head_width
     block = (1, rows, LANES)
     pairs = chunks * heads * rows * rows * (plane * plane + plane * (plane + 1) // 2)
-    key_spec = pl.BlockSpec(block, lambda c, h: (c, 0, 0))
-    value_spec = pl.BlockSpec(block, lambda c, h: (chunks + c, 0, 0))
-    query_spec = pl.BlockSpec(block, lambda c, h: (chunk0 + c, 0, 0))
-    out = (chunks, heads, plane, rows, LANES)
-    out_spec = pl.BlockSpec((1, 1) + out[2:], lambda c, h: (c, h, 0, 0, 0))
+    key_spec = pl.BlockSpec(block, lambda c: (c, 0, 0))
+    value_spec = pl.BlockSpec(block, lambda c: (chunks + c, 0, 0))
+    query_spec = pl.BlockSpec(block, lambda c: (chunk0 + c, 0, 0))
+    out = (chunks, heads, plane, head_width + 2 * SUB, rows)
+    dtype = qs[0].dtype
     return pl.pallas_call(
         functools.partial(near_kernel, win, plane, chunk0, head_width),
-        grid=(chunks, heads),
+        grid=(chunks,),
         in_specs=[SMEM, SMEM] + [query_spec] * plane + [key_spec] * plane + [value_spec] * plane
         + [key_spec] * plane + [value_spec] * plane
-        + [pl.BlockSpec(bias.shape, lambda c, h: (0, 0, 0), pipeline_mode=pl.Buffered(1))],
-        out_specs=[out_spec, out_spec],
-        out_shape=[jax.ShapeDtypeStruct(out, jnp.float32)] * 2,
+        + [pl.BlockSpec(bias.shape, lambda c: (0, 0, 0), pipeline_mode=pl.Buffered(1))],
+        out_specs=pl.BlockSpec((1,) + out[1:], lambda c: (c, 0, 0, 0, 0)),
+        out_shape=jax.ShapeDtypeStruct(out, jnp.float32),
         scratch_shapes=[
-            pltpu.VMEM((2, 2 * win, rows, rows), jnp.float32),
-            pltpu.VMEM((2 * plane, rows, LANES), qs[0].dtype),
-            pltpu.VMEM((2 * plane, rows, LANES), qs[0].dtype),
-            pltpu.VMEM((plane, rows, LANES), qs[0].dtype),
+            pltpu.VMEM((2, 2 * win * rows, rows), jnp.float32),
+            pltpu.VMEM((2 * plane * rows, LANES), dtype),
+            pltpu.VMEM((heads, head_width + 2 * SUB, 2 * plane * rows), dtype),
+            pltpu.VMEM((heads, plane, rows, LANES), dtype),
+            pltpu.VMEM((2 * win, rows, rows), jnp.float32),
         ],
         cost_estimate=pl.CostEstimate(
             flops=4 * pairs * LANES, bytes_accessed=chunks * (4 << 20), transcendentals=pairs
@@ -256,42 +279,45 @@
 
 def far_kernel(win, plane, chunk0, head_width, place_ref, slopes, *refs):
     qs, dks, dvs = (refs[n * plane:(n + 1) * plane] for n in range(3))
-    bias, acc_ref, peak_ref = refs[3 * plane:3 * plane + 3]
-    outs = refs[3 * plane + 3:4 * plane + 3]
-    store, keys, ones, query, held = refs[4 * plane + 3:]
+    bias, near_ref = refs[3 * plane:3 * plane + 2]
+    outs = refs[3 * plane + 2:4 * plane + 2]
+    store, keys, flat, query, held, scaled = refs[4 * plane + 2:]
     place = place_ref[0]
     heads = LANES // head_width
     chunk = pl.program_id(0) + chunk0
     dtype = keys.dtype
+    rows = query.shape[2]
     scale = jnp.asarray(head_width ** -0.5, dtype)
     for k in range(plane):
         at = place ^ k
-        keys[at] = dks[k][0]
+        span = pl.ds(pl.multiple_of(at * rows, rows), rows)
+        keys[span, :] = dks[k][0]
         for head in range(heads):
-            mine = lanes_of(head_width, head)
-            query[head, at] = jnp.where(mine, qs[k][0] * scale, jnp.zeros((), dtype))
-            ones[head, at] = jnp.where(mine, dvs[k][0], jnp.ones((), dtype))
+            flat[head, :head_width, span] = turned(dvs[k][0], head, head_width)
+            query[head, at] = jnp.where(
+                lanes_of(head_width, head), qs[k][0] * scale, jnp.zeros((), dtype)
+            )
+    for head in range(heads):
+        flat[head, head_width:, :] = jnp.ones((2 * SUB, flat.shape[2]), dtype)
+        slope = slopes[(chunk * plane + place) * heads + head] * LOG2E
+        for t in range(win):
+            scaled[head, t] = bias[t] * slope
     for i in range(plane):
-        upper = lower = None
+        count = min(plane, win - plane + i + 1)
+        span = pl.ds(0, count * rows)
+        both = []
         for head in range(heads):
-            slope = slopes[(chunk * plane + place) * heads + head]
-            tiles = [
-                (keys.at[b], ones.at[head, b], bias.at[b + plane - i - 1])
-                for b in range(plane) if b + plane - i <= win
-            ]
-            slot = store.at[(i * heads + head) % store.shape[0]]
-            before = peak_ref[0, head, i]
-            peak = jnp.maximum(scores(query[head, i], tiles, slope, slot), before)
-            acc = weigh(tiles, peak, slot, dtype) + acc_ref[0, head, i] * jnp.exp(before - peak)
-            if upper is None:
-                upper, lower = acc, acc
-            else:
-                mine = lanes_of(head_width, head)
-                beside = lanes_of(head_width, head - 1)
-                upper = jnp.where(mine, acc, upper)
-                lower = jnp.where(beside, acc, lower)
-        lower = pltpu.roll(lower, head_width, 1)
-        held[i ^ place] = (upper / lower).astype(dtype)
+            tiles = [scaled.at[head, b + plane - i - 1] for b in range(count)]
+            slot = store.at[(i * heads + head) % 2]
+            before = near_ref[0, head, i, head_width + SUB:]
+            peak = jnp.maximum(attend(query[head, i], keys.at[span], tiles, slot), before)
+            acc = weigh(flat.at[head, :, span], peak, count, slot)[:head_width + SUB]
+            acc = acc.reshape(-1, SUB, rows)
+            old = near_ref[0, head, i, :head_width + SUB].reshape(-1, SUB, rows)
+            acc = acc + old * jnp.exp2(before - peak)[None]
+            share = 1.0 / acc[head_width // SUB:]
+            both.append((acc[:head_width // SUB] * share).reshape(head_width, rows))
+        held[i ^ place] = jnp.concatenate(both, axis=0).T.astype(dtype)
     for k in range(plane):
         outs[k][0] = held[k]
 
@@ -303,34 +329,33 @@
     heads = LANES // head_width
     block = (1, rows, LANES)
     pairs = chunks * heads * rows * rows * (plane * (plane + 1) // 2)
-    acc, peak = before
     key_spec = pl.BlockSpec(block, lambda c: (c, 0, 0))
     value_spec = pl.BlockSpec(block, lambda c: (chunks + c, 0, 0))
     query_spec = pl.BlockSpec(block, lambda c: (chunk0 + c, 0, 0))
-    near_spec = pl.BlockSpec(
-        (1, heads, plane, rows, LANES), lambda c: (c, 0, 0, 0, 0)
-    )
+    near_spec = pl.BlockSpec((1,) + before.shape[1:], lambda c: (c, 0, 0, 0, 0))
+    dtype = qs[0].dtype
     return pl.pallas_call(
         functools.partial(far_kernel, win, plane, chunk0, head_width),
         grid=(chunks,),
         in_specs=[SMEM, SMEM] + [query_spec] * plane + [key_spec] * plane + [value_spec] * plane
         + [pl.BlockSpec(bias.shape, lambda c: (0, 0, 0), pipeline_mode=pl.Buffered(1))]
-        + [near_spec, near_spec],
+        + [near_spec],
         out_specs=[key_spec] * plane,
-        out_shape=[jax.ShapeDtypeStruct((chunks, rows, LANES), qs[0].dtype)] * plane,
+        out_shape=[jax.ShapeDtypeStruct((chunks, rows, LANES), dtype)] * plane,
         scratch_shapes=[
-            pltpu.VMEM((2 * heads, win, rows, rows), jnp.float32),
-            pltpu.VMEM((plane, rows, LANES), qs[0].dtype),
-            pltpu.VMEM((heads, plane, rows, LANES), qs[0].dtype),
-            pltpu.VMEM((heads, plane, rows, LANES), qs[0].dtype),
-            pltpu.VMEM((plane, rows, LANES), qs[0].dtype),
+            pltpu.VMEM((2, plane * rows, rows), jnp.float32),
+            pltpu.VMEM((plane * rows, LANES), dtype),
+            pltpu.VMEM((heads, head_width + 2 * SUB, plane * rows), dtype),
+            pltpu.VMEM((heads, plane, rows, LANES), dtype),
+            pltpu.VMEM((plane, rows, LANES), dtype),
+            pltpu.VMEM((heads, win, rows, rows), jnp.float32),
         ],
         cost_estimate=pl.CostEstimate(
             flops=4 * pairs * LANES, bytes_accessed=chunks * (4 << 20), transcendentals=pairs
         ),
         compiler_params=PARAMS,
         name="far",
-    )(place, slopes, *qs, *downs, *downs, bias, acc, peak)
+    )(place, slopes, *qs, *downs, *downs, bias, before)
 
 
 def per_device(queries, key_rows, values, bias_tiles, buckets, slopes):
@@ -352,15 +377,14 @@
         return [lax.ppermute(x, "seq", pairs) for x in arrays]
 
     place = (lax.axis_index("seq") % plane).astype(jnp.int32).reshape(1)
-    data = dict(q=queries, k=key_rows, v=values)
 
     def kv(start, size):
         span = range(start, start + size)
         return [("k", c) for c in span] + [("v", c) for c in span]
 
     groups = [(0, chunks - 1), (chunks - 1, 1)]
-    (first,) = pack(dict(k=key_rows, v=values), [kv(*groups[0])], plane, place)
-    second, query = pack(data, [kv(*groups[1]), [("q", c) for c in range(chunks)]], plane, place)
+    first, second = pack(dict(k=key_rows, v=values), [kv(*g) for g in groups], plane, place)
+    (query,) = pack(dict(q=queries), [[("q", c) for c in range(chunks)]], plane, place)
     owns = [send(x) for x in (first, second)]
     qs = send(query)
     near_bias, far_bias = bias_window(bias_tiles, buckets)

time: 160 us -> 156 us (0.975)
  Pallas kernels: 65.3 us -> 61 us
  starting transfers between devices: 39.5 us -> 43.1 us
  waiting for transfers between devices: 53.9 us -> 51.7 us
    ppermute x15, waiting for transfers between devices: 31.4 us -> 27 us  [send(): out.append(lax.ppermute(x, 'seq', pairs))]
    ppermute x15, starting transfers between devices: 20 us -> 23.4 us  [send(): out.append(lax.ppermute(x, 'seq', pairs))]
    pallas_call x2, Pallas kernels: 33.8 us -> 31.2 us  [near(): pl.pallas_call(functools.partial(near_kernel, win, plane, chunk0, head_wi...]
    ppermute x16, waiting for transfers between devices: 22.6 us -> 24.7 us  [shift(): return [lax.ppermute(x, 'seq', pairs) for x in arrays]]
  transfers between devices with their start and end apart: 31 -> 31, of which waited for: 8 -> 9; matrix products, arithmetic and copies ran while one was open for 0% -> 0% of each run, Pallas kernels for 38% -> 36%
where the time goes in v4:
time: 156 us
  Pallas kernels  61 us (39%)
  waiting for transfers between devices  51.7 us (33%)
  starting transfers between devices  43.1 us (28%)
    pallas_call x2, Pallas kernels, near(): pl.pallas_call(functools.partial(near_kernel, win, plane, chunk0, head_wi...  31.2 us
    ppermute x15, waiting for transfers between devices, send(): out.append(lax.ppermute(x, 'seq', pairs))  27 us
    ppermute x16, waiting for transfers between devices, shift(): return [lax.ppermute(x, 'seq', pairs) for x in arrays]  24.7 us
    ppermute x15, starting transfers between devices, send(): out.append(lax.ppermute(x, 'seq', pairs))  23.4 us
    ppermute x16, starting transfers between devices, shift(): return [lax.ppermute(x, 'seq', pairs) for x in arrays]  19.7 us
    pallas_call x2, Pallas kernels, far(): pl.pallas_call(functools.partial(far_kernel, win, plane, chunk0, head_wid...  18.4 us
    pallas_call x2, Pallas kernels, pack(): pl.pallas_call(functools.partial(pack_kernel, plane, groups, names), in_s...  4.76 us
    pallas_call x2, Pallas kernels, unpack(): pl.pallas_call(functools.partial(unpack_kernel, plane, chunk0, chunks, le...  3.66 us
  transfers between devices with their start and end apart: 31, of which 9 were waited for; matrix products, arithmetic and copies ran while one was open for 0% of the time, Pallas kernels for 36%

profile of v4, /device:TPU:1, one launch (start us, length us, event | category | flops | bytes accessed | tf_op | source)
XLA Modules:
  0.0 156.1 jit_solution(10845677202500411500)
XLA Ops:
  0.0 2.6 %shard_map.65 = (bf16[6,256,128]{2,1,0:T(8,128)(2,1)}, bf16[6,256,128]{2,1,0:T(8,128)(2,1)}, bf16[6,256,128]{2,1,0:T(8,128)(2,1)}, bf16[6,256,128]{2,1,0:T(8,128...) custom-call(s32[1]{0:T(128)} %bitcast.place_ref, ...), custom_call_target="tpu_custom_call" | custom-call | bytes 4194304 | tf_op jit(solution)/shard_map/pallas_call | solution.py:84
  2.7 0.1 collective-permute-start.4
  2.7 2.7 %collective-permute-start.6 = (bf16[2,256,128]{2,1,0:T(8,128)(2,1)}, bf16[2,256,128]{2,1,0:T(8,128)(2,1)}, u32[]{:S(2)}, u32[]{:S(2)}) collective-permute-start(bf16[2,256,128]{2,1,0:T(8,128)(2,1)} %get-tuple-element.33), channel_id=1, source_target_pairs={{0,4},{2,6},{4,0},{6,2},{8,12},{10,14},{12,8},{14,10},{16,20},{18,... | collective-permute-start | bytes 393224 | tf_op jit(solution)/shard_map/ppermute | solution.py:372
  5.4 0.4 collective-permute-start.18
  5.8 0.0 collective-permute-start.20
  5.8 1.8 %collective-permute-start.22 = (bf16[6,256,128]{2,1,0:T(8,128)(2,1)}, bf16[6,256,128]{2,1,0:T(8,128)(2,1)}, u32[]{:S(2)}, u32[]{:S(2)}) collective-permute-start(bf16[6,256,128]{2,1,0:T(8,128)(2,1)} %get-tuple-element.44), channel_id=1, source_target_pairs={{0,6},{2,4},{4,2},{6,0},{8,14},{10,12},{12,10},{14,8},{16,22},{18,... | collective-permute-start | bytes 1179656 | tf_op jit(solution)/shard_map/ppermute | solution.py:372
  7.6 0.0 collective-permute-start.8
  7.6 2.1 %shard_map.64 = (bf16[4,256,128]{2,1,0:T(8,128)(2,1)}, bf16[4,256,128]{2,1,0:T(8,128)(2,1)}, bf16[4,256,128]{2,1,0:T(8,128)(2,1)}, bf16[4,256,128]{2,1,0:T(8,128)(2,1)}) custom-call(s32[1]{0:T(128)} %bitcast.place_ref, bf16[256,2048]{1,0:T(8,128)(2,1)} %refs_0_.2), custom_call_target="tpu_custom_call" | custom-call | bytes 2097152 | tf_op jit(solution)/shard_map/pallas_call | solution.py:84
  9.7 0.7 collective-permute-start
  10.5 18.7 %collective-permute-done.8.refs_15_.refs_19_ = bf16[2,256,128]{2,1,0:T(8,128)(2,1)} collective-permute-done((bf16[2,256,128]{2,1,0:T(8,128)(2,1)}, bf16[2,256,128]{2,1,0:T(8,128)(2,1)}, u32[]{:S(2)}, u32[]{:S(2)}) %collective-permute-start.8) | collective-permute-done | bytes 131104 | tf_op jit(solution)/shard_map/ppermute | solution.py:372
  29.2 1.4 collective-permute-start.1
  30.6 1.3 collective-permute-start.24
  31.9 1.3 collective-permute-start.25
  33.2 1.3 collective-permute-start.26
  34.5 0.1 collective-permute-start.27
  34.6 2.4 %collective-permute-done.1.refs_2_ = bf16[4,256,128]{2,1,0:T(8,128)(2,1)} collective-permute-done((bf16[4,256,128]{2,1,0:T(8,128)(2,1)}, bf16[4,256,128]{2,1,0:T(8,128)(2,1)}, u32[]{:S(2)}, u32[]{:S(2)}) %collective-permute-start.1) | collective-permute-done | bytes 262176 | tf_op jit(solution)/shard_map/ppermute | solution.py:372
  37.0 2.6 %collective-permute-start.2 = (bf16[4,256,128]{2,1,0:T(8,128)(2,1)}, bf16[4,256,128]{2,1,0:T(8,128)(2,1)}, u32[]{:S(2)}, u32[]{:S(2)}) collective-permute-start(bf16[4,256,128]{2,1,0:T(8,128)(2,1)} %get-tuple-element.30), channel_id=1, source_target_pairs={{0,6},{2,4},{4,2},{6,0},{8,14},{10,12},{12,10},{14,8},{16,22},{18,... | collective-permute-start | bytes 786440 | tf_op jit(solution)/shard_map/ppermute | solution.py:372
  39.5 3.0 %bias_window.1 = (f32[8,256,256]{2,1,0:T(8,128)}, f32[4,256,256]{2,1,0:T(8,128)}) custom-call(s32[5]{0:T(128)} %buckets.1, bf16[3,256,256]{2,1,0:T(8,128)(2,1)} %tile_ref.1), custom_call_target="tpu_custom_call" | custom-call | tf_op jit(solution)/shard_map/bias_window/pallas_call | solution.py:31
  42.5 4.2 %collective-permute-done.2.refs_3_ = bf16[4,256,128]{2,1,0:T(8,128)(2,1)} collective-permute-done((bf16[4,256,128]{2,1,0:T(8,128)(2,1)}, bf16[4,256,128]{2,1,0:T(8,128)(2,1)}, u32[]{:S(2)}, u32[]{:S(2)}) %collective-permute-start.2) | collective-permute-done | bytes 262176 | tf_op jit(solution)/shard_map/ppermute | solution.py:372
  46.8 3.5 %collective-permute-start.17 = (bf16[6,256,128]{2,1,0:T(8,128)(2,1)}, bf16[6,256,128]{2,1,0:T(8,128)(2,1)}, u32[]{:S(2)}, u32[]{:S(2)}) collective-permute-start(bf16[6,256,128]{2,1,0:T(8,128)(2,1)} %get-tuple-element.41.refs_12_.refs_16_), channel_id=1, source_target_pairs={{0,24},{2,26},{4,28},{6,30},{8,0},{10,2},{12,4},{14,6},{16,8},{18,... | collective-permute-start | bytes 1179656 | tf_op jit(solution)/shard_map/ppermute | solution.py:377
  50.3 1.2 collective-permute-done.25.refs_5_.refs_9_
  51.5 2.0 %collective-permute-start.19 = (bf16[6,256,128]{2,1,0:T(8,128)(2,1)}, bf16[6,256,128]{2,1,0:T(8,128)(2,1)}, u32[]{:S(2)}, u32[]{:S(2)}) collective-permute-start(bf16[6,256,128]{2,1,0:T(8,128)(2,1)} %collective-permute-done.18.refs_13_.refs_17_), channel_id=1, source_target_pairs={{0,24},{2,26},{4,28},{6,30},{8,0},{10,2},{12,4},{14,6},{16,8},{18,... | collective-permute-start | bytes 1179656 | tf_op jit(solution)/shard_map/ppermute | solution.py:377
  53.6 6.4 %collective-permute-done.26.refs_6_.refs_10_ = bf16[6,256,128]{2,1,0:T(8,128)(2,1)} collective-permute-done((bf16[6,256,128]{2,1,0:T(8,128)(2,1)}, bf16[6,256,128]{2,1,0:T(8,128)(2,1)}, u32[]{:S(2)}, u32[]{:S(2)}) %collective-permute-start.26) | collective-permute-done | bytes 393248 | tf_op jit(solution)/shard_map/ppermute | solution.py:377
  60.0 1.4 collective-permute-start.21
  61.4 7.1 %collective-permute-done.27.refs_7_.refs_11_ = bf16[6,256,128]{2,1,0:T(8,128)(2,1)} collective-permute-done((bf16[6,256,128]{2,1,0:T(8,128)(2,1)}, bf16[6,256,128]{2,1,0:T(8,128)(2,1)}, u32[]{:S(2)}, u32[]{:S(2)}) %collective-permute-start.27) | collective-permute-done | bytes 393248 | tf_op jit(solution)/shard_map/ppermute | solution.py:377
  68.4 1.6 %collective-permute-start.23 = (bf16[6,256,128]{2,1,0:T(8,128)(2,1)}, bf16[6,256,128]{2,1,0:T(8,128)(2,1)}, u32[]{:S(2)}, u32[]{:S(2)}) collective-permute-start(bf16[6,256,128]{2,1,0:T(8,128)(2,1)} %collective-permute-done.22.refs_15_.refs_19_), channel_id=1, source_target_pairs={{0,24},{2,26},{4,28},{6,30},{8,0},{10,2},{12,4},{14,6},{16,8},{18,... | collective-permute-start | bytes 1179656 | tf_op jit(solution)/shard_map/ppermute | solution.py:377
  70.0 22.0 %near.3.refs_13_ = f32[3,2,4,80,256]{4,3,2,1,0:T(8,128)} custom-call(s32[1]{0:T(128)} %bitcast.place_ref, f32[32]{0:T(128)} %slopes.7, bf16[4,256,128]{2,1,0:T(8,128)(2,1)} %get-tuple-element.27.refs_0_, bf16[4,256,128]{2,1,0:T(8,128)(2,1)} %collective-permute-done.refs_1_, bf16[4,256,128]{2,1,0:T(8,128)(2,1)} %collective-permute-done.1.refs_2_, ...), custom_call_target="tpu_custom_call" | custom-call | flops 5234491392 | bytes 12582912 | tf_op jit(solution)/shard_map/near/pallas_call | solution.py:257
  92.1 0.1 collective-permute-start.3
  92.2 1.4 collective-permute-start.11
  93.6 1.9 %collective-permute-start.5 = (bf16[2,256,128]{2,1,0:T(8,128)(2,1)}, bf16[2,256,128]{2,1,0:T(8,128)(2,1)}, u32[]{:S(2)}, u32[]{:S(2)}) collective-permute-start(bf16[2,256,128]{2,1,0:T(8,128)(2,1)} %collective-permute-done.4.refs_13_.refs_17_), channel_id=1, source_target_pairs={{0,24},{2,26},{4,28},{6,30},{8,0},{10,2},{12,4},{14,6},{16,8},{18,... | collective-permute-start | bytes 393224 | tf_op jit(solution)/shard_map/ppermute | solution.py:377
  95.5 1.8 %collective-permute-done.21.refs_6_.refs_10_ = bf16[6,256,128]{2,1,0:T(8,128)(2,1)} collective-permute-done((bf16[6,256,128]{2,1,0:T(8,128)(2,1)}, bf16[6,256,128]{2,1,0:T(8,128)(2,1)}, u32[]{:S(2)}, u32[]{:S(2)}) %collective-permute-start.21) | collective-permute-done | bytes 393248 | tf_op jit(solution)/shard_map/ppermute | solution.py:377
  97.3 0.3 collective-permute-start.12
  97.5 8.2 %collective-permute-done.23.refs_7_.refs_11_ = bf16[6,256,128]{2,1,0:T(8,128)(2,1)} collective-permute-done((bf16[6,256,128]{2,1,0:T(8,128)(2,1)}, bf16[6,256,128]{2,1,0:T(8,128)(2,1)}, u32[]{:S(2)}, u32[]{:S(2)}) %collective-permute-start.23) | collective-permute-done | bytes 393248 | tf_op jit(solution)/shard_map/ppermute | solution.py:377
  105.7 0.3 collective-permute-start.13
  105.9 12.6 %far.3 = (bf16[3,256,128]{2,1,0:T(8,128)(2,1)}, bf16[3,256,128]{2,1,0:T(8,128)(2,1)}, bf16[3,256,128]{2,1,0:T(8,128)(2,1)}, bf16[3,256,128]{2,1,0:T(8,128)(2,1)}) custom-call(s32[1]{0:T(128)} %bitcast.place_ref, f32[32]{0:T(128)} %slopes.7, bf16[4,256,128]{2,1,0:T(8,128)(2,1)} %get-tuple-element.27.refs_0_, ...), custom_call_target="tpu_custom_call" | custom-call | flops 2013265920 | bytes 12582912 | tf_op jit(solution)/shard_map/far/pallas_call | solution.py:337
  118.6 3.1 %collective-permute-start.7 = (bf16[2,256,128]{2,1,0:T(8,128)(2,1)}, bf16[2,256,128]{2,1,0:T(8,128)(2,1)}, u32[]{:S(2)}, u32[]{:S(2)}) collective-permute-start(bf16[2,256,128]{2,1,0:T(8,128)(2,1)} %collective-permute-done.6.refs_14_.refs_18_), channel_id=1, source_target_pairs={{0,24},{2,26},{4,28},{6,30},{8,0},{10,2},{12,4},{14,6},{16,8},{18,... | collective-permute-start | bytes 393224 | tf_op jit(solution)/shard_map/ppermute | solution.py:377
  121.6 0.3 collective-permute-start.9
  121.9 9.8 %collective-permute-start.28 = (bf16[3,256,128]{2,1,0:T(8,128)(2,1)}, bf16[3,256,128]{2,1,0:T(8,128)(2,1)}, u32[]{:S(2)}, u32[]{:S(2)}) collective-permute-start(bf16[3,256,128]{2,1,0:T(8,128)(2,1)} %get-tuple-element.46), channel_id=1, source_target_pairs={{0,2},{2,0},{4,6},{6,4},{8,10},{10,8},{12,14},{14,12},{16,18},{18,... | collective-permute-start | bytes 589832 | tf_op jit(solution)/shard_map/ppermute | solution.py:372
  131.7 0.3 collective-permute-start.29
  132.0 1.4 collective-permute-start.30
  133.4 9.2 %near.2.refs_13_ = f32[1,2,4,80,256]{4,3,2,1,0:T(8,128)} custom-call(s32[1]{0:T(128)} %bitcast.place_ref, f32[32]{0:T(128)} %slopes.7, bf16[4,256,128]{2,1,0:T(8,128)(2,1)} %get-tuple-element.27.refs_0_, bf16[4,256,128]{2,1,0:T(8,128)(2,1)} %collective-permute-done.refs_1_, bf16[4,256,128]{2,1,0:T(8,128)(2,1)} %collective-permute-done.1.refs_2_, ...), custom_call_target="tpu_custom_call" | custom-call | flops 1744830464 | bytes 4194304 | tf_op jit(solution)/shard_map/near/pallas_call | solution.py:257
  142.7 5.8 %far.2 = (bf16[1,256,128]{2,1,0:T(8,128)(2,1)}, bf16[1,256,128]{2,1,0:T(8,128)(2,1)}, bf16[1,256,128]{2,1,0:T(8,128)(2,1)}, bf16[1,256,128]{2,1,0:T(8,128)(2,1)}) custom-call(s32[1]{0:T(128)} %bitcast.place_ref, f32[32]{0:T(128)} %slopes.7, bf16[4,256,128]{2,1,0:T(8,128)(2,1)} %get-tuple-element.27.refs_0_, ...), custom_call_target="tpu_custom_call" | custom-call | flops 671088640 | bytes 4194304 | tf_op jit(solution)/shard_map/far/pallas_call | solution.py:337
  148.4 0.2 collective-permute-start.14
  148.6 0.3 collective-permute-start.15
  148.9 1.7 %collective-permute-start.16 = (bf16[1,256,128]{2,1,0:T(8,128)(2,1)}, bf16[1,256,128]{2,1,0:T(8,128)(2,1)}, u32[]{:S(2)}, u32[]{:S(2)}) collective-permute-start(bf16[1,256,128]{2,1,0:T(8,128)(2,1)} %get-tuple-element.40), channel_id=1, source_target_pairs={{0,6},{2,4},{4,2},{6,0},{8,14},{10,12},{12,10},{14,8},{16,22},{18,... | collective-permute-start | bytes 196616 | tf_op jit(solution)/shard_map/ppermute | solution.py:372
  150.6 2.0 %shard_map.66.refs_4_ = bf16[256,2048]{1,0:T(8,128)(2,1)} custom-call(s32[1]{0:T(128)} %bitcast.place_ref, bf16[3,256,128]{2,1,0:T(8,128)(2,1)} %get-tuple-element.45.refs_0_, bf16[3,256,128]{2,1,0:T(8,128)(2,1)} %collective-permute-done.28.refs_1_, bf16[3,256,128]{2,1,0:T(8,128)(2,1)} %collective-permute-done.29.refs_2_, ...), custom_call_target="tpu_custom_call" | custom-call | bytes 1572864 | tf_op jit(solution)/shard_map/pallas_call | solution.py:141
  152.6 1.6 %collective-permute-done.16.refs_3_ = bf16[1,256,128]{2,1,0:T(8,128)(2,1)} collective-permute-done((bf16[1,256,128]{2,1,0:T(8,128)(2,1)}, bf16[1,256,128]{2,1,0:T(8,128)(2,1)}, u32[]{:S(2)}, u32[]{:S(2)}) %collective-permute-start.16) | collective-permute-done | bytes 65568 | tf_op jit(solution)/shard_map/ppermute | solution.py:372
  154.2 1.7 %shard_map.67 = bf16[256,2048]{1,0:T(8,128)(2,1)} custom-call(s32[1]{0:T(128)} %bitcast.place_ref, bf16[1,256,128]{2,1,0:T(8,128)(2,1)} %get-tuple-element.37.refs_0_, bf16[1,256,128]{2,1,0:T(8,128)(2,1)} %collective-permute-done.14.refs_1_, bf16[1,256,128]{2,1,0:T(8,128)(2,1)} %collective-permute-done.15.refs_2_, ...), custom_call_target="tpu_custom_call", output_to_operand_aliasing={{}: (5, {})} | custom-call | bytes 524288 | tf_op jit(solution)/shard_map/pallas_call | solution.py:141
  (23 shorter events, 0.1 us)
Async XLA Ops:
  2.7 4.9 %collective-permute-start.4 = (bf16[2,256,128]{2,1,0:T(8,128)(2,1)}, bf16[2,256,128]{2,1,0:T(8,128)(2,1)}, u32[]{:S(2)}, u32[]{:S(2)}) collective-permute-start(bf16[2,256,128]{2,1,0:T(8,128)(2,1)} %get-tuple-element.32), channel_id=1, source_target_pairs={{0,2},{2,0},{4,6},{6,4},{8,10},{10,8},{12,14},{14,12},{16,18},{18,... | collective-permute-start | bytes 393224 | tf_op jit(solution)/shard_map/ppermute | solution.py:372
  2.7 7.0 %collective-permute-start.6 = (bf16[2,256,128]{2,1,0:T(8,128)(2,1)}, bf16[2,256,128]{2,1,0:T(8,128)(2,1)}, u32[]{:S(2)}, u32[]{:S(2)}) collective-permute-start(bf16[2,256,128]{2,1,0:T(8,128)(2,1)} %get-tuple-element.33), channel_id=1, source_target_pairs={{0,4},{2,6},{4,0},{6,2},{8,12},{10,14},{12,8},{14,10},{16,20},{18,... | collective-permute-start | bytes 393224 | tf_op jit(solution)/shard_map/ppermute | solution.py:372
  5.4 26.5 %collective-permute-start.18 = (bf16[6,256,128]{2,1,0:T(8,128)(2,1)}, bf16[6,256,128]{2,1,0:T(8,128)(2,1)}, u32[]{:S(2)}, u32[]{:S(2)}) collective-permute-start(bf16[6,256,128]{2,1,0:T(8,128)(2,1)} %get-tuple-element.42), channel_id=1, source_target_pairs={{0,2},{2,0},{4,6},{6,4},{8,10},{10,8},{12,14},{14,12},{16,18},{18,... | collective-permute-start | bytes 1179656 | tf_op jit(solution)/shard_map/ppermute | solution.py:372
  5.8 27.4 %collective-permute-start.20 = (bf16[6,256,128]{2,1,0:T(8,128)(2,1)}, bf16[6,256,128]{2,1,0:T(8,128)(2,1)}, u32[]{:S(2)}, u32[]{:S(2)}) collective-permute-start(bf16[6,256,128]{2,1,0:T(8,128)(2,1)} %get-tuple-element.43), channel_id=1, source_target_pairs={{0,4},{2,6},{4,0},{6,2},{8,12},{10,14},{12,8},{14,10},{16,20},{18,... | collective-permute-start | bytes 1179656 | tf_op jit(solution)/shard_map/ppermute | solution.py:372
  5.8 28.7 %collective-permute-start.22 = (bf16[6,256,128]{2,1,0:T(8,128)(2,1)}, bf16[6,256,128]{2,1,0:T(8,128)(2,1)}, u32[]{:S(2)}, u32[]{:S(2)}) collective-permute-start(bf16[6,256,128]{2,1,0:T(8,128)(2,1)} %get-tuple-element.44), channel_id=1, source_target_pairs={{0,6},{2,4},{4,2},{6,0},{8,14},{10,12},{12,10},{14,8},{16,22},{18,... | collective-permute-start | bytes 1179656 | tf_op jit(solution)/shard_map/ppermute | solution.py:372
  7.6 21.6 %collective-permute-start.8 = (bf16[2,256,128]{2,1,0:T(8,128)(2,1)}, bf16[2,256,128]{2,1,0:T(8,128)(2,1)}, u32[]{:S(2)}, u32[]{:S(2)}) collective-permute-start(bf16[2,256,128]{2,1,0:T(8,128)(2,1)} %get-tuple-element.34), channel_id=1, source_target_pairs={{0,6},{2,4},{4,2},{6,0},{8,14},{10,12},{12,10},{14,8},{16,22},{18,... | collective-permute-start | bytes 393224 | tf_op jit(solution)/shard_map/ppermute | solution.py:372
  9.7 20.9 %collective-permute-start = (bf16[4,256,128]{2,1,0:T(8,128)(2,1)}, bf16[4,256,128]{2,1,0:T(8,128)(2,1)}, u32[]{:S(2)}, u32[]{:S(2)}) collective-permute-start(bf16[4,256,128]{2,1,0:T(8,128)(2,1)} %get-tuple-element.28), channel_id=1, source_target_pairs={{0,2},{2,0},{4,6},{6,4},{8,10},{10,8},{12,14},{14,12},{16,18},{18,... | collective-permute-start | bytes 786440 | tf_op jit(solution)/shard_map/ppermute | solution.py:372
  29.2 7.8 %collective-permute-start.1 = (bf16[4,256,128]{2,1,0:T(8,128)(2,1)}, bf16[4,256,128]{2,1,0:T(8,128)(2,1)}, u32[]{:S(2)}, u32[]{:S(2)}) collective-permute-start(bf16[4,256,128]{2,1,0:T(8,128)(2,1)} %get-tuple-element.29), channel_id=1, source_target_pairs={{0,4},{2,6},{4,0},{6,2},{8,12},{10,14},{12,8},{14,10},{16,20},{18,... | collective-permute-start | bytes 786440 | tf_op jit(solution)/shard_map/ppermute | solution.py:372
  30.6 19.7 %collective-permute-start.24 = (bf16[6,256,128]{2,1,0:T(8,128)(2,1)}, bf16[6,256,128]{2,1,0:T(8,128)(2,1)}, u32[]{:S(2)}, u32[]{:S(2)}) collective-permute-start(bf16[6,256,128]{2,1,0:T(8,128)(2,1)} %get-tuple-element.41.refs_12_.refs_16_), channel_id=1, source_target_pairs={{0,8},{2,10},{4,12},{6,14},{8,16},{10,18},{12,20},{14,22},{16,24},... | collective-permute-start | bytes 1179656 | tf_op jit(solution)/shard_map/ppermute | solution.py:377
  31.9 19.6 %collective-permute-start.25 = (bf16[6,256,128]{2,1,0:T(8,128)(2,1)}, bf16[6,256,128]{2,1,0:T(8,128)(2,1)}, u32[]{:S(2)}, u32[]{:S(2)}) collective-permute-start(bf16[6,256,128]{2,1,0:T(8,128)(2,1)} %collective-permute-done.18.refs_13_.refs_17_), channel_id=1, source_target_pairs={{0,8},{2,10},{4,12},{6,14},{8,16},{10,18},{12,20},{14,22},{16,24},... | collective-permute-start | bytes 1179656 | tf_op jit(solution)/shard_map/ppermute | solution.py:377
  33.2 26.8 %collective-permute-start.26 = (bf16[6,256,128]{2,1,0:T(8,128)(2,1)}, bf16[6,256,128]{2,1,0:T(8,128)(2,1)}, u32[]{:S(2)}, u32[]{:S(2)}) collective-permute-start(bf16[6,256,128]{2,1,0:T(8,128)(2,1)} %collective-permute-done.20.refs_14_.refs_18_), channel_id=1, source_target_pairs={{0,8},{2,10},{4,12},{6,14},{8,16},{10,18},{12,20},{14,22},{16,24},... | collective-permute-start | bytes 1179656 | tf_op jit(solution)/shard_map/ppermute | solution.py:377
  34.5 33.9 %collective-permute-start.27 = (bf16[6,256,128]{2,1,0:T(8,128)(2,1)}, bf16[6,256,128]{2,1,0:T(8,128)(2,1)}, u32[]{:S(2)}, u32[]{:S(2)}) collective-permute-start(bf16[6,256,128]{2,1,0:T(8,128)(2,1)} %collective-permute-done.22.refs_15_.refs_19_), channel_id=1, source_target_pairs={{0,8},{2,10},{4,12},{6,14},{8,16},{10,18},{12,20},{14,22},{16,24},... | collective-permute-start | bytes 1179656 | tf_op jit(solution)/shard_map/ppermute | solution.py:377
  37.0 9.8 %collective-permute-start.2 = (bf16[4,256,128]{2,1,0:T(8,128)(2,1)}, bf16[4,256,128]{2,1,0:T(8,128)(2,1)}, u32[]{:S(2)}, u32[]{:S(2)}) collective-permute-start(bf16[4,256,128]{2,1,0:T(8,128)(2,1)} %get-tuple-element.30), channel_id=1, source_target_pairs={{0,6},{2,4},{4,2},{6,0},{8,14},{10,12},{12,10},{14,8},{16,22},{18,... | collective-permute-start | bytes 786440 | tf_op jit(solution)/shard_map/ppermute | solution.py:372
  46.8 45.4 %collective-permute-start.17 = (bf16[6,256,128]{2,1,0:T(8,128)(2,1)}, bf16[6,256,128]{2,1,0:T(8,128)(2,1)}, u32[]{:S(2)}, u32[]{:S(2)}) collective-permute-start(bf16[6,256,128]{2,1,0:T(8,128)(2,1)} %get-tuple-element.41.refs_12_.refs_16_), channel_id=1, source_target_pairs={{0,24},{2,26},{4,28},{6,30},{8,0},{10,2},{12,4},{14,6},{16,8},{18,... | collective-permute-start | bytes 1179656 | tf_op jit(solution)/shard_map/ppermute | solution.py:377
  50.3 41.8 %collective-permute-start.10 = (bf16[2,256,128]{2,1,0:T(8,128)(2,1)}, bf16[2,256,128]{2,1,0:T(8,128)(2,1)}, u32[]{:S(2)}, u32[]{:S(2)}) collective-permute-start(bf16[2,256,128]{2,1,0:T(8,128)(2,1)} %get-tuple-element.31.refs_12_.refs_16_), channel_id=1, source_target_pairs={{0,8},{2,10},{4,12},{6,14},{8,16},{10,18},{12,20},{14,22},{16,24},... | collective-permute-start | bytes 393224 | tf_op jit(solution)/shard_map/ppermute | solution.py:377
  51.5 42.1 %collective-permute-start.19 = (bf16[6,256,128]{2,1,0:T(8,128)(2,1)}, bf16[6,256,128]{2,1,0:T(8,128)(2,1)}, u32[]{:S(2)}, u32[]{:S(2)}) collective-permute-start(bf16[6,256,128]{2,1,0:T(8,128)(2,1)} %collective-permute-done.18.refs_13_.refs_17_), channel_id=1, source_target_pairs={{0,24},{2,26},{4,28},{6,30},{8,0},{10,2},{12,4},{14,6},{16,8},{18,... | collective-permute-start | bytes 1179656 | tf_op jit(solution)/shard_map/ppermute | solution.py:377
  60.0 37.2 %collective-permute-start.21 = (bf16[6,256,128]{2,1,0:T(8,128)(2,1)}, bf16[6,256,128]{2,1,0:T(8,128)(2,1)}, u32[]{:S(2)}, u32[]{:S(2)}) collective-permute-start(bf16[6,256,128]{2,1,0:T(8,128)(2,1)} %collective-permute-done.20.refs_14_.refs_18_), channel_id=1, source_target_pairs={{0,24},{2,26},{4,28},{6,30},{8,0},{10,2},{12,4},{14,6},{16,8},{18,... | collective-permute-start | bytes 1179656 | tf_op jit(solution)/shard_map/ppermute | solution.py:377
  68.4 37.3 %collective-permute-start.23 = (bf16[6,256,128]{2,1,0:T(8,128)(2,1)}, bf16[6,256,128]{2,1,0:T(8,128)(2,1)}, u32[]{:S(2)}, u32[]{:S(2)}) collective-permute-start(bf16[6,256,128]{2,1,0:T(8,128)(2,1)} %collective-permute-done.22.refs_15_.refs_19_), channel_id=1, source_target_pairs={{0,24},{2,26},{4,28},{6,30},{8,0},{10,2},{12,4},{14,6},{16,8},{18,... | collective-permute-start | bytes 1179656 | tf_op jit(solution)/shard_map/ppermute | solution.py:377
  92.1 26.5 %collective-permute-start.3 = (bf16[2,256,128]{2,1,0:T(8,128)(2,1)}, bf16[2,256,128]{2,1,0:T(8,128)(2,1)}, u32[]{:S(2)}, u32[]{:S(2)}) collective-permute-start(bf16[2,256,128]{2,1,0:T(8,128)(2,1)} %get-tuple-element.31.refs_12_.refs_16_), channel_id=1, source_target_pairs={{0,24},{2,26},{4,28},{6,30},{8,0},{10,2},{12,4},{14,6},{16,8},{18,... | collective-permute-start | bytes 393224 | tf_op jit(solution)/shard_map/ppermute | solution.py:377
  92.2 29.5 %collective-permute-start.11 = (bf16[2,256,128]{2,1,0:T(8,128)(2,1)}, bf16[2,256,128]{2,1,0:T(8,128)(2,1)}, u32[]{:S(2)}, u32[]{:S(2)}) collective-permute-start(bf16[2,256,128]{2,1,0:T(8,128)(2,1)} %collective-permute-done.4.refs_13_.refs_17_), channel_id=1, source_target_pairs={{0,8},{2,10},{4,12},{6,14},{8,16},{10,18},{12,20},{14,22},{16,24},... | collective-permute-start | bytes 393224 | tf_op jit(solution)/shard_map/ppermute | solution.py:377
  93.6 38.4 %collective-permute-start.5 = (bf16[2,256,128]{2,1,0:T(8,128)(2,1)}, bf16[2,256,128]{2,1,0:T(8,128)(2,1)}, u32[]{:S(2)}, u32[]{:S(2)}) collective-permute-start(bf16[2,256,128]{2,1,0:T(8,128)(2,1)} %collective-permute-done.4.refs_13_.refs_17_), channel_id=1, source_target_pairs={{0,24},{2,26},{4,28},{6,30},{8,0},{10,2},{12,4},{14,6},{16,8},{18,... | collective-permute-start | bytes 393224 | tf_op jit(solution)/shard_map/ppermute | solution.py:377
  97.3 24.6 %collective-permute-start.12 = (bf16[2,256,128]{2,1,0:T(8,128)(2,1)}, bf16[2,256,128]{2,1,0:T(8,128)(2,1)}, u32[]{:S(2)}, u32[]{:S(2)}) collective-permute-start(bf16[2,256,128]{2,1,0:T(8,128)(2,1)} %collective-permute-done.6.refs_14_.refs_18_), channel_id=1, source_target_pairs={{0,8},{2,10},{4,12},{6,14},{8,16},{10,18},{12,20},{14,22},{16,24},... | collective-permute-start | bytes 393224 | tf_op jit(solution)/shard_map/ppermute | solution.py:377
  105.7 26.1 %collective-permute-start.13 = (bf16[2,256,128]{2,1,0:T(8,128)(2,1)}, bf16[2,256,128]{2,1,0:T(8,128)(2,1)}, u32[]{:S(2)}, u32[]{:S(2)}) collective-permute-start(bf16[2,256,128]{2,1,0:T(8,128)(2,1)} %collective-permute-done.8.refs_15_.refs_19_), channel_id=1, source_target_pairs={{0,8},{2,10},{4,12},{6,14},{8,16},{10,18},{12,20},{14,22},{16,24},... | collective-permute-start | bytes 393224 | tf_op jit(solution)/shard_map/ppermute | solution.py:377
  118.6 24.1 %collective-permute-start.7 = (bf16[2,256,128]{2,1,0:T(8,128)(2,1)}, bf16[2,256,128]{2,1,0:T(8,128)(2,1)}, u32[]{:S(2)}, u32[]{:S(2)}) collective-permute-start(bf16[2,256,128]{2,1,0:T(8,128)(2,1)} %collective-permute-done.6.refs_14_.refs_18_), channel_id=1, source_target_pairs={{0,24},{2,26},{4,28},{6,30},{8,0},{10,2},{12,4},{14,6},{16,8},{18,... | collective-permute-start | bytes 393224 | tf_op jit(solution)/shard_map/ppermute | solution.py:377
  121.6 21.0 %collective-permute-start.9 = (bf16[2,256,128]{2,1,0:T(8,128)(2,1)}, bf16[2,256,128]{2,1,0:T(8,128)(2,1)}, u32[]{:S(2)}, u32[]{:S(2)}) collective-permute-start(bf16[2,256,128]{2,1,0:T(8,128)(2,1)} %collective-permute-done.8.refs_15_.refs_19_), channel_id=1, source_target_pairs={{0,24},{2,26},{4,28},{6,30},{8,0},{10,2},{12,4},{14,6},{16,8},{18,... | collective-permute-start | bytes 393224 | tf_op jit(solution)/shard_map/ppermute | solution.py:377
  121.9 27.0 %collective-permute-start.28 = (bf16[3,256,128]{2,1,0:T(8,128)(2,1)}, bf16[3,256,128]{2,1,0:T(8,128)(2,1)}, u32[]{:S(2)}, u32[]{:S(2)}) collective-permute-start(bf16[3,256,128]{2,1,0:T(8,128)(2,1)} %get-tuple-element.46), channel_id=1, source_target_pairs={{0,2},{2,0},{4,6},{6,4},{8,10},{10,8},{12,14},{14,12},{16,18},{18,... | collective-permute-start | bytes 589832 | tf_op jit(solution)/shard_map/ppermute | solution.py:372
  131.7 18.9 %collective-permute-start.29 = (bf16[3,256,128]{2,1,0:T(8,128)(2,1)}, bf16[3,256,128]{2,1,0:T(8,128)(2,1)}, u32[]{:S(2)}, u32[]{:S(2)}) collective-permute-start(bf16[3,256,128]{2,1,0:T(8,128)(2,1)} %get-tuple-element.47), channel_id=1, source_target_pairs={{0,4},{2,6},{4,0},{6,2},{8,12},{10,14},{12,8},{14,10},{16,20},{18,... | collective-permute-start | bytes 589832 | tf_op jit(solution)/shard_map/ppermute | solution.py:372
  132.0 18.6 %collective-permute-start.30 = (bf16[3,256,128]{2,1,0:T(8,128)(2,1)}, bf16[3,256,128]{2,1,0:T(8,128)(2,1)}, u32[]{:S(2)}, u32[]{:S(2)}) collective-permute-start(bf16[3,256,128]{2,1,0:T(8,128)(2,1)} %get-tuple-element.48), channel_id=1, source_target_pairs={{0,6},{2,4},{4,2},{6,0},{8,14},{10,12},{12,10},{14,8},{16,22},{18,... | collective-permute-start | bytes 589832 | tf_op jit(solution)/shard_map/ppermute | solution.py:372
  148.4 4.2 %collective-permute-start.14 = (bf16[1,256,128]{2,1,0:T(8,128)(2,1)}, bf16[1,256,128]{2,1,0:T(8,128)(2,1)}, u32[]{:S(2)}, u32[]{:S(2)}) collective-permute-start(bf16[1,256,128]{2,1,0:T(8,128)(2,1)} %get-tuple-element.38), channel_id=1, source_target_pairs={{0,2},{2,0},{4,6},{6,4},{8,10},{10,8},{12,14},{14,12},{16,18},{18,... | collective-permute-start | bytes 196616 | tf_op jit(solution)/shard_map/ppermute | solution.py:372
  148.6 4.0 %collective-permute-start.15 = (bf16[1,256,128]{2,1,0:T(8,128)(2,1)}, bf16[1,256,128]{2,1,0:T(8,128)(2,1)}, u32[]{:S(2)}, u32[]{:S(2)}) collective-permute-start(bf16[1,256,128]{2,1,0:T(8,128)(2,1)} %get-tuple-element.39), channel_id=1, source_target_pairs={{0,4},{2,6},{4,0},{6,2},{8,12},{10,14},{12,8},{14,10},{16,20},{18,... | collective-permute-start | bytes 196616 | tf_op jit(solution)/shard_map/ppermute | solution.py:372
  148.9 5.3 %collective-permute-start.16 = (bf16[1,256,128]{2,1,0:T(8,128)(2,1)}, bf16[1,256,128]{2,1,0:T(8,128)(2,1)}, u32[]{:S(2)}, u32[]{:S(2)}) collective-permute-start(bf16[1,256,128]{2,1,0:T(8,128)(2,1)} %get-tuple-element.40), channel_id=1, source_target_pairs={{0,6},{2,4},{4,2},{6,0},{8,14},{10,12},{12,10},{14,8},{16,22},{18,... | collective-permute-start | bytes 196616 | tf_op jit(solution)/shard_map/ppermute | solution.py:372

commit v5 on v4

--- a/solution.py
+++ b/solution.py
@@ -162,32 +162,63 @@
 SUB = 8
 
 
-def attend(query, keys, bias, store):
-    rows = query.shape[0]
-    best = None
-    for t, tile_bias in enumerate(bias):
+class Block:
+    def __init__(self, query, keys, values, bias, store, piece):
+        self.query, self.keys, self.values, self.bias, self.store = query, keys, values, bias, store
+        rows, self.piece = query.shape[0], piece
+        self.pieces = [
+            (t, at) for t in range(len(bias)) for at in range(0, rows, piece)
+        ]
+        self.rows, self.best, self.acc, self.floor = rows, None, None, None
+
+    def score(self, n):
+        t, at = self.pieces[n]
+        start = t * self.rows + at
         tile = lax.dot_general(
-            keys[pl.ds(t * rows, rows), :], query, (((1,), (1,)), ((), ())),
+            self.keys[pl.ds(start, self.piece), :], self.query, (((1,), (1,)), ((), ())),
             preferred_element_type=jnp.float32,
         )
-        tile = tile * LOG2E + tile_bias[...]
-        store[pl.ds(t * rows, rows), :] = tile
-        part = jnp.max(tile.reshape(rows // SUB, SUB, rows), axis=0)
-        best = part if best is None else jnp.maximum(best, part)
-    return jnp.broadcast_to(jnp.max(best, axis=0, keepdims=True), best.shape)
-
-
-def weigh(values, peak, count, store):
-    rows = store.shape[1]
-    acc = None
-    for t in range(count):
-        tile = store[pl.ds(t * rows, rows), :].reshape(rows // SUB, SUB, rows)
-        raised = jnp.exp2(tile - peak[None]).reshape(rows, rows).astype(values.dtype)
+        tile = tile * LOG2E + self.bias[t][pl.ds(at, self.piece), :]
+        self.store[pl.ds(start, self.piece), :] = tile
+        part = jnp.max(tile.reshape(self.piece // SUB, SUB, self.rows), axis=0)
+        self.best = part if self.best is None else jnp.maximum(self.best, part)
+
+    def close(self):
+        peak = jnp.broadcast_to(jnp.max(self.best, axis=0, keepdims=True), self.best.shape)
+        self.peak = peak if self.floor is None else jnp.maximum(peak, self.floor)
+
+    def weigh(self, n):
+        t, at = self.pieces[n]
+        start = t * self.rows + at
+        tile = self.store[pl.ds(start, self.piece), :].reshape(self.piece // SUB, SUB, self.rows)
+        raised = jnp.exp2(tile - self.peak[None]).reshape(self.piece, self.rows)
         part = jnp.dot(
-            values[:, pl.ds(t * rows, rows)], raised, preferred_element_type=jnp.float32
+            self.values[:, pl.ds(start, self.piece)], raised.astype(self.keys.dtype),
+            preferred_element_type=jnp.float32,
         )
-        acc = part if acc is None else acc + part
-    return acc
+        self.acc = part if self.acc is None else self.acc + part
+
+
+def pipeline(blocks, finish):
+    before = None
+    for block in list(blocks) + [None]:
+        ahead = len(block.pieces) if block is not None else 0
+        behind = len(before.pieces) if before is not None else 0
+        most = max(ahead, behind)
+        done = [0, 0]
+        for n in range(most):
+            for which, count, run in (
+                (0, behind, before.weigh if before is not None else None),
+                (1, ahead, block.score if block is not None else None),
+            ):
+                while done[which] * most < count * (n + 1):
+                    run(done[which])
+                    done[which] += 1
+        if block is not None:
+            block.close()
+        if before is not None:
+            finish(before)
+        before = block
 
 
 def lanes_of(head_width, head):
@@ -224,22 +255,31 @@
     for head in range(heads):
         flat[head, head_width:, :] = jnp.ones((2 * SUB, flat.shape[2]), dtype)
 
-    def one(head, _):
+    for head in range(heads):
         slope = slopes[(chunk * plane + place) * heads + head] * LOG2E
         for t in range(2 * win):
-            scaled[t] = bias[t] * slope
-        for i in range(plane):
-            first = max(0, i + plane - win)
-            count = 2 * plane - first
-            tiles = [scaled.at[b - plane - i + win] for b in range(first, 2 * plane)]
-            span = pl.ds(first * rows, count * rows)
-            peak = attend(query[head, i], keys.at[span], tiles, store.at[i % 2])
-            acc = weigh(flat.at[head, :, span], peak, count, store.at[i % 2])
-            out_ref[0, head, i, :head_width + SUB] = acc[:head_width + SUB]
-            out_ref[0, head, i, head_width + SUB:] = peak
-        return 0
-
-    lax.fori_loop(0, heads, one, 0)
+            scaled[head, t] = bias[t] * slope
+
+    def blocks():
+        for head in range(heads):
+            for i in range(plane):
+                first = max(0, i + plane - win)
+                count = 2 * plane - first
+                span = pl.ds(first * rows, count * rows)
+                block = Block(
+                    query[head, i], keys.at[span], flat.at[head, :, span],
+                    [scaled.at[head, b - plane - i + win] for b in range(first, 2 * plane)],
+                    store.at[i % 2], rows,
+                )
+                block.place = head, i
+                yield block
+
+    def finish(block):
+        head, i = block.place
+        out_ref[0, head, i, :head_width + SUB] = block.acc[:head_width + SUB]
+        out_ref[0, head, i, head_width + SUB:] = block.peak
+
+    pipeline(blocks(), finish)
 
 
 def near(place, slopes, qs, ups, owns, bias, chunk0, chunks, head_width):
@@ -267,7 +307,7 @@
             pltpu.VMEM((2 * plane * rows, LANES), dtype),
             pltpu.VMEM((heads, head_width + 2 * SUB, 2 * plane * rows), dtype),
             pltpu.VMEM((heads, plane, rows, LANES), dtype),
-            pltpu.VMEM((2 * win, rows, rows), jnp.float32),
+            pltpu.VMEM((heads, 2 * win, rows, rows), jnp.float32),
         ],
         cost_estimate=pl.CostEstimate(
             flops=4 * pairs * LANES, bytes_accessed=chunks * (4 << 20), transcendentals=pairs
@@ -302,22 +342,34 @@
         slope = slopes[(chunk * plane + place) * heads + head] * LOG2E
         for t in range(win):
             scaled[head, t] = bias[t] * slope
-    for i in range(plane):
-        count = min(plane, win - plane + i + 1)
-        span = pl.ds(0, count * rows)
-        both = []
-        for head in range(heads):
-            tiles = [scaled.at[head, b + plane - i - 1] for b in range(count)]
-            slot = store.at[(i * heads + head) % 2]
-            before = near_ref[0, head, i, head_width + SUB:]
-            peak = jnp.maximum(attend(query[head, i], keys.at[span], tiles, slot), before)
-            acc = weigh(flat.at[head, :, span], peak, count, slot)[:head_width + SUB]
-            acc = acc.reshape(-1, SUB, rows)
-            old = near_ref[0, head, i, :head_width + SUB].reshape(-1, SUB, rows)
-            acc = acc + old * jnp.exp2(before - peak)[None]
-            share = 1.0 / acc[head_width // SUB:]
-            both.append((acc[:head_width // SUB] * share).reshape(head_width, rows))
-        held[i ^ place] = jnp.concatenate(both, axis=0).T.astype(dtype)
+    both = {}
+
+    def blocks():
+        for i in range(plane):
+            count = min(plane, win - plane + i + 1)
+            span = pl.ds(0, count * rows)
+            for head in range(heads):
+                block = Block(
+                    query[head, i], keys.at[span], flat.at[head, :, span],
+                    [scaled.at[head, b + plane - i - 1] for b in range(count)],
+                    store.at[(i * heads + head) % 2], rows // 2,
+                )
+                block.place = head, i
+                block.floor = near_ref[0, head, i, head_width + SUB:]
+                yield block
+
+    def finish(block):
+        head, i = block.place
+        acc = block.acc[:head_width + SUB].reshape(-1, SUB, rows)
+        old = near_ref[0, head, i, :head_width + SUB].reshape(-1, SUB, rows)
+        acc = acc + old * jnp.exp2(block.floor - block.peak)[None]
+        share = 1.0 / acc[head_width // SUB:]
+        both[head] = (acc[:head_width // SUB] * share).reshape(head_width, rows)
+        if head == heads - 1:
+            tall = jnp.concatenate([both[h] for h in range(heads)], axis=0)
+            held[i ^ place] = tall.T.astype(dtype)
+
+    pipeline(blocks(), finish)
     for k in range(plane):
         outs[k][0] = held[k]
 
@@ -396,8 +448,7 @@
     for g, (start, size) in enumerate(groups):
         outs = far(place, slopes, qs, downs[g], far_bias, sums[g], start, size, head_width)
         back.append(send(outs))
-    most = unpack(place, back[:1], 0, chunks, None)
-    return unpack(place, back[1:], chunks - 1, chunks, most)
+    return unpack(place, back, 0, chunks, None)
 
 
 def solution(mesh):

time: 156 us -> 154 us (0.987)
  Pallas kernels: 61 us -> 52.3 us
  waiting for transfers between devices: 51.7 us -> 58.9 us
    pallas_call x2, Pallas kernels: 31.2 us -> 25.9 us  [near(): pl.pallas_call(functools.partial(near_kernel, win, plane, chunk0, head_wi...]
    ppermute x16, waiting for transfers between devices: 24.7 us -> 28.7 us  [shift(): return [lax.ppermute(x, 'seq', pairs) for x in arrays]]
    ppermute x15, waiting for transfers between devices: 27 us -> 30.2 us  [send(): out.append(lax.ppermute(x, 'seq', pairs))]
    pallas_call x2, Pallas kernels: 18.4 us -> 16.6 us  [far(): pl.pallas_call(functools.partial(far_kernel, win, plane, chunk0, head_wid...]
    pallas_call x2 -> x1, Pallas kernels: 3.66 us -> 2.13 us  [unpack(): pl.pallas_call(functools.partial(unpack_kernel, plane, chunk0, chunks, le...]
  transfers between devices with their start and end apart: 31 -> 31, of which waited for: 9 -> 11; matrix products, arithmetic and copies ran while one was open for 0% -> 0% of each run, Pallas kernels for 36% -> 31%
where the time goes in v5:
time: 154 us; the launch traced here: 153 us
  waiting for transfers between devices  58.9 us (38%)
  Pallas kernels  52.3 us (34%)
  starting transfers between devices  41.9 us (27%)
    ppermute x15, waiting for transfers between devices, send(): out.append(lax.ppermute(x, 'seq', pairs))  30.2 us
    ppermute x16, waiting for transfers between devices, shift(): return [lax.ppermute(x, 'seq', pairs) for x in arrays]  28.7 us
    pallas_call x2, Pallas kernels, near(): pl.pallas_call(functools.partial(near_kernel, win, plane, chunk0, head_wi...  25.9 us
    ppermute x15, starting transfers between devices, send(): out.append(lax.ppermute(x, 'seq', pairs))  22.2 us
    ppermute x16, starting transfers between devices, shift(): return [lax.ppermute(x, 'seq', pairs) for x in arrays]  19.7 us
    pallas_call x2, Pallas kernels, far(): pl.pallas_call(functools.partial(far_kernel, win, plane, chunk0, head_wid...  16.6 us
    pallas_call x2, Pallas kernels, pack(): pl.pallas_call(functools.partial(pack_kernel, plane, groups, names), in_s...  4.76 us
  transfers between devices with their start and end apart: 31, of which 11 were waited for; matrix products, arithmetic and copies ran while one was open for 0% of the time, Pallas kernels for 31%

profile of v5, /device:TPU:1, one launch (start us, length us, event | category | flops | bytes accessed | tf_op | source)
XLA Modules:
  0.0 153.4 jit_solution(7462447698231680227)
XLA Ops:
  0.0 2.6 %shard_map.65 = (bf16[6,256,128]{2,1,0:T(8,128)(2,1)}, bf16[6,256,128]{2,1,0:T(8,128)(2,1)}, bf16[6,256,128]{2,1,0:T(8,128)(2,1)}, bf16[6,256,128]{2,1,0:T(8,128...) custom-call(s32[1]{0:T(128)} %bitcast.place_ref, ...), custom_call_target="tpu_custom_call" | custom-call | bytes 4194304 | tf_op jit(solution)/shard_map/pallas_call | solution.py:84
  2.7 0.1 collective-permute-start.18
  2.7 2.7 %collective-permute-start.20 = (bf16[2,256,128]{2,1,0:T(8,128)(2,1)}, bf16[2,256,128]{2,1,0:T(8,128)(2,1)}, u32[]{:S(2)}, u32[]{:S(2)}) collective-permute-start(bf16[2,256,128]{2,1,0:T(8,128)(2,1)} %get-tuple-element.43), channel_id=1, source_target_pairs={{0,4},{2,6},{4,0},{6,2},{8,12},{10,14},{12,8},{14,10},{16,20},{18,... | collective-permute-start | bytes 393224 | tf_op jit(solution)/shard_map/ppermute | solution.py:424
  5.4 0.4 collective-permute-start.4
  5.8 1.8 %collective-permute-start.8 = (bf16[6,256,128]{2,1,0:T(8,128)(2,1)}, bf16[6,256,128]{2,1,0:T(8,128)(2,1)}, u32[]{:S(2)}, u32[]{:S(2)}) collective-permute-start(bf16[6,256,128]{2,1,0:T(8,128)(2,1)} %get-tuple-element.34), channel_id=1, source_target_pairs={{0,6},{2,4},{4,2},{6,0},{8,14},{10,12},{12,10},{14,8},{16,22},{18,... | collective-permute-start | bytes 1179656 | tf_op jit(solution)/shard_map/ppermute | solution.py:424
  7.6 0.0 collective-permute-start.22
  7.6 2.1 %shard_map.64 = (bf16[4,256,128]{2,1,0:T(8,128)(2,1)}, bf16[4,256,128]{2,1,0:T(8,128)(2,1)}, bf16[4,256,128]{2,1,0:T(8,128)(2,1)}, bf16[4,256,128]{2,1,0:T(8,128)(2,1)}) custom-call(s32[1]{0:T(128)} %bitcast.place_ref, bf16[256,2048]{1,0:T(8,128)(2,1)} %refs_0_.2), custom_call_target="tpu_custom_call" | custom-call | bytes 2097152 | tf_op jit(solution)/shard_map/pallas_call | solution.py:84
  9.7 0.7 collective-permute-start
  10.5 18.7 %collective-permute-done.22.refs_15_.refs_19_ = bf16[2,256,128]{2,1,0:T(8,128)(2,1)} collective-permute-done((bf16[2,256,128]{2,1,0:T(8,128)(2,1)}, bf16[2,256,128]{2,1,0:T(8,128)(2,1)}, u32[]{:S(2)}, u32[]{:S(2)}) %collective-permute-start.22) | collective-permute-done | bytes 131104 | tf_op jit(solution)/shard_map/ppermute | solution.py:424
  29.2 1.4 collective-permute-start.1
  30.6 1.3 collective-permute-start.10
  31.9 1.3 collective-permute-start.11
  33.2 1.3 collective-permute-start.12
  34.5 0.1 collective-permute-start.13
  34.6 2.4 %collective-permute-done.1.refs_2_ = bf16[4,256,128]{2,1,0:T(8,128)(2,1)} collective-permute-done((bf16[4,256,128]{2,1,0:T(8,128)(2,1)}, bf16[4,256,128]{2,1,0:T(8,128)(2,1)}, u32[]{:S(2)}, u32[]{:S(2)}) %collective-permute-start.1) | collective-permute-done | bytes 262176 | tf_op jit(solution)/shard_map/ppermute | solution.py:424
  37.0 2.6 %collective-permute-start.2 = (bf16[4,256,128]{2,1,0:T(8,128)(2,1)}, bf16[4,256,128]{2,1,0:T(8,128)(2,1)}, u32[]{:S(2)}, u32[]{:S(2)}) collective-permute-start(bf16[4,256,128]{2,1,0:T(8,128)(2,1)} %get-tuple-element.30), channel_id=1, source_target_pairs={{0,6},{2,4},{4,2},{6,0},{8,14},{10,12},{12,10},{14,8},{16,22},{18,... | collective-permute-start | bytes 786440 | tf_op jit(solution)/shard_map/ppermute | solution.py:424
  39.5 3.0 %bias_window.1 = (f32[8,256,256]{2,1,0:T(8,128)}, f32[4,256,256]{2,1,0:T(8,128)}) custom-call(s32[5]{0:T(128)} %buckets.1, bf16[3,256,256]{2,1,0:T(8,128)(2,1)} %tile_ref.1), custom_call_target="tpu_custom_call" | custom-call | tf_op jit(solution)/shard_map/bias_window/pallas_call | solution.py:31
  42.5 4.2 %collective-permute-done.2.refs_3_ = bf16[4,256,128]{2,1,0:T(8,128)(2,1)} collective-permute-done((bf16[4,256,128]{2,1,0:T(8,128)(2,1)}, bf16[4,256,128]{2,1,0:T(8,128)(2,1)}, u32[]{:S(2)}, u32[]{:S(2)}) %collective-permute-start.2) | collective-permute-done | bytes 262176 | tf_op jit(solution)/shard_map/ppermute | solution.py:424
  46.8 3.5 %collective-permute-start.3 = (bf16[6,256,128]{2,1,0:T(8,128)(2,1)}, bf16[6,256,128]{2,1,0:T(8,128)(2,1)}, u32[]{:S(2)}, u32[]{:S(2)}) collective-permute-start(bf16[6,256,128]{2,1,0:T(8,128)(2,1)} %get-tuple-element.31.refs_12_.refs_16_), channel_id=1, source_target_pairs={{0,24},{2,26},{4,28},{6,30},{8,0},{10,2},{12,4},{14,6},{16,8},{18,... | collective-permute-start | bytes 1179656 | tf_op jit(solution)/shard_map/ppermute | solution.py:429
  50.3 1.2 collective-permute-done.11.refs_5_.refs_9_
  51.5 2.0 %collective-permute-start.5 = (bf16[6,256,128]{2,1,0:T(8,128)(2,1)}, bf16[6,256,128]{2,1,0:T(8,128)(2,1)}, u32[]{:S(2)}, u32[]{:S(2)}) collective-permute-start(bf16[6,256,128]{2,1,0:T(8,128)(2,1)} %collective-permute-done.4.refs_13_.refs_17_), channel_id=1, source_target_pairs={{0,24},{2,26},{4,28},{6,30},{8,0},{10,2},{12,4},{14,6},{16,8},{18,... | collective-permute-start | bytes 1179656 | tf_op jit(solution)/shard_map/ppermute | solution.py:429
  53.6 6.4 %collective-permute-done.12.refs_6_.refs_10_ = bf16[6,256,128]{2,1,0:T(8,128)(2,1)} collective-permute-done((bf16[6,256,128]{2,1,0:T(8,128)(2,1)}, bf16[6,256,128]{2,1,0:T(8,128)(2,1)}, u32[]{:S(2)}, u32[]{:S(2)}) %collective-permute-start.12) | collective-permute-done | bytes 393248 | tf_op jit(solution)/shard_map/ppermute | solution.py:429
  60.0 1.4 collective-permute-start.7
  61.4 7.1 %collective-permute-done.13.refs_7_.refs_11_ = bf16[6,256,128]{2,1,0:T(8,128)(2,1)} collective-permute-done((bf16[6,256,128]{2,1,0:T(8,128)(2,1)}, bf16[6,256,128]{2,1,0:T(8,128)(2,1)}, u32[]{:S(2)}, u32[]{:S(2)}) %collective-permute-start.13) | collective-permute-done | bytes 393248 | tf_op jit(solution)/shard_map/ppermute | solution.py:429
  68.4 1.6 %collective-permute-start.9 = (bf16[6,256,128]{2,1,0:T(8,128)(2,1)}, bf16[6,256,128]{2,1,0:T(8,128)(2,1)}, u32[]{:S(2)}, u32[]{:S(2)}) collective-permute-start(bf16[6,256,128]{2,1,0:T(8,128)(2,1)} %collective-permute-done.8.refs_15_.refs_19_), channel_id=1, source_target_pairs={{0,24},{2,26},{4,28},{6,30},{8,0},{10,2},{12,4},{14,6},{16,8},{18,... | collective-permute-start | bytes 1179656 | tf_op jit(solution)/shard_map/ppermute | solution.py:429
  70.0 18.0 %near.2.refs_13_ = f32[3,2,4,80,256]{4,3,2,1,0:T(8,128)} custom-call(s32[1]{0:T(128)} %bitcast.place_ref, f32[32]{0:T(128)} %slopes.7, bf16[4,256,128]{2,1,0:T(8,128)(2,1)} %get-tuple-element.27.refs_0_, bf16[4,256,128]{2,1,0:T(8,128)(2,1)} %collective-permute-done.refs_1_, bf16[4,256,128]{2,1,0:T(8,128)(2,1)} %collective-permute-done.1.refs_2_, ...), custom_call_target="tpu_custom_call" | custom-call | flops 5234491392 | bytes 12582912 | tf_op jit(solution)/shard_map/near/pallas_call | solution.py:297
  88.1 0.1 collective-permute-start.17
  88.2 1.4 collective-permute-start.25
  89.6 1.9 %collective-permute-start.19 = (bf16[2,256,128]{2,1,0:T(8,128)(2,1)}, bf16[2,256,128]{2,1,0:T(8,128)(2,1)}, u32[]{:S(2)}, u32[]{:S(2)}) collective-permute-start(bf16[2,256,128]{2,1,0:T(8,128)(2,1)} %collective-permute-done.18.refs_13_.refs_17_), channel_id=1, source_target_pairs={{0,24},{2,26},{4,28},{6,30},{8,0},{10,2},{12,4},{14,6},{16,8},{18,... | collective-permute-start | bytes 393224 | tf_op jit(solution)/shard_map/ppermute | solution.py:429
  91.5 5.8 %collective-permute-done.7.refs_6_.refs_10_ = bf16[6,256,128]{2,1,0:T(8,128)(2,1)} collective-permute-done((bf16[6,256,128]{2,1,0:T(8,128)(2,1)}, bf16[6,256,128]{2,1,0:T(8,128)(2,1)}, u32[]{:S(2)}, u32[]{:S(2)}) %collective-permute-start.7) | collective-permute-done | bytes 393248 | tf_op jit(solution)/shard_map/ppermute | solution.py:429
  97.3 0.3 collective-permute-start.26
  97.5 8.2 %collective-permute-done.9.refs_7_.refs_11_ = bf16[6,256,128]{2,1,0:T(8,128)(2,1)} collective-permute-done((bf16[6,256,128]{2,1,0:T(8,128)(2,1)}, bf16[6,256,128]{2,1,0:T(8,128)(2,1)}, u32[]{:S(2)}, u32[]{:S(2)}) %collective-permute-start.9) | collective-permute-done | bytes 393248 | tf_op jit(solution)/shard_map/ppermute | solution.py:429
  105.7 0.3 collective-permute-start.27
  105.9 11.2 %far.2 = (bf16[3,256,128]{2,1,0:T(8,128)(2,1)}, bf16[3,256,128]{2,1,0:T(8,128)(2,1)}, bf16[3,256,128]{2,1,0:T(8,128)(2,1)}, bf16[3,256,128]{2,1,0:T(8,128)(2,1)}) custom-call(s32[1]{0:T(128)} %bitcast.place_ref, f32[32]{0:T(128)} %slopes.7, bf16[4,256,128]{2,1,0:T(8,128)(2,1)} %get-tuple-element.27.refs_0_, ...), custom_call_target="tpu_custom_call" | custom-call | flops 2013265920 | bytes 12582912 | tf_op jit(solution)/shard_map/far/pallas_call | solution.py:389
  117.2 3.1 %collective-permute-start.21 = (bf16[2,256,128]{2,1,0:T(8,128)(2,1)}, bf16[2,256,128]{2,1,0:T(8,128)(2,1)}, u32[]{:S(2)}, u32[]{:S(2)}) collective-permute-start(bf16[2,256,128]{2,1,0:T(8,128)(2,1)} %collective-permute-done.20.refs_14_.refs_18_), channel_id=1, source_target_pairs={{0,24},{2,26},{4,28},{6,30},{8,0},{10,2},{12,4},{14,6},{16,8},{18,... | collective-permute-start | bytes 393224 | tf_op jit(solution)/shard_map/ppermute | solution.py:429
  120.2 0.3 collective-permute-start.23
  120.5 9.8 %collective-permute-start.14 = (bf16[3,256,128]{2,1,0:T(8,128)(2,1)}, bf16[3,256,128]{2,1,0:T(8,128)(2,1)}, u32[]{:S(2)}, u32[]{:S(2)}) collective-permute-start(bf16[3,256,128]{2,1,0:T(8,128)(2,1)} %get-tuple-element.38), channel_id=1, source_target_pairs={{0,2},{2,0},{4,6},{6,4},{8,10},{10,8},{12,14},{14,12},{16,18},{18,... | collective-permute-start | bytes 589832 | tf_op jit(solution)/shard_map/ppermute | solution.py:424
  130.3 0.3 collective-permute-start.15
  130.6 1.4 collective-permute-start.16
  132.1 7.8 %near.3.refs_13_ = f32[1,2,4,80,256]{4,3,2,1,0:T(8,128)} custom-call(s32[1]{0:T(128)} %bitcast.place_ref, f32[32]{0:T(128)} %slopes.7, bf16[4,256,128]{2,1,0:T(8,128)(2,1)} %get-tuple-element.27.refs_0_, bf16[4,256,128]{2,1,0:T(8,128)(2,1)} %collective-permute-done.refs_1_, bf16[4,256,128]{2,1,0:T(8,128)(2,1)} %collective-permute-done.1.refs_2_, ...), custom_call_target="tpu_custom_call" | custom-call | flops 1744830464 | bytes 4194304 | tf_op jit(solution)/shard_map/near/pallas_call | solution.py:297
  139.9 5.3 %far.3 = (bf16[1,256,128]{2,1,0:T(8,128)(2,1)}, bf16[1,256,128]{2,1,0:T(8,128)(2,1)}, bf16[1,256,128]{2,1,0:T(8,128)(2,1)}, bf16[1,256,128]{2,1,0:T(8,128)(2,1)}) custom-call(s32[1]{0:T(128)} %bitcast.place_ref, f32[32]{0:T(128)} %slopes.7, bf16[4,256,128]{2,1,0:T(8,128)(2,1)} %get-tuple-element.27.refs_0_, ...), custom_call_target="tpu_custom_call" | custom-call | flops 671088640 | bytes 4194304 | tf_op jit(solution)/shard_map/far/pallas_call | solution.py:389
  145.2 0.2 collective-permute-start.28
  145.4 0.3 collective-permute-start.29
  145.7 1.2 collective-permute-done.28.refs_5_
  146.8 0.5 collective-permute-start.30
  147.4 1.4 collective-permute-done.29.refs_6_
  148.8 2.2 %collective-permute-done.30.refs_7_ = bf16[1,256,128]{2,1,0:T(8,128)(2,1)} collective-permute-done((bf16[1,256,128]{2,1,0:T(8,128)(2,1)}, bf16[1,256,128]{2,1,0:T(8,128)(2,1)}, u32[]{:S(2)}, u32[]{:S(2)}) %collective-permute-start.30) | collective-permute-done | bytes 65568 | tf_op jit(solution)/shard_map/ppermute | solution.py:424
  151.1 2.1 %shard_map.66 = bf16[256,2048]{1,0:T(8,128)(2,1)} custom-call(s32[1]{0:T(128)} %bitcast.place_ref, bf16[3,256,128]{2,1,0:T(8,128)(2,1)} %get-tuple-element.37.refs_0_, bf16[3,256,128]{2,1,0:T(8,128)(2,1)} %collective-permute-done.14.refs_1_, bf16[3,256,128]{2,1,0:T(8,128)(2,1)} %collective-permute-done.15.refs_2_, ...), custom_call_target="tpu_custom_call" | custom-call | bytes 2097152 | tf_op jit(solution)/shard_map/pallas_call | solution.py:141
  (22 shorter events, 0.1 us)
Async XLA Ops:
  2.7 4.9 %collective-permute-start.18 = (bf16[2,256,128]{2,1,0:T(8,128)(2,1)}, bf16[2,256,128]{2,1,0:T(8,128)(2,1)}, u32[]{:S(2)}, u32[]{:S(2)}) collective-permute-start(bf16[2,256,128]{2,1,0:T(8,128)(2,1)} %get-tuple-element.42), channel_id=1, source_target_pairs={{0,2},{2,0},{4,6},{6,4},{8,10},{10,8},{12,14},{14,12},{16,18},{18,... | collective-permute-start | bytes 393224 | tf_op jit(solution)/shard_map/ppermute | solution.py:424
  2.7 7.0 %collective-permute-start.20 = (bf16[2,256,128]{2,1,0:T(8,128)(2,1)}, bf16[2,256,128]{2,1,0:T(8,128)(2,1)}, u32[]{:S(2)}, u32[]{:S(2)}) collective-permute-start(bf16[2,256,128]{2,1,0:T(8,128)(2,1)} %get-tuple-element.43), channel_id=1, source_target_pairs={{0,4},{2,6},{4,0},{6,2},{8,12},{10,14},{12,8},{14,10},{16,20},{18,... | collective-permute-start | bytes 393224 | tf_op jit(solution)/shard_map/ppermute | solution.py:424
  5.4 26.5 %collective-permute-start.4 = (bf16[6,256,128]{2,1,0:T(8,128)(2,1)}, bf16[6,256,128]{2,1,0:T(8,128)(2,1)}, u32[]{:S(2)}, u32[]{:S(2)}) collective-permute-start(bf16[6,256,128]{2,1,0:T(8,128)(2,1)} %get-tuple-element.32), channel_id=1, source_target_pairs={{0,2},{2,0},{4,6},{6,4},{8,10},{10,8},{12,14},{14,12},{16,18},{18,... | collective-permute-start | bytes 1179656 | tf_op jit(solution)/shard_map/ppermute | solution.py:424
  5.8 27.4 %collective-permute-start.6 = (bf16[6,256,128]{2,1,0:T(8,128)(2,1)}, bf16[6,256,128]{2,1,0:T(8,128)(2,1)}, u32[]{:S(2)}, u32[]{:S(2)}) collective-permute-start(bf16[6,256,128]{2,1,0:T(8,128)(2,1)} %get-tuple-element.33), channel_id=1, source_target_pairs={{0,4},{2,6},{4,0},{6,2},{8,12},{10,14},{12,8},{14,10},{16,20},{18,... | collective-permute-start | bytes 1179656 | tf_op jit(solution)/shard_map/ppermute | solution.py:424
  5.8 28.7 %collective-permute-start.8 = (bf16[6,256,128]{2,1,0:T(8,128)(2,1)}, bf16[6,256,128]{2,1,0:T(8,128)(2,1)}, u32[]{:S(2)}, u32[]{:S(2)}) collective-permute-start(bf16[6,256,128]{2,1,0:T(8,128)(2,1)} %get-tuple-element.34), channel_id=1, source_target_pairs={{0,6},{2,4},{4,2},{6,0},{8,14},{10,12},{12,10},{14,8},{16,22},{18,... | collective-permute-start | bytes 1179656 | tf_op jit(solution)/shard_map/ppermute | solution.py:424
  7.6 21.6 %collective-permute-start.22 = (bf16[2,256,128]{2,1,0:T(8,128)(2,1)}, bf16[2,256,128]{2,1,0:T(8,128)(2,1)}, u32[]{:S(2)}, u32[]{:S(2)}) collective-permute-start(bf16[2,256,128]{2,1,0:T(8,128)(2,1)} %get-tuple-element.44), channel_id=1, source_target_pairs={{0,6},{2,4},{4,2},{6,0},{8,14},{10,12},{12,10},{14,8},{16,22},{18,... | collective-permute-start | bytes 393224 | tf_op jit(solution)/shard_map/ppermute | solution.py:424
  9.7 20.9 %collective-permute-start = (bf16[4,256,128]{2,1,0:T(8,128)(2,1)}, bf16[4,256,128]{2,1,0:T(8,128)(2,1)}, u32[]{:S(2)}, u32[]{:S(2)}) collective-permute-start(bf16[4,256,128]{2,1,0:T(8,128)(2,1)} %get-tuple-element.28), channel_id=1, source_target_pairs={{0,2},{2,0},{4,6},{6,4},{8,10},{10,8},{12,14},{14,12},{16,18},{18,... | collective-permute-start | bytes 786440 | tf_op jit(solution)/shard_map/ppermute | solution.py:424
  29.2 7.8 %collective-permute-start.1 = (bf16[4,256,128]{2,1,0:T(8,128)(2,1)}, bf16[4,256,128]{2,1,0:T(8,128)(2,1)}, u32[]{:S(2)}, u32[]{:S(2)}) collective-permute-start(bf16[4,256,128]{2,1,0:T(8,128)(2,1)} %get-tuple-element.29), channel_id=1, source_target_pairs={{0,4},{2,6},{4,0},{6,2},{8,12},{10,14},{12,8},{14,10},{16,20},{18,... | collective-permute-start | bytes 786440 | tf_op jit(solution)/shard_map/ppermute | solution.py:424
  30.6 19.7 %collective-permute-start.10 = (bf16[6,256,128]{2,1,0:T(8,128)(2,1)}, bf16[6,256,128]{2,1,0:T(8,128)(2,1)}, u32[]{:S(2)}, u32[]{:S(2)}) collective-permute-start(bf16[6,256,128]{2,1,0:T(8,128)(2,1)} %get-tuple-element.31.refs_12_.refs_16_), channel_id=1, source_target_pairs={{0,8},{2,10},{4,12},{6,14},{8,16},{10,18},{12,20},{14,22},{16,24},... | collective-permute-start | bytes 1179656 | tf_op jit(solution)/shard_map/ppermute | solution.py:429
  31.9 19.6 %collective-permute-start.11 = (bf16[6,256,128]{2,1,0:T(8,128)(2,1)}, bf16[6,256,128]{2,1,0:T(8,128)(2,1)}, u32[]{:S(2)}, u32[]{:S(2)}) collective-permute-start(bf16[6,256,128]{2,1,0:T(8,128)(2,1)} %collective-permute-done.4.refs_13_.refs_17_), channel_id=1, source_target_pairs={{0,8},{2,10},{4,12},{6,14},{8,16},{10,18},{12,20},{14,22},{16,24},... | collective-permute-start | bytes 1179656 | tf_op jit(solution)/shard_map/ppermute | solution.py:429
  33.2 26.8 %collective-permute-start.12 = (bf16[6,256,128]{2,1,0:T(8,128)(2,1)}, bf16[6,256,128]{2,1,0:T(8,128)(2,1)}, u32[]{:S(2)}, u32[]{:S(2)}) collective-permute-start(bf16[6,256,128]{2,1,0:T(8,128)(2,1)} %collective-permute-done.6.refs_14_.refs_18_), channel_id=1, source_target_pairs={{0,8},{2,10},{4,12},{6,14},{8,16},{10,18},{12,20},{14,22},{16,24},... | collective-permute-start | bytes 1179656 | tf_op jit(solution)/shard_map/ppermute | solution.py:429
  34.5 33.9 %collective-permute-start.13 = (bf16[6,256,128]{2,1,0:T(8,128)(2,1)}, bf16[6,256,128]{2,1,0:T(8,128)(2,1)}, u32[]{:S(2)}, u32[]{:S(2)}) collective-permute-start(bf16[6,256,128]{2,1,0:T(8,128)(2,1)} %collective-permute-done.8.refs_15_.refs_19_), channel_id=1, source_target_pairs={{0,8},{2,10},{4,12},{6,14},{8,16},{10,18},{12,20},{14,22},{16,24},... | collective-permute-start | bytes 1179656 | tf_op jit(solution)/shard_map/ppermute | solution.py:429
  37.0 9.8 %collective-permute-start.2 = (bf16[4,256,128]{2,1,0:T(8,128)(2,1)}, bf16[4,256,128]{2,1,0:T(8,128)(2,1)}, u32[]{:S(2)}, u32[]{:S(2)}) collective-permute-start(bf16[4,256,128]{2,1,0:T(8,128)(2,1)} %get-tuple-element.30), channel_id=1, source_target_pairs={{0,6},{2,4},{4,2},{6,0},{8,14},{10,12},{12,10},{14,8},{16,22},{18,... | collective-permute-start | bytes 786440 | tf_op jit(solution)/shard_map/ppermute | solution.py:424
  46.8 41.4 %collective-permute-start.3 = (bf16[6,256,128]{2,1,0:T(8,128)(2,1)}, bf16[6,256,128]{2,1,0:T(8,128)(2,1)}, u32[]{:S(2)}, u32[]{:S(2)}) collective-permute-start(bf16[6,256,128]{2,1,0:T(8,128)(2,1)} %get-tuple-element.31.refs_12_.refs_16_), channel_id=1, source_target_pairs={{0,24},{2,26},{4,28},{6,30},{8,0},{10,2},{12,4},{14,6},{16,8},{18,... | collective-permute-start | bytes 1179656 | tf_op jit(solution)/shard_map/ppermute | solution.py:429
  50.3 37.7 %collective-permute-start.24 = (bf16[2,256,128]{2,1,0:T(8,128)(2,1)}, bf16[2,256,128]{2,1,0:T(8,128)(2,1)}, u32[]{:S(2)}, u32[]{:S(2)}) collective-permute-start(bf16[2,256,128]{2,1,0:T(8,128)(2,1)} %get-tuple-element.41.refs_12_.refs_16_), channel_id=1, source_target_pairs={{0,8},{2,10},{4,12},{6,14},{8,16},{10,18},{12,20},{14,22},{16,24},... | collective-permute-start | bytes 393224 | tf_op jit(solution)/shard_map/ppermute | solution.py:429
  51.5 38.0 %collective-permute-start.5 = (bf16[6,256,128]{2,1,0:T(8,128)(2,1)}, bf16[6,256,128]{2,1,0:T(8,128)(2,1)}, u32[]{:S(2)}, u32[]{:S(2)}) collective-permute-start(bf16[6,256,128]{2,1,0:T(8,128)(2,1)} %collective-permute-done.4.refs_13_.refs_17_), channel_id=1, source_target_pairs={{0,24},{2,26},{4,28},{6,30},{8,0},{10,2},{12,4},{14,6},{16,8},{18,... | collective-permute-start | bytes 1179656 | tf_op jit(solution)/shard_map/ppermute | solution.py:429
  60.0 37.2 %collective-permute-start.7 = (bf16[6,256,128]{2,1,0:T(8,128)(2,1)}, bf16[6,256,128]{2,1,0:T(8,128)(2,1)}, u32[]{:S(2)}, u32[]{:S(2)}) collective-permute-start(bf16[6,256,128]{2,1,0:T(8,128)(2,1)} %collective-permute-done.6.refs_14_.refs_18_), channel_id=1, source_target_pairs={{0,24},{2,26},{4,28},{6,30},{8,0},{10,2},{12,4},{14,6},{16,8},{18,... | collective-permute-start | bytes 1179656 | tf_op jit(solution)/shard_map/ppermute | solution.py:429
  68.4 37.3 %collective-permute-start.9 = (bf16[6,256,128]{2,1,0:T(8,128)(2,1)}, bf16[6,256,128]{2,1,0:T(8,128)(2,1)}, u32[]{:S(2)}, u32[]{:S(2)}) collective-permute-start(bf16[6,256,128]{2,1,0:T(8,128)(2,1)} %collective-permute-done.8.refs_15_.refs_19_), channel_id=1, source_target_pairs={{0,24},{2,26},{4,28},{6,30},{8,0},{10,2},{12,4},{14,6},{16,8},{18,... | collective-permute-start | bytes 1179656 | tf_op jit(solution)/shard_map/ppermute | solution.py:429
  88.1 29.1 %collective-permute-start.17 = (bf16[2,256,128]{2,1,0:T(8,128)(2,1)}, bf16[2,256,128]{2,1,0:T(8,128)(2,1)}, u32[]{:S(2)}, u32[]{:S(2)}) collective-permute-start(bf16[2,256,128]{2,1,0:T(8,128)(2,1)} %get-tuple-element.41.refs_12_.refs_16_), channel_id=1, source_target_pairs={{0,24},{2,26},{4,28},{6,30},{8,0},{10,2},{12,4},{14,6},{16,8},{18,... | collective-permute-start | bytes 393224 | tf_op jit(solution)/shard_map/ppermute | solution.py:429
  88.2 32.1 %collective-permute-start.25 = (bf16[2,256,128]{2,1,0:T(8,128)(2,1)}, bf16[2,256,128]{2,1,0:T(8,128)(2,1)}, u32[]{:S(2)}, u32[]{:S(2)}) collective-permute-start(bf16[2,256,128]{2,1,0:T(8,128)(2,1)} %collective-permute-done.18.refs_13_.refs_17_), channel_id=1, source_target_pairs={{0,8},{2,10},{4,12},{6,14},{8,16},{10,18},{12,20},{14,22},{16,24},... | collective-permute-start | bytes 393224 | tf_op jit(solution)/shard_map/ppermute | solution.py:429
  89.6 41.0 %collective-permute-start.19 = (bf16[2,256,128]{2,1,0:T(8,128)(2,1)}, bf16[2,256,128]{2,1,0:T(8,128)(2,1)}, u32[]{:S(2)}, u32[]{:S(2)}) collective-permute-start(bf16[2,256,128]{2,1,0:T(8,128)(2,1)} %collective-permute-done.18.refs_13_.refs_17_), channel_id=1, source_target_pairs={{0,24},{2,26},{4,28},{6,30},{8,0},{10,2},{12,4},{14,6},{16,8},{18,... | collective-permute-start | bytes 393224 | tf_op jit(solution)/shard_map/ppermute | solution.py:429
  97.3 23.3 %collective-permute-start.26 = (bf16[2,256,128]{2,1,0:T(8,128)(2,1)}, bf16[2,256,128]{2,1,0:T(8,128)(2,1)}, u32[]{:S(2)}, u32[]{:S(2)}) collective-permute-start(bf16[2,256,128]{2,1,0:T(8,128)(2,1)} %collective-permute-done.20.refs_14_.refs_18_), channel_id=1, source_target_pairs={{0,8},{2,10},{4,12},{6,14},{8,16},{10,18},{12,20},{14,22},{16,24},... | collective-permute-start | bytes 393224 | tf_op jit(solution)/shard_map/ppermute | solution.py:429
  105.7 24.7 %collective-permute-start.27 = (bf16[2,256,128]{2,1,0:T(8,128)(2,1)}, bf16[2,256,128]{2,1,0:T(8,128)(2,1)}, u32[]{:S(2)}, u32[]{:S(2)}) collective-permute-start(bf16[2,256,128]{2,1,0:T(8,128)(2,1)} %collective-permute-done.22.refs_15_.refs_19_), channel_id=1, source_target_pairs={{0,8},{2,10},{4,12},{6,14},{8,16},{10,18},{12,20},{14,22},{16,24},... | collective-permute-start | bytes 393224 | tf_op jit(solution)/shard_map/ppermute | solution.py:429
  117.2 22.7 %collective-permute-start.21 = (bf16[2,256,128]{2,1,0:T(8,128)(2,1)}, bf16[2,256,128]{2,1,0:T(8,128)(2,1)}, u32[]{:S(2)}, u32[]{:S(2)}) collective-permute-start(bf16[2,256,128]{2,1,0:T(8,128)(2,1)} %collective-permute-done.20.refs_14_.refs_18_), channel_id=1, source_target_pairs={{0,24},{2,26},{4,28},{6,30},{8,0},{10,2},{12,4},{14,6},{16,8},{18,... | collective-permute-start | bytes 393224 | tf_op jit(solution)/shard_map/ppermute | solution.py:429
  120.2 19.6 %collective-permute-start.23 = (bf16[2,256,128]{2,1,0:T(8,128)(2,1)}, bf16[2,256,128]{2,1,0:T(8,128)(2,1)}, u32[]{:S(2)}, u32[]{:S(2)}) collective-permute-start(bf16[2,256,128]{2,1,0:T(8,128)(2,1)} %collective-permute-done.22.refs_15_.refs_19_), channel_id=1, source_target_pairs={{0,24},{2,26},{4,28},{6,30},{8,0},{10,2},{12,4},{14,6},{16,8},{18,... | collective-permute-start | bytes 393224 | tf_op jit(solution)/shard_map/ppermute | solution.py:429
  120.5 30.5 %collective-permute-start.14 = (bf16[3,256,128]{2,1,0:T(8,128)(2,1)}, bf16[3,256,128]{2,1,0:T(8,128)(2,1)}, u32[]{:S(2)}, u32[]{:S(2)}) collective-permute-start(bf16[3,256,128]{2,1,0:T(8,128)(2,1)} %get-tuple-element.38), channel_id=1, source_target_pairs={{0,2},{2,0},{4,6},{6,4},{8,10},{10,8},{12,14},{14,12},{16,18},{18,... | collective-permute-start | bytes 589832 | tf_op jit(solution)/shard_map/ppermute | solution.py:424
  130.3 20.7 %collective-permute-start.15 = (bf16[3,256,128]{2,1,0:T(8,128)(2,1)}, bf16[3,256,128]{2,1,0:T(8,128)(2,1)}, u32[]{:S(2)}, u32[]{:S(2)}) collective-permute-start(bf16[3,256,128]{2,1,0:T(8,128)(2,1)} %get-tuple-element.39), channel_id=1, source_target_pairs={{0,4},{2,6},{4,0},{6,2},{8,12},{10,14},{12,8},{14,10},{16,20},{18,... | collective-permute-start | bytes 589832 | tf_op jit(solution)/shard_map/ppermute | solution.py:424
  130.6 20.4 %collective-permute-start.16 = (bf16[3,256,128]{2,1,0:T(8,128)(2,1)}, bf16[3,256,128]{2,1,0:T(8,128)(2,1)}, u32[]{:S(2)}, u32[]{:S(2)}) collective-permute-start(bf16[3,256,128]{2,1,0:T(8,128)(2,1)} %get-tuple-element.40), channel_id=1, source_target_pairs={{0,6},{2,4},{4,2},{6,0},{8,14},{10,12},{12,10},{14,8},{16,22},{18,... | collective-permute-start | bytes 589832 | tf_op jit(solution)/shard_map/ppermute | solution.py:424
  145.2 1.6 %collective-permute-start.28 = (bf16[1,256,128]{2,1,0:T(8,128)(2,1)}, bf16[1,256,128]{2,1,0:T(8,128)(2,1)}, u32[]{:S(2)}, u32[]{:S(2)}) collective-permute-start(bf16[1,256,128]{2,1,0:T(8,128)(2,1)} %get-tuple-element.46), channel_id=1, source_target_pairs={{0,2},{2,0},{4,6},{6,4},{8,10},{10,8},{12,14},{14,12},{16,18},{18,... | collective-permute-start | bytes 196616 | tf_op jit(solution)/shard_map/ppermute | solution.py:424
  145.4 3.4 %collective-permute-start.29 = (bf16[1,256,128]{2,1,0:T(8,128)(2,1)}, bf16[1,256,128]{2,1,0:T(8,128)(2,1)}, u32[]{:S(2)}, u32[]{:S(2)}) collective-permute-start(bf16[1,256,128]{2,1,0:T(8,128)(2,1)} %get-tuple-element.47), channel_id=1, source_target_pairs={{0,4},{2,6},{4,0},{6,2},{8,12},{10,14},{12,8},{14,10},{16,20},{18,... | collective-permute-start | bytes 196616 | tf_op jit(solution)/shard_map/ppermute | solution.py:424
  146.8 4.2 %collective-permute-start.30 = (bf16[1,256,128]{2,1,0:T(8,128)(2,1)}, bf16[1,256,128]{2,1,0:T(8,128)(2,1)}, u32[]{:S(2)}, u32[]{:S(2)}) collective-permute-start(bf16[1,256,128]{2,1,0:T(8,128)(2,1)} %get-tuple-element.48), channel_id=1, source_target_pairs={{0,6},{2,4},{4,2},{6,0},{8,14},{10,12},{12,10},{14,8},{16,22},{18,... | collective-permute-start | bytes 196616 | tf_op jit(solution)/shard_map/ppermute | solution.py:424
